TPU v7x, 32 devices: a whole 2x2x4 slice. The times are simulated.
32 devices in a mesh: dp: 32 (over z, y, x, core).
Axes of the slice: x: 2, y: 2, z: 4, core: 2. Of those that a mesh axis runs over, the one named last changes fastest.
Arguments:
- tokens: bfloat16 [64, 512, 1024], P('dp'), may hold values from -6 to 6
- lengths: int32 [64, 16], P('dp'), may hold values from 1 to 64, 512 in all within a row
- w_query: float32 [2, 1024, 1024], P(None, 'dp'), may hold values from -0.1875 to 0.1875
- w_key: float32 [2, 1024, 1024], P(None, 'dp'), may hold values from -0.1875 to 0.1875
- w_value: float32 [2, 1024, 1024], P(None, 'dp'), may hold values from -0.1875 to 0.1875
- w_out: float32 [2, 1024, 1024], P(None, 'dp'), may hold values from -0.75 to 0.75
- w_inner: float32 [2, 1024, 4096], P(None, 'dp'), may hold values from -0.1875 to 0.1875
- w_outer: float32 [2, 4096, 1024], P(None, 'dp'), may hold values from -0.09375 to 0.09375
- bias_query: float32 [2, 1024], replicated, may hold values from -3 to 3
- bias_value: float32 [2, 1024], replicated, may hold values from -3 to 3
- bias_out: float32 [2, 1024], replicated, may hold values from -3 to 3
- bias_inner: float32 [2, 4096], replicated, may hold values from -3 to 3
- bias_outer: float32 [2, 1024], replicated, may hold values from -3 to 3
- shift_attn: float32 [2, 1024], replicated, may hold values from -3 to 3
- shift_ffn: float32 [2, 1024], replicated, may hold values from -3 to 3
- gain_attn: float32 [2, 1024], replicated, may hold values from 0.1 to 1.9
- gain_ffn: float32 [2, 1024], replicated, may hold values from 0.1 to 1.9
- cotangent: bfloat16 [64, 512, 1024], P('dp'), may hold values from -6 to 6
Outputs:
- output: bfloat16 [64, 512, 1024], P('dp')
- grad_tokens: float32 [64, 512, 1024], P('dp')
- grad_bias_query: float32 [2, 1024], replicated
- grad_bias_value: float32 [2, 1024], replicated
- grad_bias_out: float32 [2, 1024], replicated
- grad_bias_inner: float32 [2, 4096], replicated
- grad_bias_outer: float32 [2, 1024], replicated
- grad_shift_attn: float32 [2, 1024], replicated
- grad_shift_ffn: float32 [2, 1024], replicated
Inputs may be any that keep to these rules, and one draw needn't show every extreme that they name: In each row the 16 entries sum to 512: the first 15 are sentence lengths in slot order, the last counts padding slots at the row's end; the largest entry of each row is 64.
All inputs are finite; a program needn't handle non-finite values.
Results may differ from a plain program's by a relative error of at most 0.019.
Values may be sent and summed in bfloat16 or wider, within the bound.
A program may use at most 320 MiB of HBM per device.

v0:
```python
import jax
import jax.numpy as jnp
from jax import lax
from jax.sharding import PartitionSpec as P

HEADS = 16
LAYERS = 2


EPSILON = 1e-12
NEGATIVE = -1000000000.0


def product(left, right):
    return jnp.dot(left, right, preferred_element_type=jnp.float32)


def product_back(left, right):
    return lax.dot_general(
        left, right, (((1,), (1,)), ((), ())), preferred_element_type=jnp.float32
    )


def column_sum(values):
    return jnp.sum(values, axis=0, dtype=jnp.float32)


def layer_norm(residual, gain_row, shift_row):
    average = jnp.mean(residual, axis=-1, keepdims=True)
    centered = residual - average
    variance = jnp.mean(centered * centered, axis=-1, keepdims=True)
    return centered * lax.rsqrt(variance + EPSILON) * gain_row + shift_row


def gelu_exact(values):
    return jax.nn.gelu(values, approximate=False)


def sentence_numbers(lengths, slot_count):
    sentence_ends = jnp.cumsum(lengths, axis=-1)
    position = jnp.arange(slot_count, dtype=jnp.int32)
    return jnp.sum(
        (position[None, :, None] >= sentence_ends[:, None, :]).astype(jnp.int32), axis=-1
    )


def allowed_pairs(numbers, count):
    same = numbers[:, :, None] == numbers[:, None, :]
    key_real = numbers[:, None, :] < count - 1
    position = jnp.arange(numbers.shape[1], dtype=jnp.int32)
    diagonal = (position[:, None] == position[None, :])[None]
    return same & key_real | diagonal


def row_scores(query_rows, key_rows, allowed):
    score_scale = query_rows.shape[-1] ** (-0.5)
    scores = (
        jnp.einsum("qhd,khd->hqk", query_rows, key_rows, preferred_element_type=jnp.float32)
        * score_scale
    )
    return jnp.where(allowed[None], scores, NEGATIVE)


def attend_forward(query_rows, key_rows, value_rows, allowed):
    scores = row_scores(query_rows, key_rows, allowed)
    row_max = jnp.max(scores, axis=-1, keepdims=True)
    exp_total = jnp.sum(jnp.exp(scores - row_max), axis=-1, keepdims=True)
    log_total = row_max + jnp.log(exp_total)
    probabilities = jnp.exp(scores - log_total).astype(jnp.bfloat16)
    attended = jnp.einsum(
        "hqk,khd->qhd", probabilities, value_rows, preferred_element_type=jnp.float32
    )
    return (attended.reshape(attended.shape[0], -1).astype(jnp.bfloat16), log_total)


def attend_backward(query_rows, key_rows, value_rows, allowed, log_total, grad_attended):
    score_scale = query_rows.shape[-1] ** (-0.5)
    scores = row_scores(query_rows, key_rows, allowed)
    probabilities = jnp.exp(scores - log_total)
    grad_probs = jnp.einsum(
        "qhd,khd->hqk", grad_attended, value_rows, preferred_element_type=jnp.float32
    )
    grad_scores = probabilities * (
        grad_probs - jnp.sum(probabilities * grad_probs, axis=-1, keepdims=True)
    )
    grad_scores = jnp.where(allowed[None], grad_scores, 0.0).astype(jnp.bfloat16)
    grad_query = (
        jnp.einsum("hqk,khd->qhd", grad_scores, key_rows, preferred_element_type=jnp.float32)
        * score_scale
    )
    grad_key = (
        jnp.einsum("hqk,qhd->khd", grad_scores, query_rows, preferred_element_type=jnp.float32)
        * score_scale
    )
    grad_value = jnp.einsum(
        "hqk,qhd->khd",
        probabilities.astype(jnp.bfloat16),
        grad_attended,
        preferred_element_type=jnp.float32,
    )
    slot_count = query_rows.shape[0]
    return (
        grad_query.reshape(slot_count, -1).astype(jnp.bfloat16),
        grad_key.reshape(slot_count, -1).astype(jnp.bfloat16),
        grad_value.reshape(slot_count, -1).astype(jnp.bfloat16),
    )


def fetch_forward(layer_index, w_query, w_key, w_value, w_out, w_inner, w_outer):
    rounded = [
        matrix[layer_index].astype(jnp.bfloat16)
        for matrix in (w_query, w_key, w_value, w_out, w_inner, w_outer)
    ]
    return (
        lax.all_gather(rounded[0], "dp", axis=0, tiled=True),
        lax.all_gather(rounded[1], "dp", axis=0, tiled=True),
        lax.all_gather(rounded[2], "dp", axis=0, tiled=True),
        lax.all_gather(rounded[3], "dp", axis=0, tiled=True),
        lax.all_gather(rounded[4], "dp", axis=0, tiled=True),
        lax.all_gather(rounded[5], "dp", axis=0, tiled=True),
    )


def layer_forward(hidden, matrices, parameters, allowed, row_count):
    weight_query, weight_key, weight_value, weight_out, weight_inner, weight_outer = matrices
    (
        bias_query,
        bias_value,
        bias_out,
        bias_inner,
        bias_outer,
        shift_attn,
        shift_ffn,
        gain_attn,
        gain_ffn,
    ) = parameters
    width = hidden.shape[1]
    active = hidden.astype(jnp.bfloat16)
    query_rows = (product(active, weight_query) + bias_query).astype(jnp.bfloat16)
    key_rows = product(active, weight_key).astype(jnp.bfloat16)
    value_rows = (product(active, weight_value) + bias_value).astype(jnp.bfloat16)
    split = (row_count, hidden.shape[0] // row_count, HEADS, width // HEADS)
    attended, log_total = lax.map(
        lambda row_item: attend_forward(*row_item),
        (query_rows.reshape(split), key_rows.reshape(split), value_rows.reshape(split), allowed),
    )
    attended = attended.reshape(hidden.shape)
    first_residual = hidden + (product(attended, weight_out) + bias_out)
    normed = layer_norm(first_residual, gain_attn, shift_attn)
    inner_pre = product(normed.astype(jnp.bfloat16), weight_inner) + bias_inner
    activated = gelu_exact(inner_pre).astype(jnp.bfloat16)
    second_residual = normed + (product(activated, weight_outer) + bias_outer)
    result = layer_norm(second_residual, gain_ffn, shift_ffn)
    return (
        result,
        (query_rows, key_rows, value_rows, log_total, first_residual, inner_pre, second_residual),
    )


def layer_backward(gradient, matrices, parameters, allowed, saved_state, row_count):
    weight_query, weight_key, weight_value, weight_out, weight_inner, weight_outer = matrices
    (
        bias_query,
        bias_value,
        bias_out,
        bias_inner,
        bias_outer,
        shift_attn,
        shift_ffn,
        gain_attn,
        gain_ffn,
    ) = parameters
    query_rows, key_rows, value_rows, log_total, first_residual, inner_pre, second_residual = (
        saved_state
    )
    width = gradient.shape[1]
    _, back_ffn = jax.vjp(
        lambda residual, shift_row: layer_norm(residual, gain_ffn, shift_row),
        second_residual,
        shift_ffn,
    )
    grad_second, grad_shift_ffn = back_ffn(gradient)
    grad_outer = grad_second.astype(jnp.bfloat16)
    grad_activated = product_back(grad_outer, weight_outer)
    _, back_gelu = jax.vjp(gelu_exact, inner_pre)
    grad_inner = back_gelu(grad_activated)[0].astype(jnp.bfloat16)
    grad_normed = grad_second + product_back(grad_inner, weight_inner)
    _, back_attn = jax.vjp(
        lambda residual, shift_row: layer_norm(residual, gain_attn, shift_row),
        first_residual,
        shift_attn,
    )
    grad_first, grad_shift_attn = back_attn(grad_normed)
    grad_branch = grad_first.astype(jnp.bfloat16)
    grad_attended = product_back(grad_branch, weight_out).astype(jnp.bfloat16)
    split = (row_count, gradient.shape[0] // row_count, HEADS, width // HEADS)
    grad_query, grad_key, grad_value = lax.map(
        lambda row_item: attend_backward(*row_item),
        (
            query_rows.reshape(split),
            key_rows.reshape(split),
            value_rows.reshape(split),
            allowed,
            log_total,
            grad_attended.reshape(split),
        ),
    )
    grad_query = grad_query.reshape(gradient.shape)
    grad_key = grad_key.reshape(gradient.shape)
    grad_value = grad_value.reshape(gradient.shape)
    grad_hidden = (
        grad_first
        + product_back(grad_query, weight_query)
        + product_back(grad_key, weight_key)
        + product_back(grad_value, weight_value)
    )
    layer_sums = (
        column_sum(grad_query),
        column_sum(grad_value),
        column_sum(grad_branch),
        column_sum(grad_inner),
        column_sum(grad_outer),
        grad_shift_attn,
        grad_shift_ffn,
    )
    return (grad_hidden, layer_sums)


def per_device(
    tokens,
    lengths,
    w_query,
    w_key,
    w_value,
    w_out,
    w_inner,
    w_outer,
    bias_query,
    bias_value,
    bias_out,
    bias_inner,
    bias_outer,
    shift_attn,
    shift_ffn,
    gain_attn,
    gain_ffn,
    cotangent,
):
    row_count, slot_count, width = tokens.shape
    numbers = sentence_numbers(lengths, slot_count)
    allowed = allowed_pairs(numbers, lengths.shape[1])
    is_real = (
        (numbers < lengths.shape[1] - 1).astype(jnp.float32).reshape(row_count * slot_count, 1)
    )
    hidden = tokens.astype(jnp.float32).reshape(row_count * slot_count, width)
    kept_matrices = []
    kept_states = []
    layer_parameters = []
    for layer_index in range(LAYERS):
        matrices = fetch_forward(layer_index, w_query, w_key, w_value, w_out, w_inner, w_outer)
        parameters = tuple(
            (
                parameter[layer_index]
                for parameter in (
                    bias_query,
                    bias_value,
                    bias_out,
                    bias_inner,
                    bias_outer,
                    shift_attn,
                    shift_ffn,
                    gain_attn,
                    gain_ffn,
                )
            )
        )
        hidden, saved_state = layer_forward(hidden, matrices, parameters, allowed, row_count)
        kept_matrices.append(matrices)
        kept_states.append(saved_state)
        layer_parameters.append(parameters)
    output = hidden.reshape(row_count, slot_count, width).astype(jnp.bfloat16)
    gradient = cotangent.astype(jnp.float32).reshape(row_count * slot_count, width) * is_real
    sums_by_layer = [None] * LAYERS
    for layer_index in reversed(range(LAYERS)):
        rounded = [
            matrix[layer_index].astype(jnp.bfloat16)
            for matrix in (w_query, w_key, w_value, w_out, w_inner, w_outer)
        ]
        matrices = (
            lax.all_gather(rounded[0], "dp", axis=0, tiled=True),
            lax.all_gather(rounded[1], "dp", axis=0, tiled=True),
            lax.all_gather(rounded[2], "dp", axis=0, tiled=True),
            lax.all_gather(rounded[3], "dp", axis=0, tiled=True),
            lax.all_gather(rounded[4], "dp", axis=0, tiled=True),
            lax.all_gather(rounded[5], "dp", axis=0, tiled=True),
        )
        gradient, layer_sums = layer_backward(
            gradient,
            matrices,
            layer_parameters[layer_index],
            allowed,
            kept_states[layer_index],
            row_count,
        )
        sums_by_layer[layer_index] = layer_sums
    stacked = [
        jnp.stack([sums_by_layer[layer_index][member_index] for layer_index in range(LAYERS)])
        for member_index in range(7)
    ]
    totals = lax.psum(
        (stacked[0], stacked[1], stacked[2], stacked[3], stacked[4], stacked[5], stacked[6]), "dp"
    )
    return (
        output,
        gradient.reshape(row_count, slot_count, width),
        totals[0],
        totals[1],
        totals[2],
        totals[3],
        totals[4],
        totals[5],
        totals[6],
    )


def solution(mesh):
    placed = (
        P("dp", None, None),
        P("dp", None),
        P(None, "dp", None),
        P(None, "dp", None),
        P(None, "dp", None),
        P(None, "dp", None),
        P(None, "dp", None),
        P(None, "dp", None),
        P(),
        P(),
        P(),
        P(),
        P(),
        P(),
        P(),
        P(),
        P(),
        P("dp", None, None),
    )
    return jax.shard_map(
        per_device,
        mesh=mesh,
        in_specs=placed,
        out_specs=(P("dp", None, None), P("dp", None, None), P(), P(), P(), P(), P(), P(), P()),
        check_vma=False,
    )
```

profile of v0, /device:TPU:0, one launch (start us, length us, event | category | flops | bytes accessed | tf_op | source)
XLA Modules:
  0.0 1452.5 jit_solution(14700106993869879353)
XLA Ops:
  30.5 40.1 %all-gather.25.cloned.1.call-done = bf16[1,1024,1024]{2,1,0:T(8,128)(2,1)} async-done(((bf16[1,32,1024]{2,1,0:T(8,128)(2,1)}), bf16[1,1024,1024]{2,1,0:T(8,128)(2,1)}) %all-gather.25.cloned.1.call-update) | async-done | bytes 2097168 | tf_op jit(solution)/shard_map/all_gather | solution.py:117
  79.1 5.5 copy.98
  84.5 44.2 %all-gather.27.cloned.1.call-done = bf16[1,1024,1024]{2,1,0:T(8,128)(2,1)} async-done(((bf16[1,32,1024]{2,1,0:T(8,128)(2,1)}), bf16[1,1024,1024]{2,1,0:T(8,128)(2,1)}) %all-gather.27.cloned.1.call-update) | async-done | bytes 2097168 | tf_op jit(solution)/shard_map/all_gather | solution.py:115
  137.2 5.5 copy.99
  142.6 44.2 %all-gather.29.cloned.1.call-done = bf16[1,1024,1024]{2,1,0:T(8,128)(2,1)} async-done(((bf16[1,32,1024]{2,1,0:T(8,128)(2,1)}), bf16[1,1024,1024]{2,1,0:T(8,128)(2,1)}) %all-gather.29.cloned.1.call-update) | async-done | bytes 2097168 | tf_op jit(solution)/shard_map/all_gather | solution.py:116
  195.3 5.5 copy.100
  202.3 64.4 %while.52 = (s32[]{:T(128)}, bf16[2,512,1024]{2,1,0:T(8,128)(2,1)}, f32[2,16,512,1]{2,1,3,0:T(8,128)S(1)}, bf16[2,512,16,64]{1,3,2,0:T(8,128)(2,1)}, pred[2,512,...) while((s32[]{:T(128)}, bf16[2,512,1024]{2,1,0:T(8,128)(2,1)}, ...), condition=%wide.region_5.6_spmd, body=%wide.region_2.5_spmd.sunk | while | flops 1120395264 | bytes 60295260 | solution.py:143
  203.8 10.0 fusion.310
  213.7 9.2 exponential_reduce_fusion.4
  222.9 10.2 fusion.311
  235.7 10.0 fusion.310
  245.7 9.2 exponential_reduce_fusion.4
  254.9 10.3 fusion.311
  275.3 48.6 %all-gather.33.cloned.1.call-done = bf16[1,1024,4096]{2,1,0:T(8,128)(2,1)} async-done(((bf16[1,32,4096]{2,1,0:T(8,128)(2,1)}), bf16[1,1024,4096]{2,1,0:T(8,128)(2,1)}) %all-gather.33.cloned.1.call-update) | async-done | bytes 8388624 | tf_op jit(solution)/shard_map/all_gather | solution.py:119
  323.9 49.6 %fusion.112 = (f32[1024,4096]{1,0:T(8,128)}, f32[1024,4096]{1,0:T(8,128)}) fusion(f32[4096]{0:T(1024)S(1)} %bitcast.401, bf16[1,1024,4096]{2,1,0:T(8,128)(2,1)} %all-gather.33.cloned.1.call-done, f32[1024,1024]{1,0:T(8,128)} %copy-done.18, f32[1024]{0:T(1024)S(1)} %bitcast.423, f32[1024]{0:T(1024)S(1)} %bitcast.389, f32[1024]{0:T(1024)S(1)} %fusion.230, ...), kind=kOutput, calls=%fused_computation.124 | convolution fusion | flops 8859418624 | bytes 46170112 | tf_op jit(solution)/shard_map/dot_general | solution.py:15
  373.5 29.2 %all-gather.35.cloned.1.call-done = bf16[1,4096,1024]{2,1,0:T(8,128)(2,1)} async-done(((bf16[1,128,1024]{2,1,0:T(8,128)(2,1)}), bf16[1,4096,1024]{2,1,0:T(8,128)(2,1)}) %all-gather.35.cloned.1.call-update) | async-done | bytes 8388624 | tf_op jit(solution)/shard_map/all_gather | solution.py:120
  402.7 24.8 %fusion.260 = (f32[1024]{0:T(1024)S(1)}, f32[1024,1024]{1,0:T(8,128)}) fusion(f32[1024]{0:T(1024)S(1)} %bitcast.425, bf16[1,4096,1024]{2,1,0:T(8,128)(2,1)} %all-gather.35.cloned.1.call-done, f32[1024,4096]{1,0:T(8,128)} %get-tuple-element.445, f32[1024,4096]{1,0:T(8,128)} %get-tuple-element.446, f32[4096]{0:T(1024)S(1)} %bitcast.402, ...), kind=kOutput, calls=%fused_computation.327 | convolution fusion | flops 8614050816 | bytes 50372608 | tf_op jit(solution)/shard_map/dot_general | solution.py:15
  431.8 28.7 %all-gather.39.cloned.1.call-done = bf16[1,1024,1024]{2,1,0:T(8,128)(2,1)} async-done(((bf16[1,32,1024]{2,1,0:T(8,128)(2,1)}), bf16[1,1024,1024]{2,1,0:T(8,128)(2,1)}) %all-gather.39.cloned.1.call-update) | async-done | bytes 2097168 | tf_op jit(solution)/shard_map/all_gather | solution.py:115
  465.8 6.4 reshape.444
  472.1 5.5 copy.106
  477.6 41.0 %all-gather.41.cloned.1.call-done = bf16[1,1024,1024]{2,1,0:T(8,128)(2,1)} async-done(((bf16[1,32,1024]{2,1,0:T(8,128)(2,1)}), bf16[1,1024,1024]{2,1,0:T(8,128)(2,1)}) %all-gather.41.cloned.1.call-update) | async-done | bytes 2097168 | tf_op jit(solution)/shard_map/all_gather | solution.py:116
  523.9 6.4 reshape.445
  530.3 5.6 copy.107
  535.9 40.9 %all-gather.37.cloned.1.call-done = bf16[1,1024,1024]{2,1,0:T(8,128)(2,1)} async-done(((bf16[1,32,1024]{2,1,0:T(8,128)(2,1)}), bf16[1,1024,1024]{2,1,0:T(8,128)(2,1)}) %all-gather.37.cloned.1.call-update) | async-done | bytes 2097168 | tf_op jit(solution)/shard_map/all_gather | solution.py:117
  582.0 6.4 reshape.443
  595.4 64.7 %while.53 = (s32[]{:T(128)}, bf16[2,512,1024]{2,1,0:T(8,128)(2,1)}, f32[2,16,512,1]{2,1,3,0:T(8,128)S(1)}, bf16[2,512,16,64]{1,3,2,0:T(8,128)(2,1)}, pred[2,512,...) while((s32[]{:T(128)}, bf16[2,512,1024]{2,1,0:T(8,128)(2,1)}, ...), condition=%wide.region_13.14_spmd, body=%wide.region_10.13_spmd.sunk | while | flops 1120395264 | bytes 60295260 | solution.py:143
  596.4 10.0 fusion.313
  606.4 9.2 exponential_reduce_fusion.5
  615.6 10.5 fusion.314
  628.7 10.0 fusion.313
  638.6 9.2 exponential_reduce_fusion.5
  647.9 10.3 fusion.314
  660.2 6.4 fusion.261
  669.7 44.3 %all-gather.45.cloned.1.call-done = bf16[1,1024,4096]{2,1,0:T(8,128)(2,1)} async-done(((bf16[1,32,4096]{2,1,0:T(8,128)(2,1)}), bf16[1,1024,4096]{2,1,0:T(8,128)(2,1)}) %all-gather.45.cloned.1.call-update) | async-done | bytes 8388624 | tf_op jit(solution)/shard_map/all_gather | solution.py:119
  713.9 49.4 %fusion.113 = (f32[1024,4096]{1,0:T(8,128)}, f32[1024,4096]{1,0:T(8,128)}) fusion(f32[4096]{0:T(1024)S(1)} %bitcast.404, bf16[1,1024,4096]{2,1,0:T(8,128)(2,1)} %all-gather.45.cloned.1.call-done, f32[1024,1024]{1,0:T(8,128)} %copy-done.22, f32[1024]{0:T(1024)S(1)} %bitcast.417, f32[1024]{0:T(1024)S(1)} %bitcast.393, f32[1024]{0:T(1024)S(1)} %fusion.232, ...), kind=kOutput, calls=%fused_computation.125 | convolution fusion | flops 8859418624 | bytes 46170112 | tf_op jit(solution)/shard_map/dot_general | solution.py:15
  763.4 29.4 %all-gather.47.cloned.1.call-done = bf16[1,4096,1024]{2,1,0:T(8,128)(2,1)} async-done(((bf16[1,128,1024]{2,1,0:T(8,128)(2,1)}), bf16[1,4096,1024]{2,1,0:T(8,128)(2,1)}) %all-gather.47.cloned.1.call-update) | async-done | bytes 8388624 | tf_op jit(solution)/shard_map/all_gather | solution.py:120
  792.8 24.7 %fusion.262 = (f32[1024]{0:T(1024)S(1)}, f32[1024,1024]{1,0:T(8,128)}) fusion(f32[1024]{0:T(1024)S(1)} %bitcast.419, bf16[1,4096,1024]{2,1,0:T(8,128)(2,1)} %all-gather.47.cloned.1.call-done, f32[1024,4096]{1,0:T(8,128)} %get-tuple-element.451, f32[1024,4096]{1,0:T(8,128)} %get-tuple-element.452, f32[4096]{0:T(1024)S(1)} %bitcast.405, ...), kind=kOutput, calls=%fused_computation.329 | convolution fusion | flops 8614050816 | bytes 50372608 | tf_op jit(solution)/shard_map/dot_general | solution.py:15
  827.3 25.1 %convert_reduce_fusion = (f32[4096]{0:T(1024)}, bf16[1024,4096]{1,0:T(8,128)(2,1)}) fusion(f32[1024,4096]{1,0:T(8,128)} %get-tuple-element.451, bf16[1,4096,1024]{2,1,0:T(8,128)(2,1)} %all-gather.47.cloned.1.call-done, f32[1024,1024]{1,0:T(8,128)} %copy-done.26, f32[1024]{0:T(1024)S(1)} %negate_multiply_fusion.5, f32[1024,4096]{1,0:T(8,128)} %get-tuple-element.452, ...), kind=kOutput, calls=%fused_computation.126 | convolution fusion | flops 8663330816 | bytes 54562816 | tf_op jit(solution)/shard_map/dot_general | solution.py:19
  852.5 17.3 %fusion.238 = (f32[1024]{0:T(1024)}, f32[1024]{0:T(1024)S(1)}, f32[1024,1024]{1,0:T(8,128)S(1)}) fusion(f32[1024]{0:T(1024)S(1)} %bitcast.395, f32[1024,1024]{1,0:T(8,128)} %copy-done.22, f32[1024]{0:T(1024)S(1)} %broadcast_multiply_fusion.1, bf16[1024,4096]{1,0:T(8,128)(2,1)} %get-tuple-element.459, ...), kind=kOutput, calls=%fused_computation.305 | convolution fusion | flops 8597272576 | bytes 29380608 | tf_op jit(solution)/shard_map/dot_general | solution.py:19
  890.0 160.9 %while.54 = (s32[]{:T(128)}, bf16[2,512,1024]{1,2,0:T(8,128)(2,1)}, bf16[2,512,1024]{2,1,0:T(8,128)(2,1)}, bf16[2,512,1024]{1,2,0:T(8,128)(2,1)}, bf16[2,512,16,...) while((s32[]{:T(128)}, bf16[2,512,1024]{1,2,0:T(8,128)(2,1)}, ...), condition=%wide.region_24.25_spmd, body=%wide.region_22.24_spmd.sunk | while | flops 2745713664 | bytes 246779664 | solution.py:197
  891.4 11.4 subtract_exponential_fusion.4
  902.9 8.1 fusion.326
  911.0 22.3 %multiply_convert_fusion.16 = bf16[16,64,512]{2,1,0:T(8,128)(2,1)S(1)} fusion(f32[16,512,512]{1,2,0:T(8,128)} %subtract_exponential_fusion.4, f32[16,512,512]{1,2,0:T(8,128)} %fusion.326, pred[512,512]{0,1:T(8,128)(4,1)S(1)} %dynamic-slice_bitcast_fusion.15, bf16[2,512,16,64]{1,3,2,0:T(8,128)(2,1)} %get-tuple-element.776, s32[]{:T(128)} %get-tuple-element.761), kind=kOutput, calls=%fused_computation.54.clone.1 | convolution fusion | flops 558899712 | bytes 69468672 | tf_op jit(solution)/shard_map/while/body/eval_jaxpr/hqk,khd->qhd/dot_general | solution.py:88
  933.3 8.6 fusion.325
  944.7 23.4 %multiply_convert_fusion.17 = bf16[16,64,512]{2,1,0:T(8,128)(2,1)} fusion(f32[16,512,512]{1,2,0:T(8,128)} %subtract_exponential_fusion.4, f32[16,512,512]{1,2,0:T(8,128)} %fusion.326, pred[512,512]{0,1:T(8,128)(4,1)S(1)} %dynamic-slice_bitcast_fusion.15, bf16[2,512,16,64]{1,3,2,0:T(8,128)(2,1)} %get-tuple-element.778, s32[]{:T(128)} %get-tuple-element.761), kind=kOutput, calls=%fused_computation.53.clone.1 | convolution fusion | flops 558899712 | bytes 69468672 | tf_op jit(solution)/shard_map/while/body/eval_jaxpr/hqk,qhd->khd/dot_general | solution.py:92
  971.7 11.4 subtract_exponential_fusion.4
  983.1 8.1 fusion.326
  991.2 22.3 %multiply_convert_fusion.16 = bf16[16,64,512]{2,1,0:T(8,128)(2,1)S(1)} fusion(f32[16,512,512]{1,2,0:T(8,128)} %subtract_exponential_fusion.4, f32[16,512,512]{1,2,0:T(8,128)} %fusion.326, pred[512,512]{0,1:T(8,128)(4,1)S(1)} %dynamic-slice_bitcast_fusion.15, bf16[2,512,16,64]{1,3,2,0:T(8,128)(2,1)} %get-tuple-element.776, s32[]{:T(128)} %get-tuple-element.761), kind=kOutput, calls=%fused_computation.54.clone.1 | convolution fusion | flops 558899712 | bytes 69468672 | tf_op jit(solution)/shard_map/while/body/eval_jaxpr/hqk,khd->qhd/dot_general | solution.py:88
  1013.5 8.6 fusion.325
  1025.0 23.4 %multiply_convert_fusion.17 = bf16[16,64,512]{2,1,0:T(8,128)(2,1)} fusion(f32[16,512,512]{1,2,0:T(8,128)} %subtract_exponential_fusion.4, f32[16,512,512]{1,2,0:T(8,128)} %fusion.326, pred[512,512]{0,1:T(8,128)(4,1)S(1)} %dynamic-slice_bitcast_fusion.15, bf16[2,512,16,64]{1,3,2,0:T(8,128)(2,1)} %get-tuple-element.778, s32[]{:T(128)} %get-tuple-element.761), kind=kOutput, calls=%fused_computation.53.clone.1 | convolution fusion | flops 558899712 | bytes 69468672 | tf_op jit(solution)/shard_map/while/body/eval_jaxpr/hqk,qhd->khd/dot_general | solution.py:92
  1077.6 25.3 %convert_reduce_fusion.1 = (f32[4096]{0:T(1024)}, bf16[1024,4096]{1,0:T(8,128)(2,1)}) fusion(f32[1024,4096]{1,0:T(8,128)} %get-tuple-element.445, bf16[1,4096,1024]{2,1,0:T(8,128)(2,1)} %all-gather.35.cloned.1.call-done, f32[1024,1024]{1,0:T(8,128)} %copy-done.24, f32[1024]{0:T(1024)S(1)} %negate_multiply_fusion.3, f32[1024,4096]{1,0:T(8,128)} %get-tuple-element.446, ...), kind=kOutput, calls=%fused_computation.127 | convolution fusion | flops 8663330816 | bytes 54562816 | tf_op jit(solution)/shard_map/dot_general | solution.py:19
  1102.9 17.1 %fusion.237 = (f32[1024]{0:T(1024)}, f32[1024]{0:T(1024)S(1)}, f32[1024,1024]{1,0:T(8,128)S(1)}) fusion(f32[1024]{0:T(1024)S(1)} %bitcast.391, f32[1024,1024]{1,0:T(8,128)} %copy-done.18, f32[1024]{0:T(1024)S(1)} %copy-done.46, bf16[1024,4096]{1,0:T(8,128)(2,1)} %get-tuple-element.461, bf16[1,1024,4096]{2,1,0:T(8,128)(2,1)} %all-gather.33.cloned.1.call-done, ...), kind=kOutput, calls=%fused_computation.304 | convolution fusion | flops 8597272576 | bytes 29380608 | tf_op jit(solution)/shard_map/dot_general | solution.py:19
  1140.6 160.7 %while.55 = (s32[]{:T(128)}, bf16[2,512,1024]{1,2,0:T(8,128)(2,1)}, bf16[2,512,1024]{2,1,0:T(8,128)(2,1)}, bf16[2,512,1024]{1,2,0:T(8,128)(2,1)}, bf16[2,512,16,...) while((s32[]{:T(128)}, bf16[2,512,1024]{1,2,0:T(8,128)(2,1)}, ...), condition=%wide.region_31.32_spmd, body=%wide.region_29.31_spmd.sunk | while | flops 2745713664 | bytes 246779664 | solution.py:197
  1141.6 11.4 subtract_exponential_fusion.5
  1153.1 8.1 fusion.338
  1161.2 22.3 %multiply_convert_fusion.18 = bf16[16,64,512]{2,1,0:T(8,128)(2,1)S(1)} fusion(f32[16,512,512]{1,2,0:T(8,128)} %subtract_exponential_fusion.5, f32[16,512,512]{1,2,0:T(8,128)} %fusion.338, pred[512,512]{0,1:T(8,128)(4,1)S(1)} %dynamic-slice_bitcast_fusion.17, bf16[2,512,16,64]{1,3,2,0:T(8,128)(2,1)} %get-tuple-element.809, s32[]{:T(128)} %get-tuple-element.794), kind=kOutput, calls=%fused_computation.93.clone.1 | convolution fusion | flops 558899712 | bytes 69468672 | tf_op jit(solution)/shard_map/while/body/eval_jaxpr/hqk,khd->qhd/dot_general | solution.py:88
  1183.5 8.6 fusion.337
  1195.0 23.4 %multiply_convert_fusion.19 = bf16[16,64,512]{2,1,0:T(8,128)(2,1)} fusion(f32[16,512,512]{1,2,0:T(8,128)} %subtract_exponential_fusion.5, f32[16,512,512]{1,2,0:T(8,128)} %fusion.338, pred[512,512]{0,1:T(8,128)(4,1)S(1)} %dynamic-slice_bitcast_fusion.17, bf16[2,512,16,64]{1,3,2,0:T(8,128)(2,1)} %get-tuple-element.811, s32[]{:T(128)} %get-tuple-element.794), kind=kOutput, calls=%fused_computation.92.clone.1 | convolution fusion | flops 558899712 | bytes 69468672 | tf_op jit(solution)/shard_map/while/body/eval_jaxpr/hqk,qhd->khd/dot_general | solution.py:92
  1222.0 11.4 subtract_exponential_fusion.5
  1233.4 8.1 fusion.338
  1241.5 22.3 %multiply_convert_fusion.18 = bf16[16,64,512]{2,1,0:T(8,128)(2,1)S(1)} fusion(f32[16,512,512]{1,2,0:T(8,128)} %subtract_exponential_fusion.5, f32[16,512,512]{1,2,0:T(8,128)} %fusion.338, pred[512,512]{0,1:T(8,128)(4,1)S(1)} %dynamic-slice_bitcast_fusion.17, bf16[2,512,16,64]{1,3,2,0:T(8,128)(2,1)} %get-tuple-element.809, s32[]{:T(128)} %get-tuple-element.794), kind=kOutput, calls=%fused_computation.93.clone.1 | convolution fusion | flops 558899712 | bytes 69468672 | tf_op jit(solution)/shard_map/while/body/eval_jaxpr/hqk,khd->qhd/dot_general | solution.py:88
  1263.8 8.6 fusion.337
  1275.3 23.4 %multiply_convert_fusion.19 = bf16[16,64,512]{2,1,0:T(8,128)(2,1)} fusion(f32[16,512,512]{1,2,0:T(8,128)} %subtract_exponential_fusion.5, f32[16,512,512]{1,2,0:T(8,128)} %fusion.338, pred[512,512]{0,1:T(8,128)(4,1)S(1)} %dynamic-slice_bitcast_fusion.17, bf16[2,512,16,64]{1,3,2,0:T(8,128)(2,1)} %get-tuple-element.811, s32[]{:T(128)} %get-tuple-element.794), kind=kOutput, calls=%fused_computation.92.clone.1 | convolution fusion | flops 558899712 | bytes 69468672 | tf_op jit(solution)/shard_map/while/body/eval_jaxpr/hqk,qhd->khd/dot_general | solution.py:92
  1326.7 109.9 %all-reduce.3.cloned.1.call-done = (f32[2,1024]{1,0:T(2,128)}, f32[2,1024]{1,0:T(2,128)}, f32[2,1024]{1,0:T(2,128)}, f32[2,4096]{1,0:T(2,128)}, f32[2,1024]{1,0:...) async-done(((f32[2,1024]{1,0:T(2,128)}, f32[2,1024]{1,0:T(2,128)}, f32[2,1024]{1,0:T(2,128)}, f32[2,4096]{1,0:T(2,128)}, f32[2,1024]{1,0:T(2,128)}, ...) | async-done | bytes 81936 | tf_op jit(solution)/shard_map/psum | solution.py:310
  (394 shorter events, 235.8 us)
Async XLA Ops:
  7.2 9.3 copy-start.32
  7.2 63.4 %all-gather.25.cloned.1.call-start = ((), (), s32[]{:S(2)}) async-start(), calls=%async_computation | async-start | bytes 2162688 | tf_op jit(solution)/shard_map/all_gather | solution.py:117
  9.0 119.7 %all-gather.27.cloned.1.call-start = ((), (), s32[]{:S(2)}) async-start(), calls=%async_computation.1 | async-start | bytes 2162688 | tf_op jit(solution)/shard_map/all_gather | solution.py:115
  10.7 11.0 copy-start.94
  10.7 176.1 %all-gather.29.cloned.1.call-start = ((), (), s32[]{:S(2)}) async-start(), calls=%async_computation.2 | async-start | bytes 2162688 | tf_op jit(solution)/shard_map/all_gather | solution.py:116
  12.4 10.9 copy-start.78
  12.4 11.5 copy-start.79
  12.4 12.1 copy-start.80
  12.4 12.7 copy-start.81
  12.5 13.3 copy-start.55
  12.5 13.9 copy-start.82
  12.5 14.5 copy-start.83
  12.5 15.1 %copy-start.84 = (f32[2,1024]{1,0:T(2,128)S(1)}, f32[2,1024]{1,0:T(2,128)}, u32[]{:S(2)}) copy-start(f32[2,1024]{1,0:T(2,128)} %param.42) | copy-start | bytes 24580
  12.5 254.3 %all-gather.31.cloned.1.call-start = ((), (), s32[]{:S(2)}) async-start(), calls=%async_computation.3 | async-start | bytes 2162688 | tf_op jit(solution)/shard_map/all_gather | solution.py:118
  13.5 14.7 %copy-start.85 = (f32[2,1024]{1,0:T(2,128)S(1)}, f32[2,1024]{1,0:T(2,128)}, u32[]{:S(2)}) copy-start(f32[2,1024]{1,0:T(2,128)} %param.40) | copy-start | bytes 24580
  13.5 15.9 %copy-start.6 = (bf16[2,512,1024]{2,1,0:T(8,128)(2,1)S(1)}, bf16[2,512,1024]{2,1,0:T(8,128)(2,1)}, u32[]{:S(2)}) copy-start(bf16[2,512,1024]{2,1,0:T(8,128)(2,1)} %param.43) | copy-start | bytes 6291460
  14.2 309.6 %all-gather.33.cloned.1.call-start = ((), (), s32[]{:S(2)}) async-start(), calls=%async_computation.4 | async-start | bytes 8650752 | tf_op jit(solution)/shard_map/all_gather | solution.py:119
  16.4 386.2 %all-gather.35.cloned.1.call-start = ((), (), s32[]{:S(2)}) async-start(), calls=%async_computation.5 | async-start | bytes 8650752 | tf_op jit(solution)/shard_map/all_gather | solution.py:120
  17.4 443.1 %all-gather.39.cloned.1.call-start = ((), (), s32[]{:S(2)}) async-start(), calls=%async_computation.7 | async-start | bytes 2162688 | tf_op jit(solution)/shard_map/all_gather | solution.py:115
  18.1 500.5 %all-gather.41.cloned.1.call-start = ((), (), s32[]{:S(2)}) async-start(), calls=%async_computation.8 | async-start | bytes 2162688 | tf_op jit(solution)/shard_map/all_gather | solution.py:116
  18.9 557.9 %all-gather.37.cloned.1.call-start = ((), (), s32[]{:S(2)}) async-start(), calls=%async_computation.6 | async-start | bytes 2162688 | tf_op jit(solution)/shard_map/all_gather | solution.py:117
  19.6 640.5 %all-gather.43.cloned.1.call-start = ((), (), s32[]{:S(2)}) async-start(), calls=%async_computation.9 | async-start | bytes 2162688 | tf_op jit(solution)/shard_map/all_gather | solution.py:118
  20.2 693.7 %all-gather.45.cloned.1.call-start = ((), (), s32[]{:S(2)}) async-start(), calls=%async_computation.10 | async-start | bytes 8650752 | tf_op jit(solution)/shard_map/all_gather | solution.py:119
  21.0 771.8 %all-gather.47.cloned.1.call-start = ((), (), s32[]{:S(2)}) async-start(), calls=%async_computation.11 | async-start | bytes 8650752 | tf_op jit(solution)/shard_map/all_gather | solution.py:120
  21.5 1415.1 %all-reduce.3.cloned.1.call-start = ((), (), s32[]{:S(2)}) async-start(), calls=%async_computation.12 | async-start | bytes 163840 | tf_op jit(solution)/shard_map/psum | solution.py:310
  25.7 376.9 %copy-start.59 = (f32[1,1024]{1,0:T(1,128)}, f32[1,1024]{1,0:T(1,128)S(1)}, u32[]{:S(2)}) copy-start(f32[1,1024]{1,0:T(1,128)S(1)} %get-tuple-element.432) | copy-start | bytes 12292
  26.4 376.3 %copy-start.65 = (f32[1,4096]{1,0:T(1,128)}, f32[1,4096]{1,0:T(1,128)S(1)}, u32[]{:S(2)}) copy-start(f32[1,4096]{1,0:T(1,128)S(1)} %get-tuple-element.424) | copy-start | bytes 49156
  272.1 130.5 %copy-start.45 = (f32[1024]{0:T(1024)}, f32[1024]{0:T(1024)S(1)}, u32[]{:S(2)}) copy-start(f32[1024]{0:T(1024)S(1)} %broadcast_multiply_fusion.3) | copy-start | bytes 12292
  275.3 127.4 %copy-start.57 = (f32[1024]{0:T(1024)}, f32[1024]{0:T(1024)S(1)}, u32[]{:S(2)}) copy-start(f32[1024]{0:T(1024)S(1)} %fusion.230) | copy-start | bytes 12292
  323.9 78.8 %copy-start.91 = (f32[1,1024]{1,0:T(1,128)S(1)}, f32[1,1024]{1,0:T(1,128)}, u32[]{:S(2)}) copy-start(f32[1,1024]{1,0:T(1,128)} %get-tuple-element.430) | copy-start | bytes 12292
  427.5 232.6 %copy-start.37 = (f32[1024]{0:T(1024)}, f32[1024]{0:T(1024)S(1)}, u32[]{:S(2)}) copy-start(f32[1024]{0:T(1024)S(1)} %broadcast_multiply_fusion.2) | copy-start | bytes 12292
  430.5 30.0 %copy-start.90 = (f32[1,1024]{1,0:T(1,128)S(1)}, f32[1,1024]{1,0:T(1,128)}, u32[]{:S(2)}) copy-start(f32[1,1024]{1,0:T(1,128)} %get-tuple-element.435) | copy-start | bytes 12292
  430.5 229.6 %copy-start.43 = (f32[1024]{0:T(1024)}, f32[1024]{0:T(1024)S(1)}, u32[]{:S(2)}) copy-start(f32[1024]{0:T(1024)S(1)} %fusion.231) | copy-start | bytes 12292
  530.3 46.5 %copy-start.89 = (f32[1,1024]{1,0:T(1,128)S(1)}, f32[1,1024]{1,0:T(1,128)}, u32[]{:S(2)}) copy-start(f32[1,1024]{1,0:T(1,128)} %get-tuple-element.437) | copy-start | bytes 12292
  595.4 64.8 %copy-start.88 = (f32[1,1024]{1,0:T(1,128)S(1)}, f32[1,1024]{1,0:T(1,128)}, u32[]{:S(2)}) copy-start(f32[1,1024]{1,0:T(1,128)} %get-tuple-element.439) | copy-start | bytes 12292
  666.6 47.4 %copy-start.61 = (f32[1,1024]{1,0:T(1,128)S(1)}, f32[1,1024]{1,0:T(1,128)}, u32[]{:S(2)}) copy-start(f32[1,1024]{1,0:T(1,128)} %get-tuple-element.431) | copy-start | bytes 12292
  666.6 47.4 %copy-start.67 = (f32[1,4096]{1,0:T(1,128)S(1)}, f32[1,4096]{1,0:T(1,128)}, u32[]{:S(2)}) copy-start(f32[1,4096]{1,0:T(1,128)} %get-tuple-element.423) | copy-start | bytes 49156
  666.6 47.4 %copy-start.86 = (f32[1,1024]{1,0:T(1,128)S(1)}, f32[1,1024]{1,0:T(1,128)}, u32[]{:S(2)}) copy-start(f32[1,1024]{1,0:T(1,128)} %get-tuple-element.433) | copy-start | bytes 12292
  713.9 78.8 %copy-start.87 = (f32[1,1024]{1,0:T(1,128)S(1)}, f32[1,1024]{1,0:T(1,128)}, u32[]{:S(2)}) copy-start(f32[1,1024]{1,0:T(1,128)} %get-tuple-element.429) | copy-start | bytes 12292
  792.8 24.7 %copy-start.7 = (bf16[2,512,1024]{2,1,0:T(8,128)(2,1)S(1)}, bf16[2,512,1024]{2,1,0:T(8,128)(2,1)}, u32[]{:S(2)}) copy-start(bf16[2,512,1024]{2,1,0:T(8,128)(2,1)} %param.43) | copy-start | bytes 6291460
  792.8 24.7 %copy-start.41 = (f32[1,4,2,128]{3,1,2,0:T(4,128)S(1)}, f32[1,4,2,128]{3,1,2,0:T(4,128)}, u32[]{:S(2)}) copy-start(f32[1,4,2,128]{3,1,2,0:T(4,128)} %copy.157) | copy-start | bytes 12292
  792.8 24.7 %copy-start.42 = (f32[1,1024]{1,0:T(1,128)S(1)}, f32[1,1024]{1,0:T(1,128)}, u32[]{:S(2)}) copy-start(f32[1,1024]{1,0:T(1,128)} %get-tuple-element.425) | copy-start | bytes 12292
  852.5 17.3 %copy-start.54 = (f32[1024]{0:T(1024)S(1)}, f32[1024]{0:T(1024)}, u32[]{:S(2)}) copy-start(f32[1024]{0:T(1024)} %copy-done.53) | copy-start | bytes 12292
  852.5 17.3 %copy-start.23 = (f32[1024,1024]{1,0:T(8,128)S(1)}, f32[1024,1024]{1,0:T(8,128)}, u32[]{:S(2)}) copy-start(f32[1024,1024]{1,0:T(8,128)} %copy-done.22) | copy-start | bytes 12582916
  891.4 11.4 copy-start.5
  933.3 8.6 copy-start.13
  933.3 8.6 copy-start.16
  971.6 11.5 copy-start.5
  1013.5 8.6 copy-start.13
  1013.5 8.6 copy-start.16
  1050.9 8.3 copy-start.15
  1077.6 25.3 %copy-start.46 = (f32[1024]{0:T(1024)S(1)}, f32[1024]{0:T(1024)}, u32[]{:S(2)}) copy-start(f32[1024]{0:T(1024)} %copy-done.45) | copy-start | bytes 12292
  1077.6 25.3 %copy-start.60 = (f32[1,1024]{1,0:T(1,128)S(1)}, f32[1,1024]{1,0:T(1,128)}, u32[]{:S(2)}) copy-start(f32[1,1024]{1,0:T(1,128)} %copy-done.59) | copy-start | bytes 12292
  1102.9 17.1 %copy-start.50 = (f32[1024]{0:T(1024)S(1)}, f32[1024]{0:T(1024)}, u32[]{:S(2)}) copy-start(f32[1024]{0:T(1024)} %copy-done.49) | copy-start | bytes 12292
  1102.9 17.1 %copy-start.19 = (f32[1024,1024]{1,0:T(8,128)S(1)}, f32[1024,1024]{1,0:T(8,128)}, u32[]{:S(2)}) copy-start(f32[1024,1024]{1,0:T(8,128)} %copy-done.18) | copy-start | bytes 12582916
  1102.9 17.1 %copy-start.58 = (f32[1024]{0:T(1024)S(1)}, f32[1024]{0:T(1024)}, u32[]{:S(2)}) copy-start(f32[1024]{0:T(1024)} %copy-done.57) | copy-start | bytes 12292
  1141.6 11.4 copy-start.4
  1183.5 8.6 copy-start.8
  1183.5 8.6 copy-start.11
  1221.9 11.4 copy-start.4
  1263.8 8.6 copy-start.8
  1263.8 8.6 copy-start.11
  1305.5 8.0 copy-start.74
  1305.5 8.0 copy-start.75
  (60 other events, 213.8 us)
Sparse Core Ops, SparseCore 0:
  11.5 59.0 all-gather.24
  73.4 55.2 all-gather.26
  131.5 55.2 all-gather.28
  189.5 55.2 all-gather.30
  247.5 76.3 all-gather.32
  326.6 76.0 all-gather.34
  405.5 54.9 all-gather.38
  463.4 55.2 all-gather.40
  521.5 55.2 all-gather.36
  579.5 55.2 all-gather.42
  637.6 76.2 all-gather.44
  716.6 76.0 all-gather.46
  1314.3 122.2 all-reduce.2
where the time goes:
time: 1460 us; the launch traced here: 1450 us
  matrix products  676 us (46%)
  waiting for transfers between devices  504 us (35%)
  local copies, waits for them, and re-layouts  181 us (12%)
  other arithmetic  73.8 us (5%)
  between operations  15.2 us (1%)
    dot_general x12, matrix products, product(): return jnp.dot(left, right, preferred_element_type=jnp.float32)  190 us
    psum x1, waiting for transfers between devices, per_device(): lax.psum((stacked[0], stacked[1], stacked[2], stacked[3], stacked[4], sta...  110 us
    dot_general x12, matrix products, product_back(): lax.dot_general(left, right, (((1,), (1,)), ((), ())), preferred_element_...  110 us
    dot_general x4, matrix products, attend_backward(): jnp.einsum('hqk,qhd->khd', grad_scores, query_rows, preferred_element_typ...  93.6 us
    all_gather x2, waiting for transfers between devices, fetch_forward(): lax.all_gather(rounded[4], 'dp', axis=0, tiled=True)  92.8 us
    dot_general x4, matrix products, attend_backward(): jnp.einsum('hqk,khd->qhd', grad_scores, key_rows, preferred_element_type=...  89.1 us
    dot_general x8, matrix products, row_scores(): jnp.einsum('qhd,khd->hqk', query_rows, key_rows, preferred_element_type=j...  85.6 us
    all_gather x2, waiting for transfers between devices, fetch_forward(): lax.all_gather(rounded[1], 'dp', axis=0, tiled=True)  85.2 us
  transfers between devices with their start and end apart: 13, of which 11 were waited for; matrix products, arithmetic and copies ran while one was open for 27% of the time, Pallas kernels for 0%

commit v1 on v0

v1 whole, which is shorter than its diff:
```python
import functools

import jax
import jax.numpy as jnp
from jax import lax
from jax.experimental import pallas as pl
from jax.experimental.pallas import tpu as pltpu
from jax.sharding import PartitionSpec as P

HEADS = 16
LAYERS = 2
EPSILON = 1e-12
NEGATIVE = -1e9
PADDING_ID = 1000
MESH = pl.DeviceIdType.MESH
HBM = pltpu.MemorySpace.HBM
VMEM = pltpu.VMEM
DMA = pltpu.SemaphoreType.DMA

WIDTH = 512
GROUPS = 24
AT_OUT, AT_INNER, AT_OUTER = 6, 8, 16
BLOCK = 128
WINDOW = 256
ROW_TILE = 128
ROOT_HALF = 0.7071067811865476
DENSITY = 0.3989422804014327
B_Q, B_K, B_V, B_OUT, B_OUTER, S_ATTN, S_FFN, G_ATTN, G_FFN = range(9)
D_Q, D_V, D_OUT, D_OUTER, D_ATTN, D_FFN, D_INNER = range(7)
SUM_ROWS = 16


def chip_dims(devices):
    bits = (devices // 2).bit_length() - 1
    first = -(-bits // 3)
    second = -(-(bits - first) // 2)
    return (1 << first, 1 << second, 1 << (bits - first - second))


ORDERS = (((0, 2, 1), (1, 0, 2)), ((0, 1, 2), (2, 0, 1)))
SLOTS = 8


class Gather:
    def __init__(self, dims, own, buf, ssem, rsem, total):
        self.dims, self.own, self.buf = dims, own, buf
        self.ssem, self.rsem, self.total = ssem, rsem, total
        self.me = lax.axis_index("dp")
        _, n1, n2 = dims
        self.core = lax.rem(self.me, 2)
        chip = self.me // 2
        self.at = (chip // (n1 * n2), lax.rem(chip // n2, n1), lax.rem(chip, n2))
        self.step = (n1 * n2 * 2, n2 * 2, 2)
        rows, cols = own.shape[-2:]
        if rows % 32 == 0:
            cut = rows * 3 // 4
            self.parts = (
                (pl.ds(0, cut), pl.ds(0, cols)),
                (pl.ds(cut, rows - cut), pl.ds(0, cols)),
            )
        else:
            cut = cols * 3 // 4
            self.parts = (
                (pl.ds(0, rows), pl.ds(0, cut)),
                (pl.ds(0, rows), pl.ds(cut, cols - cut)),
            )

    def peers(self, dim):
        if dim == 3:
            return [self.me + 1 - 2 * self.core]
        out = []
        for d in range(1, self.dims[dim]):
            to = lax.rem(self.at[dim] + d, self.dims[dim])
            out.append(self.me + (to - self.at[dim]) * self.step[dim])
        return out

    def copies(self, g, par, s, p):
        order = ORDERS[par][s] + (3,)
        full = order[:p]
        where = tuple(
            pl.ds(0, self.dims[d]) if d in full else self.at[d] for d in range(3)
        )
        sub = self.parts[s]
        dst = self.buf.at[(g,) + where + (self.core,) + sub]
        src = self.own.at[(g,) + sub] if p == 0 else dst
        slot = lax.rem(g, SLOTS)
        first = sum(self.dims[d] - 1 for d in order[:p])
        return [
            pltpu.make_async_remote_copy(
                src_ref=src,
                dst_ref=dst,
                send_sem=self.ssem.at[slot, s, first + i],
                recv_sem=self.rsem.at[slot, s, first + i],
                device_id=(to,),
                device_id_type=MESH,
            )
            for i, to in enumerate(self.peers(order[p]))
        ]

    def barrier(self):
        bar = pltpu.get_barrier_semaphore()
        everyone = [to for d in range(4) for to in self.peers(d)]
        for to in everyone:
            pl.semaphore_signal(bar, inc=1, device_id=(to,), device_id_type=MESH)
        pl.semaphore_wait(bar, len(everyone))

    def pump(self, pair_step, par):
        for p in (3, 2, 1, 0):
            pair = pair_step - p

            @pl.when((pair >= 0) & (pair < self.total // 2))
            def _():
                g = 2 * pair + par
                for s in range(2):
                    if p > 0:
                        for c in self.copies(g, par, s, p - 1):
                            c.wait()
                    for c in self.copies(g, par, s, p):
                        c.start()

    def arrive(self, pair, par):
        for s in range(2):
            for c in self.copies(2 * pair + par, par, s, 3):
                c.wait()


def gather_kernel(dims, total, own, buf, ssem, rsem, lsem):
    gather = Gather(dims, own, buf, ssem, rsem, total)
    here = pltpu.make_async_copy(
        own, buf.at[(pl.ds(0, total),) + gather.at + (gather.core,)], lsem
    )
    here.start()
    gather.barrier()
    here.wait()

    def body(step, _):
        for par in range(2):
            gather.pump(step, par)

            @pl.when(step >= 4)
            def _():
                gather.arrive(step - 4, par)

        return 0

    lax.fori_loop(0, total // 2 + 4, body, 0)


def gather_weights(own, devices):
    total, rows, cols = own.shape
    dims = chip_dims(devices)
    sems = sum(d - 1 for d in dims) + 1
    return pl.pallas_call(
        functools.partial(gather_kernel, dims, total),
        out_shape=jax.ShapeDtypeStruct((total,) + dims + (2, rows, cols), own.dtype),
        in_specs=[pl.BlockSpec(memory_space=HBM)],
        out_specs=pl.BlockSpec(memory_space=HBM),
        scratch_shapes=[DMA((SLOTS, 2, sems)), DMA((SLOTS, 2, sems)), DMA],
        compiler_params=pltpu.CompilerParams(collective_id=0, has_side_effects=True),
    )(own)


def matmul(left, right):
    return jnp.dot(left, right, preferred_element_type=jnp.float32)


def matmul_nt(left, right):
    return lax.dot_general(
        left, right, (((1,), (1,)), ((), ())), preferred_element_type=jnp.float32
    )


def matmul_tn(left, right):
    return lax.dot_general(
        left, right, (((0,), (0,)), ((), ())), preferred_element_type=jnp.float32
    )


def loop(count, body):
    lax.fori_loop(0, count, lambda i, c: (body(i), c)[1], 0)


def tile(i, size):
    return pl.ds(pl.multiple_of(i * size, size), size)


def window_starts(slots):
    return [
        min(max(b * BLOCK - (WINDOW - BLOCK) // 2, 0), slots - WINDOW)
        for b in range(slots // BLOCK)
    ]


def pair_stack(rows):
    lane = lax.broadcasted_iota(jnp.int32, rows.shape, 1)
    zero = jnp.zeros_like(rows)
    half = rows.shape[1] // 2
    return jnp.concatenate(
        [jnp.where(lane < half, rows, zero), jnp.where(lane < half, zero, rows)], axis=0
    )


def pair_join(stacked):
    rows = stacked.shape[0] // 2
    lane = lax.broadcasted_iota(jnp.int32, (rows, stacked.shape[1]), 1)
    return jnp.where(lane < stacked.shape[1] // 2, stacked[:rows], stacked[rows:])


def forward_kernel(
    dims,
    wbuf, tokens, id_row, id_col, vectors, inner_bias,
    out, saved_qkv, saved_p, saved_x, saved_s, saved_d,
    h, a, qkv, o, z, u, w, p_stage, d_stage, x_stage, s_stage,
    wsem, psem, dsem, xsem, ssem, qsem, tsem,
):
    rows, slots = dims
    count = h.shape[0]
    pairs = HEADS // 2
    total = LAYERS * GROUPS

    def wload(g):
        slot = lax.rem(g, 3)
        return pltpu.make_async_copy(wbuf.at[g], w.at[slot], wsem.at[slot])

    def weights(g):
        @pl.when(g + 2 < total)
        def _():
            wload(g + 2).start()

        wload(g).wait()
        return w[lax.rem(g, 3)]

    load = pltpu.make_async_copy(tokens, a, tsem)
    load.start()
    wload(0).start()
    wload(1).start()
    load.wait()

    def widen(i):
        h[tile(i, ROW_TILE), :] = a[tile(i, ROW_TILE), :].astype(jnp.float32)

    loop(count // ROW_TILE, widen)

    def normalize(l, which):
        bias, gain, shift = ((B_OUT, G_ATTN, S_ATTN), (B_OUTER, G_FFN, S_FFN))[which]
        store_x = pltpu.make_async_copy(x_stage, saved_x.at[l, which], xsem)
        store_s = pltpu.make_async_copy(s_stage, saved_s.at[l, which], ssem)
        if which == 1:
            store_x.wait()
            store_s.wait()
        else:

            @pl.when(l > 0)
            def _():
                store_x.wait()
                store_s.wait()

        def body(i):
            t = tile(i, ROW_TILE)
            r = h[t, :] + vectors[l, bias : bias + 1, :]
            centered = r - jnp.mean(r, axis=1, keepdims=True)
            var = jnp.mean(centered * centered, axis=1, keepdims=True)
            scale = lax.rsqrt(var + EPSILON)
            xhat = centered * scale
            x_stage[t, :] = xhat
            s_stage[t, :] = jnp.broadcast_to(scale, (ROW_TILE, 128))
            y = xhat * vectors[l, gain : gain + 1, :] + vectors[l, shift : shift + 1, :]
            h[t, :] = y
            a[t, :] = y.astype(jnp.bfloat16)

        loop(count // ROW_TILE, body)
        store_x.start()
        store_s.start()

    def layer(l):
        base = l * GROUPS

        @pl.when(l > 0)
        def _():
            for m in range(3):
                pltpu.make_async_copy(qkv.at[m], saved_qkv.at[l, m], qsem.at[m]).wait()

        def project(i):
            m = i // 2
            y = matmul(a[...], weights(base + i)) + vectors[l, pl.ds(m, 1), tile(i % 2, WIDTH)]
            y = y * jnp.where(m == 0, jnp.float32((h.shape[1] // HEADS) ** -0.5), jnp.float32(1))
            qkv[m, :, tile(i % 2, WIDTH)] = y.astype(jnp.bfloat16)

        loop(6, project)
        for m in range(3):
            pltpu.make_async_copy(qkv.at[m], saved_qkv.at[l, m], qsem.at[m]).start()

        def attend(i):
            r = i // pairs
            lanes = tile(lax.rem(i, pairs), 128)
            slot = lax.rem(i, 2)
            store_p = pltpu.make_async_copy(p_stage.at[slot], saved_p.at[l, i], psem.at[slot])

            @pl.when((i >= 2) | (l > 0))
            def _():
                store_p.wait()

            top = pl.multiple_of(r * slots, slots)
            for b, start in enumerate(window_starts(slots)):
                qm = pair_stack(qkv[0, pl.ds(top + b * BLOCK, BLOCK), lanes])
                km = qkv[1, pl.ds(top + start, WINDOW), lanes]
                vm = qkv[2, pl.ds(top + start, WINDOW), lanes]
                same = id_col[r, start : start + WINDOW, :] == id_row[r, :, b * BLOCK : (b + 1) * BLOCK]
                s = matmul_nt(km, qm)
                s = jnp.where(jnp.concatenate([same, same], axis=1), s, NEGATIVE)
                e = jnp.exp(s - jnp.max(s, axis=0, keepdims=True))
                p = e * (1.0 / jnp.sum(e, axis=0, keepdims=True))
                p = p.astype(jnp.bfloat16)
                p_stage[slot, b] = p
                o[pl.ds(top + b * BLOCK, BLOCK), lanes] = pair_join(matmul_tn(p, vm)).astype(jnp.bfloat16)
            store_p.start()

        loop(rows * pairs, attend)

        def attn_out(i):
            cols = tile(i, WIDTH)
            h[:, cols] += matmul(o[...], weights(base + AT_OUT + i))

        loop(2, attn_out)
        normalize(l, 0)

        def inner(i):
            cols = tile(i, WIDTH)
            u[...] = matmul(a[...], weights(base + AT_INNER + i)) + inner_bias[l, :, cols]
            slot = lax.rem(i, 2)
            store_d = pltpu.make_async_copy(d_stage.at[slot], saved_d.at[l, i], dsem.at[slot])

            @pl.when((i >= 2) | (l > 0))
            def _():
                store_d.wait()

            def activate(t):
                part = tile(t, ROW_TILE)
                x = u[part, :]
                cdf = 0.5 + 0.5 * lax.erf(x * ROOT_HALF)
                z[i // 2, part, tile(i % 2, WIDTH)] = (x * cdf).astype(jnp.bfloat16)
                slope = cdf + x * (DENSITY * jnp.exp(-0.5 * x * x))
                d_stage[slot, part, :] = slope.astype(jnp.bfloat16)

            loop(count // ROW_TILE, activate)
            store_d.start()

        loop(8, inner)

        def outer(i):
            cols = tile(i // 4, WIDTH)
            h[:, cols] += matmul(z[lax.rem(i, 4)], weights(base + AT_OUTER + i))

        loop(8, outer)
        normalize(l, 1)

    loop(LAYERS, layer)
    store = pltpu.make_async_copy(a, out, tsem)
    store.start()
    last = LAYERS - 1
    for m in range(3):
        pltpu.make_async_copy(qkv.at[m], saved_qkv.at[last, m], qsem.at[m]).wait()
    for i in range(2):
        pltpu.make_async_copy(p_stage.at[i], saved_p.at[last, i], psem.at[i]).wait()
        pltpu.make_async_copy(d_stage.at[i], saved_d.at[last, i], dsem.at[i]).wait()
    pltpu.make_async_copy(x_stage, saved_x.at[last, 1], xsem).wait()
    pltpu.make_async_copy(s_stage, saved_s.at[last, 1], ssem).wait()
    store.wait()


def forward(wbuf, tokens, id_row, id_col, vectors, inner_bias, rows, slots):
    count, width = tokens.shape
    hidden = inner_bias.shape[-1]
    bf, f32 = jnp.bfloat16, jnp.float32
    blocks = slots // BLOCK
    any_ = pl.BlockSpec(memory_space=HBM)
    vm = pl.BlockSpec(memory_space=VMEM)
    return pl.pallas_call(
        functools.partial(forward_kernel, (rows, slots)),
        out_shape=(
            jax.ShapeDtypeStruct((count, width), bf),
            jax.ShapeDtypeStruct((LAYERS, 3, count, width), bf),
            jax.ShapeDtypeStruct((LAYERS, rows * HEADS // 2, blocks, WINDOW, 2 * BLOCK), bf),
            jax.ShapeDtypeStruct((LAYERS, 2, count, width), f32),
            jax.ShapeDtypeStruct((LAYERS, 2, count, 128), f32),
            jax.ShapeDtypeStruct((LAYERS, hidden // WIDTH, count, WIDTH), bf),
        ),
        in_specs=[any_, any_, vm, vm, vm, vm],
        out_specs=(any_,) * 6,
        scratch_shapes=[
            VMEM((count, width), f32),
            VMEM((count, width), bf),
            VMEM((3, count, width), bf),
            VMEM((count, width), bf),
            VMEM((hidden // width, count, width), bf),
            VMEM((count, WIDTH), f32),
            VMEM((3, width, WIDTH), bf),
            VMEM((2, blocks, WINDOW, 2 * BLOCK), bf),
            VMEM((2, count, WIDTH), bf),
            VMEM((count, width), f32),
            VMEM((count, 128), f32),
            DMA((3,)), DMA((2,)), DMA((2,)), DMA, DMA, DMA((3,)), DMA,
        ],
        compiler_params=pltpu.CompilerParams(vmem_limit_bytes=56 << 20),
    )(wbuf, tokens, id_row, id_col, vectors, inner_bias)


def fold(x):
    rows, width = x.shape
    return jnp.sum(x.reshape(rows // 8, 8, width), axis=0)


def backward_kernel(
    dims,
    wbuf, cotangent, real, vectors, saved_qkv, saved_p, saved_x, saved_s, saved_d,
    grad, sums,
    g, db, du, dh, qkv, dqkv, x, sc, d, w, p, dk, dv, part,
    wsem, psem, dsem, xsem, ssem, qsem, gsem,
):
    rows, slots = dims
    count, width = g.shape
    pairs = HEADS // 2
    total = LAYERS * GROUPS
    items = rows * pairs

    def block_of(i):
        l = LAYERS - 1 - i // GROUPS
        j = lax.rem(i, GROUPS)
        quarter, within = j // 4, lax.rem(j, 4)
        ffn = jnp.where(within < 2, AT_OUTER + 4 * within + quarter, AT_INNER + 2 * quarter + within - 2)
        late = jnp.where(j < 18, AT_OUT + j - 16, j - 18)
        return l * GROUPS + jnp.where(j < 16, ffn, late)

    def wload(i):
        slot = lax.rem(i, 3)
        return pltpu.make_async_copy(wbuf.at[block_of(i)], w.at[slot], wsem.at[slot])

    def weights(i):
        @pl.when(i + 2 < total)
        def _():
            wload(i + 2).start()

        wload(i).wait()
        return lax.rem(i, 3)

    def xload(l, which):
        return (
            pltpu.make_async_copy(saved_x.at[l, which], x.at[which], xsem.at[which]),
            pltpu.make_async_copy(saved_s.at[l, which], sc.at[which], ssem.at[which]),
        )

    def dload(l, i):
        slot = lax.rem(i, 2)
        return pltpu.make_async_copy(saved_d.at[l, i], d.at[slot], dsem.at[slot])

    def pload(l, i):
        slot = lax.rem(i, 2)
        return pltpu.make_async_copy(saved_p.at[l, i], p.at[slot], psem.at[slot])

    def qload(l):
        return [pltpu.make_async_copy(saved_qkv.at[l, m], qkv.at[m], qsem.at[m]) for m in range(3)]

    top_layer = LAYERS - 1
    first = pltpu.make_async_copy(cotangent, db, gsem)
    first.start()
    for which in (1, 0):
        for c in xload(top_layer, which):
            c.start()
    wload(0).start()
    wload(1).start()
    dload(top_layer, 0).start()
    first.wait()

    def widen(i):
        t = tile(i, ROW_TILE)
        g[t, :] = db[t, :].astype(jnp.float32) * real[t, :]

    loop(count // ROW_TILE, widen)

    def normalize_back(l, which):
        gain = (G_ATTN, G_FFN)[which]
        row_shift = (D_ATTN, D_FFN)[which]
        row_bias = (D_OUT, D_OUTER)[which]
        for c in xload(l, which):
            c.wait()

        def body(i, carry):
            t = tile(i, ROW_TILE)
            up = g[t, :]
            xh = x[which, t, :]
            scaled = up * vectors[l, gain : gain + 1, :]
            m1 = jnp.mean(scaled, axis=1, keepdims=True)
            m2 = jnp.mean(scaled * xh, axis=1, keepdims=True)
            down = sc[which, t, :1] * (scaled - m1 - xh * m2)
            g[t, :] = down
            low = down.astype(jnp.bfloat16)
            db[t, :] = low
            return carry[0] + fold(up), carry[1] + fold(low.astype(jnp.float32))

        zero = jnp.zeros((8, width), jnp.float32)
        shift_sum, bias_sum = lax.fori_loop(0, count // ROW_TILE, body, (zero, zero))
        part[row_shift] = shift_sum
        part[row_bias] = bias_sum

        @pl.when(l > 0)
        def _():
            for c in xload(l - 1, which):
                c.start()

    def layer(step):
        l = top_layer - step
        base = step * GROUPS
        for c in qload(l):
            c.start()
        normalize_back(l, 1)

        def quarter(kc):
            at = base + 4 * kc
            slot = weights(at)
            for c in range(width // 256):
                n = slice(c * 256, (c + 1) * 256)
                dh[:, n] = matmul_nt(db[:, :WIDTH], w[slot, n, :])
            slot = weights(at + 1)
            for c in range(width // 256):
                n = slice(c * 256, (c + 1) * 256)
                dh[:, n] += matmul_nt(db[:, WIDTH:], w[slot, n, :])

            total_ = []
            for half in range(2):
                i = 2 * kc + half

                @pl.when(i + 1 < 8)
                def _():
                    dload(l, i + 1).start()

                dload(l, i).wait()

                def slope(t, carry):
                    tl = tile(t, ROW_TILE)
                    cols = pl.ds(half * WIDTH, WIDTH)
                    low = (dh[tl, cols] * d[half, tl, :].astype(jnp.float32)).astype(jnp.bfloat16)
                    du[tl, cols] = low
                    return carry + fold(low.astype(jnp.float32))

                total_.append(
                    lax.fori_loop(0, count // ROW_TILE, slope, jnp.zeros((8, WIDTH), jnp.float32))
                )
            part[D_INNER + kc] = jnp.concatenate(total_, axis=1)

            def into(half):
                slot = weights(at + 2 + half)
                for c in range(width // 256):
                    n = slice(c * 256, (c + 1) * 256)
                    g[:, n] += matmul_nt(du[:, tile(half, WIDTH)], w[slot, n, :])

            loop(2, into)

        loop(4, quarter)

        @pl.when(l > 0)
        def _():
            dload(l - 1, 0).start()

        pload(l, 0).start()
        normalize_back(l, 0)

        slot = weights(base + 16)
        for c in range(width // 256):
            n = slice(c * 256, (c + 1) * 256)
            dh[:, n] = matmul_nt(db[:, :WIDTH], w[slot, n, :])
        slot = weights(base + 17)
        for c in range(width // 256):
            n = slice(c * 256, (c + 1) * 256)
            du[:, n] = (dh[:, n] + matmul_nt(db[:, WIDTH:], w[slot, n, :])).astype(jnp.bfloat16)
        for c in qload(l):
            c.wait()

        def attend(i):
            r = i // pairs
            lanes = tile(lax.rem(i, pairs), 128)
            slot = lax.rem(i, 2)

            @pl.when(i + 1 < items)
            def _():
                pload(l, i + 1).start()

            pload(l, i).wait()
            dk[...] = jnp.zeros_like(dk)
            dv[...] = jnp.zeros_like(dv)
            top = pl.multiple_of(r * slots, slots)
            for b, start in enumerate(window_starts(slots)):
                mine = pl.ds(top + b * BLOCK, BLOCK)
                reach = pl.ds(top + start, WINDOW)
                qm = pair_stack(qkv[0, mine, lanes])
                om = pair_stack(du[mine, lanes])
                pb = p[slot, b]
                pf = pb.astype(jnp.float32)
                dp = matmul_nt(qkv[2, reach, lanes], om)
                weighted = pf * dp
                ds = weighted - pf * jnp.sum(weighted, axis=0, keepdims=True)
                ds = ds.astype(jnp.bfloat16)
                dk[start : start + WINDOW, :] += matmul(ds, qm)
                dv[start : start + WINDOW, :] += matmul(pb, om)
                dq = pair_join(matmul_tn(ds, qkv[1, reach, lanes]))
                dqkv[0, mine, lanes] = (dq * (width // HEADS) ** -0.5).astype(jnp.bfloat16)
            every = pl.ds(top, slots)
            dqkv[1, every, lanes] = dk[...].astype(jnp.bfloat16)
            dqkv[2, every, lanes] = dv[...].astype(jnp.bfloat16)

        loop(items, attend)

        for m, row in ((0, D_Q), (2, D_V)):

            def add(t, carry):
                return carry + fold(dqkv[m, tile(t, ROW_TILE), :].astype(jnp.float32))

            part[row] = lax.fori_loop(
                0, count // ROW_TILE, add, jnp.zeros((8, width), jnp.float32)
            )

        def project(i):
            slot = weights(base + 18 + i)
            for c in range(width // 256):
                n = slice(c * 256, (c + 1) * 256)
                g[:, n] += matmul_nt(dqkv[i // 2, :, tile(lax.rem(i, 2), WIDTH)], w[slot, n, :])

        loop(6, project)
        sums[l] = jnp.sum(part[...], axis=1)

    part[...] = jnp.zeros_like(part)
    loop(LAYERS, layer)
    last = pltpu.make_async_copy(g, grad, gsem)
    last.start()
    last.wait()


def backward(wbuf, cotangent, real, vectors, saved, rows, slots):
    count, width = cotangent.shape
    bf, f32 = jnp.bfloat16, jnp.float32
    blocks = slots // BLOCK
    any_ = pl.BlockSpec(memory_space=HBM)
    vm = pl.BlockSpec(memory_space=VMEM)
    return pl.pallas_call(
        functools.partial(backward_kernel, (rows, slots)),
        out_shape=(
            jax.ShapeDtypeStruct((count, width), f32),
            jax.ShapeDtypeStruct((LAYERS, SUM_ROWS, width), f32),
        ),
        in_specs=[any_, any_, vm, vm] + [any_] * 5,
        out_specs=(any_, vm),
        scratch_shapes=[
            VMEM((count, width), f32),
            VMEM((count, width), bf),
            VMEM((count, width), bf),
            VMEM((count, width), f32),
            VMEM((3, count, width), bf),
            VMEM((3, count, width), bf),
            VMEM((2, count, width), f32),
            VMEM((2, count, 128), f32),
            VMEM((2, count, WIDTH), bf),
            VMEM((3, width, WIDTH), bf),
            VMEM((2, blocks, WINDOW, 2 * BLOCK), bf),
            VMEM((slots, 128), f32),
            VMEM((slots, 128), f32),
            VMEM((SUM_ROWS, 8, width), f32),
            DMA((3,)), DMA((2,)), DMA((2,)), DMA((2,)), DMA((2,)), DMA((3,)), DMA,
        ],
        compiler_params=pltpu.CompilerParams(vmem_limit_bytes=58 << 20),
    )(wbuf, cotangent, real, vectors, *saved)


def reduce_kernel(devices, x, out, got, ssem, rsem):
    me = lax.axis_index("dp")
    steps = devices.bit_length() - 1
    mates = [me + (1 << i) - 2 * (1 << i) * lax.rem(me >> i, 2) for i in range(steps)]
    bar = pltpu.get_barrier_semaphore()
    for to in mates:
        pl.semaphore_signal(bar, inc=1, device_id=(to,), device_id_type=MESH)
    pl.semaphore_wait(bar, steps)
    out[0] = x[...]
    for i, to in enumerate(mates):
        copy = pltpu.make_async_remote_copy(
            src_ref=out.at[i],
            dst_ref=got.at[i],
            send_sem=ssem.at[i],
            recv_sem=rsem.at[i],
            device_id=(to,),
            device_id_type=MESH,
        )
        copy.start()
        copy.wait()
        out[i + 1] = out[i] + got[i]


def all_sum(x, devices):
    steps = devices.bit_length() - 1
    out = pl.pallas_call(
        functools.partial(reduce_kernel, devices),
        out_shape=jax.ShapeDtypeStruct((steps + 1,) + x.shape, x.dtype),
        in_specs=[pl.BlockSpec(memory_space=VMEM)],
        out_specs=pl.BlockSpec(memory_space=VMEM),
        scratch_shapes=[VMEM((steps,) + x.shape, x.dtype), DMA((steps,)), DMA((steps,))],
        compiler_params=pltpu.CompilerParams(collective_id=1, has_side_effects=True),
    )(x)
    return out[steps]


def pack(devices, w_query, w_key, w_value, w_out, w_inner, w_outer):
    layers, rows, width = w_query.shape
    hidden = w_inner.shape[2]

    def halves(m):
        return m.astype(jnp.bfloat16).reshape(layers, rows, -1, WIDTH).transpose(0, 2, 1, 3)

    inner = w_inner.astype(jnp.bfloat16).reshape(layers, rows, devices, hidden // width, rows)
    inner = inner.transpose(0, 3, 2, 1, 4)
    inner = inner.reshape(layers, hidden // WIDTH, WIDTH // rows, rows, rows)
    inner = inner.transpose(0, 1, 3, 2, 4).reshape(layers, hidden // WIDTH, rows, WIDTH)
    outer = w_outer.astype(jnp.bfloat16).reshape(layers, hidden // width, rows, width // WIDTH, WIDTH)
    outer = outer.transpose(0, 3, 1, 2, 4).reshape(layers, -1, rows, WIDTH)
    parts = [halves(m) for m in (w_query, w_key, w_value, w_out)] + [inner, outer]
    return jnp.concatenate(parts, axis=1).reshape(layers * GROUPS, rows, WIDTH)


def per_device(
    devices,
    tokens,
    lengths,
    w_query,
    w_key,
    w_value,
    w_out,
    w_inner,
    w_outer,
    bias_query,
    bias_value,
    bias_out,
    bias_inner,
    bias_outer,
    shift_attn,
    shift_ffn,
    gain_attn,
    gain_ffn,
    cotangent,
):
    rows, slots, width = tokens.shape
    hidden = bias_inner.shape[1]
    unit = w_query.shape[1]
    count = rows * slots
    segments = lengths.shape[1]
    ends = jnp.cumsum(lengths, axis=-1)
    position = jnp.arange(slots, dtype=jnp.int32)
    numbers = jnp.sum((position[None, :, None] >= ends[:, None, :]).astype(jnp.int32), axis=-1)
    is_real = numbers < segments - 1
    ids = jnp.where(is_real, numbers, PADDING_ID + position[None, :])
    id_row = ids[:, None, :]
    id_col = jnp.broadcast_to(ids[:, :, None], (rows, slots, 128))
    real = is_real.astype(jnp.float32).reshape(count, 1)
    vectors = jnp.stack(
        [bias_query, jnp.zeros_like(bias_query), bias_value, bias_out, bias_outer,
         shift_attn, shift_ffn, gain_attn, gain_ffn],
        axis=1,
    )
    inner_bias = (
        bias_inner.reshape(LAYERS, devices, hidden // width, unit)
        .transpose(0, 2, 1, 3)
        .reshape(LAYERS, 1, hidden)
    )
    own = pack(devices, w_query, w_key, w_value, w_out, w_inner, w_outer)
    wbuf = gather_weights(own, devices).reshape(LAYERS * GROUPS, width, WIDTH)
    out, *saved = forward(
        wbuf, tokens.reshape(count, width), id_row, id_col, vectors, inner_bias, rows, slots
    )
    grad, sums = backward(
        wbuf, cotangent.reshape(count, width), real, vectors, saved, rows, slots
    )
    sums = all_sum(sums, devices)
    grad_inner = sums[:, D_INNER : D_INNER + hidden // width].reshape(
        LAYERS, hidden // width, devices, unit
    )
    grad_inner = grad_inner.transpose(0, 2, 1, 3).reshape(LAYERS, hidden)
    return (
        out.reshape(rows, slots, width),
        grad.reshape(rows, slots, width),
        sums[:, D_Q],
        sums[:, D_V],
        sums[:, D_OUT],
        grad_inner,
        sums[:, D_OUTER],
        sums[:, D_ATTN],
        sums[:, D_FFN],
    )


def solution(mesh):
    rows, whole = P("dp", None, None), P()
    weight = P(None, "dp", None)
    placed = (rows, P("dp", None)) + (weight,) * 6 + (whole,) * 9 + (rows,)
    return jax.shard_map(
        functools.partial(per_device, mesh.shape["dp"]),
        mesh=mesh,
        in_specs=placed,
        out_specs=(rows, rows) + (whole,) * 7,
        check_vma=False,
    )
```

time: 1460 us -> 569 us (0.39)
  matrix products: 676 us -> 0 us
  Pallas kernels: 0 us -> 545 us
  waiting for transfers between devices: 504 us -> 0 us
  local copies, waits for them, and re-layouts: 181 us -> 19.8 us
  other arithmetic: 73.8 us -> 3.03 us
    dot_general x52 -> x0, matrix products: 676 us -> none  [the longest x12 190 us: product(): return jnp.dot(left, right, preferred_element_type=jnp.float32)]
    pallas_call x0 -> x4, Pallas kernels: none -> 545 us  [the longest x1 254 us: gather_weights(): pl.pallas_call(functools.partial(gather_kernel, dims, total), out_shape=j...]
    all_gather x12 -> x0, waiting for transfers between devices: 390 us -> none  [the longest x2 92.8 us: fetch_forward(): lax.all_gather(rounded[4], 'dp', axis=0, tiled=True)]
    psum x1 -> x0, waiting for transfers between devices: 110 us -> none  [per_device(): lax.psum((stacked[0], stacked[1], stacked[2], stacked[3], stacked[4], sta...]
    while x52 -> x0, local copies, waits for them, and re-layouts: 68 us -> none  [the longest x6 32.9 us: layer_forward(): lax.map(lambda row_item: attend_forward(*row_item), (query_rows.reshape(s...]
    reduce_sum x20 -> x1, other arithmetic: 62.9 us -> 0.09 us  [per_device(): jnp.sum((position[None, :, None] >= ends[:, None, :]).astype(jnp.int32),...]
    reshape x8 -> x13, local copies, waits for them, and re-layouts: 39.4 us -> 6.16 us  [the longest x1 2.05 us: pack(): inner.transpose(0, 1, 3, 2, 4).reshape(layers, hidden // WIDTH, rows, WIDTH)]
    unnamed x190 -> x38, local copies, waits for them, and re-layouts: 26.6 us -> 7.04 us
  transfers between devices with their start and end apart: 13 -> 0, of which waited for: 11 -> 0; matrix products, arithmetic and copies ran while one was open for 27% -> 0% of each run, Pallas kernels for 0% -> 0%
where the time goes in v1:
time: 569 us
  Pallas kernels  545 us (96%)
  local copies, waits for them, and re-layouts  19.8 us (3%)
    pallas_call x1, Pallas kernels, gather_weights(): pl.pallas_call(functools.partial(gather_kernel, dims, total), out_shape=j...  254 us
    pallas_call x1, Pallas kernels, forward(): pl.pallas_call(functools.partial(forward_kernel, (rows, slots)), out_shap...  135 us
    pallas_call x1, Pallas kernels, backward(): pl.pallas_call(functools.partial(backward_kernel, (rows, slots)), out_sha...  129 us
    pallas_call x1, Pallas kernels, all_sum(): pl.pallas_call(functools.partial(reduce_kernel, devices), out_shape=jax.S...  26.5 us

profile of v1, /device:TPU:0, one launch (start us, length us, event | category | flops | bytes accessed | tf_op | source)
XLA Modules:
  0.0 568.9 jit_solution(9895470517810674037)
XLA Ops:
  0.6 0.0 copy-start.2
  0.7 0.0 copy-start.3
  0.7 1.0 convert_element_type.34
  1.7 0.1 reshape.145
  1.8 0.0 copy-start
  1.8 0.7 copy_dynamic-update-slice_fusion.3
  2.5 1.0 convert_element_type.35
  3.4 0.1 reshape.146
  3.5 0.7 copy_dynamic-update-slice_fusion.2
  4.2 0.0 copy-done.2
  4.2 0.1 reshape.147
  4.3 0.7 copy_dynamic-update-slice_fusion.1
  5.0 0.0 copy-done.3
  5.0 0.1 reshape.148
  5.1 0.7 copy_dynamic-update-slice_fusion
  5.7 0.0 copy-done
  5.7 0.1 convert_element_type.38
  5.8 1.6 reshape.149
  7.4 1.4 copy.58
  8.8 0.9 copy.59
  9.7 2.1 reshape.151
  11.8 0.0 copy-start.1
  11.8 0.8 constant_dynamic-update-slice_fusion.1
  12.6 0.6 copy-done.1
  13.2 0.1 convert_element_type.39
  13.2 0.4 reshape.152
  13.6 0.1 copy.60
  13.7 0.8 constant_dynamic-update-slice_fusion
  14.5 0.0 copy-start.13
  14.5 0.0 copy-start.8
  14.6 0.0 copy-start.9
  14.6 0.0 copy-start.10
  14.6 0.0 copy-start.11
  14.6 0.0 copy-start.12
  14.6 0.0 copy-start.4
  14.6 254.2 %shard_map.241 = bf16[48,4,2,2,2,32,512]{6,5,4,3,2,1,0:T(8,128)(2,1)} custom-call(bf16[48,32,512]{2,1,0:T(8,128)(2,1)} %bitcast.52), custom_call_target="tpu_custom_call" | custom-call | tf_op jit(solution)/shard_map/pallas_call | solution.py:153
  268.9 0.0 copy-done.13
  268.9 0.2 reduce_window_sum.11
  269.1 0.1 convert_reduce_fusion
  269.2 0.6 compare_select_fusion.id_row
  269.8 1.0 broadcast_in_dim.22.id_col
  270.8 0.0 copy-done.5
  270.8 0.0 copy-done.6
  270.8 0.0 copy-done.7
  270.8 0.0 copy-done.8
  270.8 0.0 copy-done.9
  270.9 0.0 copy-done.10
  270.9 0.0 copy-done.11
  270.9 0.0 copy-done.12
  271.0 1.4 stack.35.vectors
  272.4 0.0 copy-done.4
  272.4 0.1 reshape.157
  272.5 0.7 reshape.158.inner_bias
  273.2 135.1 %shard_map.242 = (bf16[1024,1024]{1,0:T(8,128)(2,1)}, bf16[2,3,1024,1024]{3,2,1,0:T(8,128)(2,1)}, bf16[2,16,4,256,256]{4,3,2,1,0:T(8,128)(2,1)}, f32[2,2,1024,10...) custom-call(bf16[48,1024,512]{2,1,0:T(8,128)(2,1)} %bitcast.44, ...), custom_call_target="tpu_custom_call" | custom-call | tf_op jit(solution)/shard_map/pallas_call | solution.py:378
  408.4 1.0 copy.75
  409.4 129.2 %shard_map.243 = (f32[1024,1024]{1,0:T(8,128)}, f32[2,16,1024]{2,1,0:T(8,128)}) custom-call(bf16[48,1024,512]{2,1,0:T(8,128)(2,1)} %bitcast.45, bf16[1024,1024]{1,0:T(8,128)(2,1)} %bitcast.48, f32[1024,1]{1,0:T(8,128)} %bitcast.49, f32[2,9,1024]{2,1,0:T(8,128)} %stack.35.vectors, bf16[2,3,1024,1024]{3,2,1,0:T(8,128)(2,1)} %get-tuple-element.18.saved_qkv, ...), custom_call_target="tpu_custom_call" | custom-call | tf_op jit(solution)/shard_map/pallas_call | solution.py:643
  538.6 26.5 %shard_map.244 = f32[6,2,16,1024]{3,2,1,0:T(8,128)} custom-call(f32[2,16,1024]{2,1,0:T(8,128)} %get-tuple-element.24.x), custom_call_target="tpu_custom_call" | custom-call | tf_op jit(solution)/shard_map/pallas_call | solution.py:697
  565.1 0.9 slice_bitcast_fusion
  566.1 0.6 copy_bitcast_fusion.5
  566.7 0.6 copy_bitcast_fusion.3
  567.3 0.1 reshape.162
  567.4 0.1 copy.67
  567.5 0.8 reshape.163
  568.3 0.6 copy_bitcast_fusion.1
  (21 shorter events, 0.2 us)
Async XLA Ops:
  0.6 3.5 copy-start.2
  0.7 4.3 copy-start.3
  1.8 4.0 copy-start
  11.8 1.4 copy-start.1
  14.5 254.3 %copy-start.13 = (s32[2,16]{1,0:T(2,128)S(1)}, s32[2,16]{1,0:T(2,128)}, u32[]{:S(2)}) copy-start(s32[2,16]{1,0:T(2,128)} %param.19) | copy-start | bytes 388
  14.5 256.2 %copy-start.5 = (f32[2,1024]{1,0:T(2,128)S(1)}, f32[2,1024]{1,0:T(2,128)}, u32[]{:S(2)}) copy-start(f32[2,1024]{1,0:T(2,128)} %param.26) | copy-start | bytes 24580
  14.5 256.2 %copy-start.6 = (f32[2,1024]{1,0:T(2,128)S(1)}, f32[2,1024]{1,0:T(2,128)}, u32[]{:S(2)}) copy-start(f32[2,1024]{1,0:T(2,128)} %param.27) | copy-start | bytes 24580
  14.5 256.3 %copy-start.7 = (f32[2,1024]{1,0:T(2,128)S(1)}, f32[2,1024]{1,0:T(2,128)}, u32[]{:S(2)}) copy-start(f32[2,1024]{1,0:T(2,128)} %param.28) | copy-start | bytes 24580
  14.5 256.3 %copy-start.8 = (f32[2,1024]{1,0:T(2,128)S(1)}, f32[2,1024]{1,0:T(2,128)}, u32[]{:S(2)}) copy-start(f32[2,1024]{1,0:T(2,128)} %param.30) | copy-start | bytes 24580
  14.6 256.3 %copy-start.9 = (f32[2,1024]{1,0:T(2,128)S(1)}, f32[2,1024]{1,0:T(2,128)}, u32[]{:S(2)}) copy-start(f32[2,1024]{1,0:T(2,128)} %param.31) | copy-start | bytes 24580
  14.6 256.3 %copy-start.10 = (f32[2,1024]{1,0:T(2,128)S(1)}, f32[2,1024]{1,0:T(2,128)}, u32[]{:S(2)}) copy-start(f32[2,1024]{1,0:T(2,128)} %param.32) | copy-start | bytes 24580
  14.6 256.3 %copy-start.11 = (f32[2,1024]{1,0:T(2,128)S(1)}, f32[2,1024]{1,0:T(2,128)}, u32[]{:S(2)}) copy-start(f32[2,1024]{1,0:T(2,128)} %param.33) | copy-start | bytes 24580
  14.6 256.3 %copy-start.12 = (f32[2,1024]{1,0:T(2,128)S(1)}, f32[2,1024]{1,0:T(2,128)}, u32[]{:S(2)}) copy-start(f32[2,1024]{1,0:T(2,128)} %param.34) | copy-start | bytes 24580
  14.6 257.8 %copy-start.4 = (f32[2,4096]{1,0:T(2,128)S(1)}, f32[2,4096]{1,0:T(2,128)}, u32[]{:S(2)}) copy-start(f32[2,4096]{1,0:T(2,128)} %param.29) | copy-start | bytes 98308

commit v2 on v1

--- a/solution.py
+++ b/solution.py
@@ -118,46 +118,13 @@
                     for c in self.copies(g, par, s, p):
                         c.start()
 
-    def arrive(self, pair, par):
-        for s in range(2):
-            for c in self.copies(2 * pair + par, par, s, 3):
-                c.wait()
-
-
-def gather_kernel(dims, total, own, buf, ssem, rsem, lsem):
-    gather = Gather(dims, own, buf, ssem, rsem, total)
-    here = pltpu.make_async_copy(
-        own, buf.at[(pl.ds(0, total),) + gather.at + (gather.core,)], lsem
-    )
-    here.start()
-    gather.barrier()
-    here.wait()
-
-    def body(step, _):
-        for par in range(2):
-            gather.pump(step, par)
-
-            @pl.when(step >= 4)
-            def _():
-                gather.arrive(step - 4, par)
-
-        return 0
-
-    lax.fori_loop(0, total // 2 + 4, body, 0)
-
-
-def gather_weights(own, devices):
-    total, rows, cols = own.shape
-    dims = chip_dims(devices)
-    sems = sum(d - 1 for d in dims) + 1
-    return pl.pallas_call(
-        functools.partial(gather_kernel, dims, total),
-        out_shape=jax.ShapeDtypeStruct((total,) + dims + (2, rows, cols), own.dtype),
-        in_specs=[pl.BlockSpec(memory_space=HBM)],
-        out_specs=pl.BlockSpec(memory_space=HBM),
-        scratch_shapes=[DMA((SLOTS, 2, sems)), DMA((SLOTS, 2, sems)), DMA],
-        compiler_params=pltpu.CompilerParams(collective_id=0, has_side_effects=True),
-    )(own)
+        pair = pair_step - 4
+
+        @pl.when((pair >= 0) & (pair < self.total // 2))
+        def _():
+            for s in range(2):
+                for c in self.copies(2 * pair + par, par, s, 3):
+                    c.wait()
 
 
 def matmul(left, right):
@@ -207,39 +174,59 @@
 
 
 def forward_kernel(
-    dims,
-    wbuf, tokens, id_row, id_col, vectors, inner_bias,
-    out, saved_qkv, saved_p, saved_x, saved_s, saved_d,
+    dims, devices_dims,
+    own, tokens, id_row, id_col, vectors, inner_bias,
+    wbuf, out, saved_qkv, saved_p, saved_x, saved_s, saved_d,
     h, a, qkv, o, z, u, w, p_stage, d_stage, x_stage, s_stage,
-    wsem, psem, dsem, xsem, ssem, qsem, tsem,
+    wsem, psem, dsem, xsem, ssem, qsem, tsem, hsem, send_sem, recv_sem,
 ):
     rows, slots = dims
     count = h.shape[0]
     pairs = HEADS // 2
     total = LAYERS * GROUPS
+    gather = Gather(devices_dims, own, wbuf, send_sem, recv_sem, total)
 
     def wload(g):
-        slot = lax.rem(g, 3)
+        slot = lax.rem(g, 2)
         return pltpu.make_async_copy(wbuf.at[g], w.at[slot], wsem.at[slot])
 
     def weights(g):
-        @pl.when(g + 2 < total)
+        @pl.when(g + 1 < total)
         def _():
-            wload(g + 2).start()
+            wload(g + 1).start()
 
         wload(g).wait()
-        return w[lax.rem(g, 3)]
+        return w[lax.rem(g, 2)].reshape(h.shape[1], WIDTH)
+
+    def pump(half):
+        for par in range(2):
+
+            @pl.when(lax.rem(half, 2) == par)
+            def _():
+                gather.pump(half // 2 + 4, par)
 
     load = pltpu.make_async_copy(tokens, a, tsem)
     load.start()
-    wload(0).start()
-    wload(1).start()
+    here = pltpu.make_async_copy(
+        own, wbuf.at[(pl.ds(0, total),) + gather.at + (gather.core,)], hsem
+    )
+    here.start()
+    gather.barrier()
+    here.wait()
     load.wait()
 
     def widen(i):
         h[tile(i, ROW_TILE), :] = a[tile(i, ROW_TILE), :].astype(jnp.float32)
 
     loop(count // ROW_TILE, widen)
+
+    def start(i):
+        for par in range(2):
+            gather.pump(i, par)
+
+    loop(4, start)
+    pump(0)
+    wload(0).start()
 
     def normalize(l, which):
         bias, gain, shift = ((B_OUT, G_ATTN, S_ATTN), (B_OUTER, G_FFN, S_FFN))[which]
@@ -281,6 +268,7 @@
                 pltpu.make_async_copy(qkv.at[m], saved_qkv.at[l, m], qsem.at[m]).wait()
 
         def project(i):
+            pump(base + i + 1)
             m = i // 2
             y = matmul(a[...], weights(base + i)) + vectors[l, pl.ds(m, 1), tile(i % 2, WIDTH)]
             y = y * jnp.where(m == 0, jnp.float32((h.shape[1] // HEADS) ** -0.5), jnp.float32(1))
@@ -291,6 +279,10 @@
             pltpu.make_async_copy(qkv.at[m], saved_qkv.at[l, m], qsem.at[m]).start()
 
         def attend(i):
+            @pl.when(lax.rem(i, 2) == 0)
+            def _():
+                pump(base + 7 + i // 2)
+
             r = i // pairs
             lanes = tile(lax.rem(i, pairs), 128)
             slot = lax.rem(i, 2)
@@ -318,6 +310,7 @@
         loop(rows * pairs, attend)
 
         def attn_out(i):
+            pump(base + 15 + i)
             cols = tile(i, WIDTH)
             h[:, cols] += matmul(o[...], weights(base + AT_OUT + i))
 
@@ -325,6 +318,10 @@
         normalize(l, 0)
 
         def inner(i):
+            @pl.when(i < 6)
+            def _():
+                pump(base + 17 + i)
+
             cols = tile(i, WIDTH)
             u[...] = matmul(a[...], weights(base + AT_INNER + i)) + inner_bias[l, :, cols]
             slot = lax.rem(i, 2)
@@ -348,6 +345,10 @@
         loop(8, inner)
 
         def outer(i):
+            @pl.when(i < 2)
+            def _():
+                pump(base + 23 + i)
+
             cols = tile(i // 4, WIDTH)
             h[:, cols] += matmul(z[lax.rem(i, 4)], weights(base + AT_OUTER + i))
 
@@ -368,16 +369,20 @@
     store.wait()
 
 
-def forward(wbuf, tokens, id_row, id_col, vectors, inner_bias, rows, slots):
+def forward(devices, own, tokens, id_row, id_col, vectors, inner_bias, rows, slots):
     count, width = tokens.shape
     hidden = inner_bias.shape[-1]
     bf, f32 = jnp.bfloat16, jnp.float32
     blocks = slots // BLOCK
+    devices_dims = chip_dims(devices)
+    held = devices_dims + (2,) + own.shape[1:]
+    sems = sum(d - 1 for d in devices_dims) + 1
     any_ = pl.BlockSpec(memory_space=HBM)
     vm = pl.BlockSpec(memory_space=VMEM)
     return pl.pallas_call(
-        functools.partial(forward_kernel, (rows, slots)),
+        functools.partial(forward_kernel, (rows, slots), devices_dims),
         out_shape=(
+            jax.ShapeDtypeStruct((LAYERS * GROUPS,) + held, bf),
             jax.ShapeDtypeStruct((count, width), bf),
             jax.ShapeDtypeStruct((LAYERS, 3, count, width), bf),
             jax.ShapeDtypeStruct((LAYERS, rows * HEADS // 2, blocks, WINDOW, 2 * BLOCK), bf),
@@ -386,7 +391,7 @@
             jax.ShapeDtypeStruct((LAYERS, hidden // WIDTH, count, WIDTH), bf),
         ),
         in_specs=[any_, any_, vm, vm, vm, vm],
-        out_specs=(any_,) * 6,
+        out_specs=(any_,) * 7,
         scratch_shapes=[
             VMEM((count, width), f32),
             VMEM((count, width), bf),
@@ -394,15 +399,18 @@
             VMEM((count, width), bf),
             VMEM((hidden // width, count, width), bf),
             VMEM((count, WIDTH), f32),
-            VMEM((3, width, WIDTH), bf),
+            VMEM((2,) + held, bf),
             VMEM((2, blocks, WINDOW, 2 * BLOCK), bf),
             VMEM((2, count, WIDTH), bf),
             VMEM((count, width), f32),
             VMEM((count, 128), f32),
-            DMA((3,)), DMA((2,)), DMA((2,)), DMA, DMA, DMA((3,)), DMA,
+            DMA((2,)), DMA((2,)), DMA((2,)), DMA, DMA, DMA((3,)), DMA, DMA,
+            DMA((SLOTS, 2, sems)), DMA((SLOTS, 2, sems)),
         ],
-        compiler_params=pltpu.CompilerParams(vmem_limit_bytes=56 << 20),
-    )(wbuf, tokens, id_row, id_col, vectors, inner_bias)
+        compiler_params=pltpu.CompilerParams(
+            vmem_limit_bytes=56 << 20, collective_id=0, has_side_effects=True
+        ),
+    )(own, tokens, id_row, id_col, vectors, inner_bias)
 
 
 def fold(x):
@@ -767,10 +775,10 @@
         .reshape(LAYERS, 1, hidden)
     )
     own = pack(devices, w_query, w_key, w_value, w_out, w_inner, w_outer)
-    wbuf = gather_weights(own, devices).reshape(LAYERS * GROUPS, width, WIDTH)
-    out, *saved = forward(
-        wbuf, tokens.reshape(count, width), id_row, id_col, vectors, inner_bias, rows, slots
-    )
+    wbuf, out, *saved = forward(
+        devices, own, tokens.reshape(count, width), id_row, id_col, vectors, inner_bias, rows, slots
+    )
+    wbuf = wbuf.reshape(LAYERS * GROUPS, width, WIDTH)
     grad, sums = backward(
         wbuf, cotangent.reshape(count, width), real, vectors, saved, rows, slots
     )

time: 569 us -> 475 us (0.83)
  Pallas kernels: 545 us -> 443 us
  local copies, waits for them, and re-layouts: 19.8 us -> 26.7 us
    pallas_call x2 -> x1, Pallas kernels: 389 us -> 289 us  [forward(): pl.pallas_call(functools.partial(forward_kernel, (rows, slots), devices_d...]
where the time goes in v2:
time: 475 us; the launch traced here: 474 us
  Pallas kernels  443 us (93%)
  local copies, waits for them, and re-layouts  26.7 us (6%)
    pallas_call x1, Pallas kernels, forward(): pl.pallas_call(functools.partial(forward_kernel, (rows, slots), devices_d...  289 us
    pallas_call x1, Pallas kernels, backward(): pl.pallas_call(functools.partial(backward_kernel, (rows, slots)), out_sha...  129 us
    pallas_call x1, Pallas kernels, all_sum(): pl.pallas_call(functools.partial(reduce_kernel, devices), out_shape=jax.S...  25 us

profile of v2, /device:TPU:0, one launch (start us, length us, event | category | flops | bytes accessed | tf_op | source)
XLA Modules:
  0.0 474.1 jit_solution(5607088089240814146)
XLA Ops:
  0.6 0.0 copy-start.6
  0.7 0.0 copy-start.5
  0.7 0.0 copy-start.4
  0.7 0.9 reduce_window_sum.11
  1.6 0.1 convert_reduce_fusion
  1.7 0.6 compare_select_fusion.id_row
  2.3 0.7 stack.27
  3.0 0.7 stack.28
  3.7 0.7 stack.29
  4.4 0.7 stack.30
  5.1 0.7 stack.31
  5.8 0.7 stack.32
  6.5 0.7 stack.33
  7.2 0.7 stack.34
  7.9 1.4 stack.35.vectors
  9.3 1.0 convert_element_type.34
  10.3 0.1 reshape.145
  10.3 1.0 convert_element_type.35
  11.3 0.0 copy-start.1
  11.3 0.1 reshape.146
  11.4 0.0 copy-done.4
  11.4 0.1 reshape.147
  11.5 0.0 copy-done.5
  11.6 0.7 reshape.148
  12.3 0.0 copy-done.6
  12.3 0.0 copy-start.2
  12.3 0.1 reshape.156
  12.4 0.7 reshape.157.inner_bias
  13.2 1.1 copy.75
  14.2 1.0 broadcast_in_dim.22.id_col
  15.2 0.0 copy-done.1
  15.2 0.1 convert_element_type.38
  15.3 0.0 copy-done.2
  15.3 0.1 convert_element_type.39
  15.4 0.0 copy-start.3
  15.4 0.4 reshape.152
  15.8 0.1 copy.60
  15.8 0.7 copy_dynamic-update-slice_fusion.3
  16.5 0.7 copy_dynamic-update-slice_fusion.2
  17.2 0.7 copy_dynamic-update-slice_fusion.1
  17.9 0.0 copy-done.3
  17.9 0.7 copy_dynamic-update-slice_fusion
  18.5 1.6 reshape.149
  20.2 1.4 copy.58
  21.5 0.9 copy.59
  22.4 2.1 reshape.151
  24.5 0.8 constant_dynamic-update-slice_fusion.1
  25.3 0.8 constant_dynamic-update-slice_fusion
  26.1 288.5 %shard_map.241 = (bf16[48,4,2,2,2,32,512]{6,5,4,3,2,1,0:T(8,128)(2,1)}, bf16[1024,1024]{1,0:T(8,128)(2,1)}, bf16[2,3,1024,1024]{3,2,1,0:T(8,128)(2,1)}, bf16[2,1...) custom-call(bf16[48,32,512]{2,1,0:T(8,128)(2,1)} %bitcast.9.own, ...), custom_call_target="tpu_custom_call" | custom-call | tf_op jit(solution)/shard_map/pallas_call | solution.py:382
  314.7 0.0 copy-start
  314.7 129.4 %shard_map.242 = (f32[1024,1024]{1,0:T(8,128)}, f32[2,16,1024]{2,1,0:T(8,128)}) custom-call(bf16[48,1024,512]{2,1,0:T(8,128)(2,1)} %bitcast.44, bf16[1024,1024]{1,0:T(8,128)(2,1)} %bitcast.47, f32[1024,1]{1,0:T(8,128)} %bitcast.48, f32[2,9,1024]{2,1,0:T(8,128)} %stack.35.vectors, bf16[2,3,1024,1024]{3,2,1,0:T(8,128)(2,1)} %get-tuple-element.20.saved_qkv, ...), custom_call_target="tpu_custom_call" | custom-call | tf_op jit(solution)/shard_map/pallas_call | solution.py:651
  444.0 25.0 %shard_map.243 = f32[6,2,16,1024]{3,2,1,0:T(8,128)} custom-call(f32[2,16,1024]{2,1,0:T(8,128)} %get-tuple-element.26.x), custom_call_target="tpu_custom_call" | custom-call | tf_op jit(solution)/shard_map/pallas_call | solution.py:705
  469.1 0.9 slice_bitcast_fusion
  470.0 0.6 copy_bitcast_fusion.1
  470.7 0.6 copy_bitcast_fusion.3
  471.3 0.6 copy_bitcast_fusion.5
  471.9 0.1 reshape.162
  472.0 0.1 copy.67
  472.1 0.8 reshape.163
  472.8 0.0 copy-done
  472.8 1.3 copy.94
  (10 shorter events, 0.1 us)
Async XLA Ops:
  0.6 11.6 %copy-start.6 = (f32[2,4096]{1,0:T(2,128)S(1)}, f32[2,4096]{1,0:T(2,128)}, u32[]{:S(2)}) copy-start(f32[2,4096]{1,0:T(2,128)} %param.29) | copy-start | bytes 98308
  0.7 10.9 %copy-start.5 = (f32[2,32,1024]{2,1,0:T(8,128)S(1)}, f32[2,32,1024]{2,1,0:T(8,128)}, u32[]{:S(2)}) copy-start(f32[2,32,1024]{2,1,0:T(8,128)} %param.23) | copy-start | bytes 786436
  0.7 10.8 %copy-start.4 = (f32[2,32,1024]{2,1,0:T(8,128)S(1)}, f32[2,32,1024]{2,1,0:T(8,128)}, u32[]{:S(2)}) copy-start(f32[2,32,1024]{2,1,0:T(8,128)} %param.22) | copy-start | bytes 786436
  11.3 3.9 copy-start.1
  12.3 3.0 copy-start.2
  15.4 2.5 copy-start.3
  314.7 158.2 %copy-start = (bf16[1024,1024]{1,0:T(8,128)(2,1)S(1)}, bf16[1024,1024]{1,0:T(8,128)(2,1)}, u32[]{:S(2)}) copy-start(bf16[1024,1024]{1,0:T(8,128)(2,1)} %get-tuple-element.18) | copy-start | bytes 6291460

commit v3 on v2

--- a/solution.py
+++ b/solution.py
@@ -25,9 +25,9 @@
 ROW_TILE = 128
 ROOT_HALF = 0.7071067811865476
 DENSITY = 0.3989422804014327
-B_Q, B_K, B_V, B_OUT, B_OUTER, S_ATTN, S_FFN, G_ATTN, G_FFN = range(9)
-D_Q, D_V, D_OUT, D_OUTER, D_ATTN, D_FFN, D_INNER = range(7)
-SUM_ROWS = 16
+B_Q, B_V, B_OUT, B_OUTER, S_ATTN, S_FFN, G_ATTN, G_FFN = range(8)
+D_OUT, D_OUTER, D_ATTN, D_FFN, D_INNER = range(5)
+EARLY = 8
 
 
 def chip_dims(devices):
@@ -173,13 +173,50 @@
     return jnp.where(lane < stacked.shape[1] // 2, stacked[:rows], stacked[rows:])
 
 
+def permute_hidden(load, store, unit, hidden):
+    devices = hidden // (4 * unit)
+    for b in range(hidden // 128):
+        block = None
+        for piece in range(128 // unit):
+            quarter, device = divmod(b * (128 // unit) + piece, devices)
+            source = (4 * device + quarter) * unit
+            x = load(source // 128)
+            shift = (piece * unit - source) % 128
+            if shift:
+                x = pltpu.roll(x, shift, axis=1)
+            if block is None:
+                block = x
+            else:
+                lane = lax.broadcasted_iota(jnp.int32, x.shape, 1)
+                block = jnp.where(lane >= piece * unit, x, block)
+        store(b, block)
+
+
+def store_block(own, first, b, x):
+    per = WIDTH // 128
+    own[first + b // per, :, b % per * 128 : (b % per + 1) * 128] = x.astype(own.dtype)
+
+
+def slot_ids(lengths, r, position):
+    segments = lengths.shape[1]
+    number = jnp.zeros_like(position)
+    end = jnp.int32(0)
+    for j in range(segments):
+        end = end + lengths[r, j]
+        number = number + (position >= end).astype(jnp.int32)
+    return jnp.where(number < segments - 1, number, PADDING_ID + position)
+
+
 def forward_kernel(
     dims, devices_dims,
-    own, tokens, id_row, id_col, vectors, inner_bias,
-    wbuf, out, saved_qkv, saved_p, saved_x, saved_s, saved_d,
-    h, a, qkv, o, z, u, w, p_stage, d_stage, x_stage, s_stage,
-    wsem, psem, dsem, xsem, ssem, qsem, tsem, hsem, send_sem, recv_sem,
+    lengths, w_query, w_key, w_value, w_out, w_inner, w_outer, tokens, *rest,
 ):
+    vectors, rest = rest[:8], rest[8:]
+    (
+        inner_raw, wbuf, out, saved_qkv, saved_p, saved_x, saved_s, saved_d,
+        h, a, qkv, o, z, u, w, p_stage, d_stage, x_stage, s_stage, own, id_row, id_col, inner_bias,
+        wsem, psem, dsem, xsem, ssem, qsem, tsem, hsem, send_sem, recv_sem,
+    ) = rest
     rows, slots = dims
     count = h.shape[0]
     pairs = HEADS // 2
@@ -207,24 +244,53 @@
 
     load = pltpu.make_async_copy(tokens, a, tsem)
     load.start()
+    unit = own.shape[1]
+    for l in range(LAYERS):
+        at = l * GROUPS
+        for m, matrix in enumerate((w_query, w_key, w_value, w_out)):
+            for c in range(2):
+                own[at + 2 * m + c] = matrix[l, :, c * WIDTH : (c + 1) * WIDTH].astype(jnp.bfloat16)
+        for c in range(2):
+            for kc in range(4):
+                piece = w_outer[l, kc * unit : (kc + 1) * unit, c * WIDTH : (c + 1) * WIDTH]
+                own[at + AT_OUTER + 4 * c + kc] = piece.astype(jnp.bfloat16)
+        permute_hidden(
+            lambda b: w_inner[l, :, b * 128 : (b + 1) * 128],
+            lambda b, x: store_block(own, at + AT_INNER, b, x),
+            unit,
+            w_inner.shape[2],
+        )
     here = pltpu.make_async_copy(
         own, wbuf.at[(pl.ds(0, total),) + gather.at + (gather.core,)], hsem
     )
     here.start()
     gather.barrier()
     here.wait()
-    load.wait()
-
-    def widen(i):
-        h[tile(i, ROW_TILE), :] = a[tile(i, ROW_TILE), :].astype(jnp.float32)
-
-    loop(count // ROW_TILE, widen)
 
     def start(i):
         for par in range(2):
             gather.pump(i, par)
 
-    loop(4, start)
+    start(0)
+
+    def keep_bias(b, x):
+        inner_bias[:, b * 128 : (b + 1) * 128] = x
+
+    permute_hidden(
+        lambda b: inner_raw[:, b * 128 : (b + 1) * 128], keep_bias, unit, w_inner.shape[2]
+    )
+    for r in range(rows):
+        id_row[r] = slot_ids(lengths, r, lax.broadcasted_iota(jnp.int32, (8, slots), 1))
+        id_col[r] = slot_ids(lengths, r, lax.broadcasted_iota(jnp.int32, (slots, 128), 0))
+    load.wait()
+
+    def widen(i):
+        h[tile(i, ROW_TILE), :] = a[tile(i, ROW_TILE), :].astype(jnp.float32)
+
+    loop(count // ROW_TILE, widen)
+
+    for i in (1, 2, 3):
+        start(i)
     pump(0)
     wload(0).start()
 
@@ -244,14 +310,14 @@
 
         def body(i):
             t = tile(i, ROW_TILE)
-            r = h[t, :] + vectors[l, bias : bias + 1, :]
+            r = h[t, :] + vectors[bias][pl.ds(l, 1), :]
             centered = r - jnp.mean(r, axis=1, keepdims=True)
             var = jnp.mean(centered * centered, axis=1, keepdims=True)
             scale = lax.rsqrt(var + EPSILON)
             xhat = centered * scale
             x_stage[t, :] = xhat
             s_stage[t, :] = jnp.broadcast_to(scale, (ROW_TILE, 128))
-            y = xhat * vectors[l, gain : gain + 1, :] + vectors[l, shift : shift + 1, :]
+            y = xhat * vectors[gain][pl.ds(l, 1), :] + vectors[shift][pl.ds(l, 1), :]
             h[t, :] = y
             a[t, :] = y.astype(jnp.bfloat16)
 
@@ -270,9 +336,13 @@
         def project(i):
             pump(base + i + 1)
             m = i // 2
-            y = matmul(a[...], weights(base + i)) + vectors[l, pl.ds(m, 1), tile(i % 2, WIDTH)]
+            cols = tile(i % 2, WIDTH)
+            bias_q = vectors[B_Q][pl.ds(l, 1), cols]
+            bias_v = vectors[B_V][pl.ds(l, 1), cols]
+            bias = jnp.where(m == 0, bias_q, jnp.where(m == 1, jnp.zeros_like(bias_v), bias_v))
+            y = matmul(a[...], weights(base + i)) + bias
             y = y * jnp.where(m == 0, jnp.float32((h.shape[1] // HEADS) ** -0.5), jnp.float32(1))
-            qkv[m, :, tile(i % 2, WIDTH)] = y.astype(jnp.bfloat16)
+            qkv[m, :, cols] = y.astype(jnp.bfloat16)
 
         loop(6, project)
         for m in range(3):
@@ -297,7 +367,7 @@
                 qm = pair_stack(qkv[0, pl.ds(top + b * BLOCK, BLOCK), lanes])
                 km = qkv[1, pl.ds(top + start, WINDOW), lanes]
                 vm = qkv[2, pl.ds(top + start, WINDOW), lanes]
-                same = id_col[r, start : start + WINDOW, :] == id_row[r, :, b * BLOCK : (b + 1) * BLOCK]
+                same = id_col[r, start : start + WINDOW, :] == id_row[r, :1, b * BLOCK : (b + 1) * BLOCK]
                 s = matmul_nt(km, qm)
                 s = jnp.where(jnp.concatenate([same, same], axis=1), s, NEGATIVE)
                 e = jnp.exp(s - jnp.max(s, axis=0, keepdims=True))
@@ -323,7 +393,7 @@
                 pump(base + 17 + i)
 
             cols = tile(i, WIDTH)
-            u[...] = matmul(a[...], weights(base + AT_INNER + i)) + inner_bias[l, :, cols]
+            u[...] = matmul(a[...], weights(base + AT_INNER + i)) + inner_bias[pl.ds(l, 1), cols]
             slot = lax.rem(i, 2)
             store_d = pltpu.make_async_copy(d_stage.at[slot], saved_d.at[l, i], dsem.at[slot])
 
@@ -369,13 +439,14 @@
     store.wait()
 
 
-def forward(devices, own, tokens, id_row, id_col, vectors, inner_bias, rows, slots):
+def forward(devices, lengths, matrices, tokens, vectors, inner_bias, rows, slots):
     count, width = tokens.shape
     hidden = inner_bias.shape[-1]
+    unit = matrices[0].shape[1]
     bf, f32 = jnp.bfloat16, jnp.float32
     blocks = slots // BLOCK
     devices_dims = chip_dims(devices)
-    held = devices_dims + (2,) + own.shape[1:]
+    held = devices_dims + (2, unit, WIDTH)
     sems = sum(d - 1 for d in devices_dims) + 1
     any_ = pl.BlockSpec(memory_space=HBM)
     vm = pl.BlockSpec(memory_space=VMEM)
@@ -390,7 +461,7 @@
             jax.ShapeDtypeStruct((LAYERS, 2, count, 128), f32),
             jax.ShapeDtypeStruct((LAYERS, hidden // WIDTH, count, WIDTH), bf),
         ),
-        in_specs=[any_, any_, vm, vm, vm, vm],
+        in_specs=[pl.BlockSpec(memory_space=pltpu.SMEM)] + [vm] * 6 + [any_] + [vm] * 9,
         out_specs=(any_,) * 7,
         scratch_shapes=[
             VMEM((count, width), f32),
@@ -404,13 +475,40 @@
             VMEM((2, count, WIDTH), bf),
             VMEM((count, width), f32),
             VMEM((count, 128), f32),
+            VMEM((LAYERS * GROUPS, unit, WIDTH), bf),
+            VMEM((rows, 8, slots), jnp.int32),
+            VMEM((rows, slots, 128), jnp.int32),
+            VMEM((LAYERS, hidden), f32),
             DMA((2,)), DMA((2,)), DMA((2,)), DMA, DMA, DMA((3,)), DMA, DMA,
             DMA((SLOTS, 2, sems)), DMA((SLOTS, 2, sems)),
         ],
         compiler_params=pltpu.CompilerParams(
-            vmem_limit_bytes=56 << 20, collective_id=0, has_side_effects=True
+            vmem_limit_bytes=58 << 20, collective_id=0, has_side_effects=True
         ),
-    )(own, tokens, id_row, id_col, vectors, inner_bias)
+    )(lengths, *matrices, tokens, *vectors, inner_bias)
+
+
+class Exchange:
+    def __init__(self, mates, held, got, ssem, rsem):
+        self.mates, self.held, self.got = mates, held, got
+        self.ssem, self.rsem = ssem, rsem
+
+    def copy(self, k):
+        return pltpu.make_async_remote_copy(
+            src_ref=self.held.at[k],
+            dst_ref=self.got.at[k],
+            send_sem=self.ssem.at[k],
+            recv_sem=self.rsem.at[k],
+            device_id=(self.mates[k],),
+            device_id_type=MESH,
+        )
+
+    def step(self, k):
+        if k > 0:
+            self.copy(k - 1).wait()
+            self.held[k] = self.held[k - 1] + self.got[k - 1]
+        if k < len(self.mates):
+            self.copy(k).start()
 
 
 def fold(x):
@@ -419,11 +517,12 @@
 
 
 def backward_kernel(
-    dims,
-    wbuf, cotangent, real, vectors, saved_qkv, saved_p, saved_x, saved_s, saved_d,
-    grad, sums,
-    g, db, du, dh, qkv, dqkv, x, sc, d, w, p, dk, dv, part,
-    wsem, psem, dsem, xsem, ssem, qsem, gsem,
+    dims, devices,
+    lengths, wbuf, cotangent, gain_attn, gain_ffn, saved_qkv, saved_p, saved_x, saved_s, saved_d,
+    grad, sums, late_sums,
+    g, db, du, dh, qkv, dqkv, x, sc, d, w, p, dk, dv, part, late,
+    held, got, late_held, late_got,
+    wsem, psem, dsem, xsem, ssem, qsem, gsem, send_sem, recv_sem, late_send, late_recv,
 ):
     rows, slots = dims
     count, width = g.shape
@@ -477,16 +576,26 @@
     wload(0).start()
     wload(1).start()
     dload(top_layer, 0).start()
+    me = lax.axis_index("dp")
+    steps = devices.bit_length() - 1
+    mates = [me + (1 << k) - 2 * (1 << k) * lax.rem(me // (1 << k), 2) for k in range(steps)]
+    barrier = pltpu.get_barrier_semaphore()
+    for to in mates:
+        pl.semaphore_signal(barrier, inc=1, device_id=(to,), device_id_type=MESH)
     first.wait()
-
-    def widen(i):
-        t = tile(i, ROW_TILE)
-        g[t, :] = db[t, :].astype(jnp.float32) * real[t, :]
-
-    loop(count // ROW_TILE, widen)
+    for r in range(rows):
+        real = slots - lengths[r, lengths.shape[1] - 1]
+
+        def widen(i):
+            t = pl.ds(pl.multiple_of(r * slots + i * ROW_TILE, ROW_TILE), ROW_TILE)
+            slot = i * ROW_TILE + lax.broadcasted_iota(jnp.int32, (ROW_TILE, width), 0)
+            g[t, :] = jnp.where(slot < real, db[t, :].astype(jnp.float32), 0.0)
+
+        loop(slots // ROW_TILE, widen)
+    pl.semaphore_wait(barrier, steps)
 
     def normalize_back(l, which):
-        gain = (G_ATTN, G_FFN)[which]
+        gain = (gain_attn, gain_ffn)[which]
         row_shift = (D_ATTN, D_FFN)[which]
         row_bias = (D_OUT, D_OUTER)[which]
         for c in xload(l, which):
@@ -496,7 +605,7 @@
             t = tile(i, ROW_TILE)
             up = g[t, :]
             xh = x[which, t, :]
-            scaled = up * vectors[l, gain : gain + 1, :]
+            scaled = up * gain[pl.ds(l, 1), :]
             m1 = jnp.mean(scaled, axis=1, keepdims=True)
             m2 = jnp.mean(scaled * xh, axis=1, keepdims=True)
             down = sc[which, t, :1] * (scaled - m1 - xh * m2)
@@ -583,7 +692,18 @@
         for c in qload(l):
             c.wait()
 
+        early = Exchange(mates, held.at[l], got.at[l], send_sem.at[l], recv_sem.at[l])
+        held[l, 0] = jnp.sum(part[...], axis=1)
+        early.step(0)
+        apart = (items - 1) // steps
+
         def attend(i):
+            for k in range(1, steps + 1):
+
+                @pl.when(i == k * apart)
+                def _():
+                    early.step(k)
+
             r = i // pairs
             lanes = tile(lax.rem(i, pairs), 128)
             slot = lax.rem(i, 2)
@@ -617,45 +737,62 @@
 
         loop(items, attend)
 
-        for m, row in ((0, D_Q), (2, D_V)):
+        sums[l] = held[l, steps]
+        for m, row in ((0, 0), (2, 1)):
 
             def add(t, carry):
                 return carry + fold(dqkv[m, tile(t, ROW_TILE), :].astype(jnp.float32))
 
-            part[row] = lax.fori_loop(
+            late[2 * l + row] = lax.fori_loop(
                 0, count // ROW_TILE, add, jnp.zeros((8, width), jnp.float32)
             )
 
+        @pl.when(l == 0)
+        def _():
+            late_held[0] = jnp.sum(late[...], axis=1)
+            last_sums.step(0)
+
         def project(i):
+            for k in range(1, min(steps, 5) + 1):
+
+                @pl.when((l == 0) & (i == k))
+                def _():
+                    last_sums.step(k)
+
             slot = weights(base + 18 + i)
             for c in range(width // 256):
                 n = slice(c * 256, (c + 1) * 256)
                 g[:, n] += matmul_nt(dqkv[i // 2, :, tile(lax.rem(i, 2), WIDTH)], w[slot, n, :])
 
         loop(6, project)
-        sums[l] = jnp.sum(part[...], axis=1)
-
-    part[...] = jnp.zeros_like(part)
+
+    last_sums = Exchange(mates, late_held, late_got, late_send, late_recv)
+    late[...] = jnp.zeros_like(late)
     loop(LAYERS, layer)
     last = pltpu.make_async_copy(g, grad, gsem)
     last.start()
+    for k in range(min(steps, 5) + 1, steps + 1):
+        last_sums.step(k)
+    late_sums[...] = late_held[steps]
     last.wait()
 
 
-def backward(wbuf, cotangent, real, vectors, saved, rows, slots):
+def backward(devices, lengths, wbuf, cotangent, gain_attn, gain_ffn, saved, rows, slots):
     count, width = cotangent.shape
     bf, f32 = jnp.bfloat16, jnp.float32
     blocks = slots // BLOCK
+    steps = devices.bit_length() - 1
     any_ = pl.BlockSpec(memory_space=HBM)
     vm = pl.BlockSpec(memory_space=VMEM)
     return pl.pallas_call(
-        functools.partial(backward_kernel, (rows, slots)),
+        functools.partial(backward_kernel, (rows, slots), devices),
         out_shape=(
             jax.ShapeDtypeStruct((count, width), f32),
-            jax.ShapeDtypeStruct((LAYERS, SUM_ROWS, width), f32),
+            jax.ShapeDtypeStruct((LAYERS, EARLY, width), f32),
+            jax.ShapeDtypeStruct((8, width), f32),
         ),
-        in_specs=[any_, any_, vm, vm] + [any_] * 5,
-        out_specs=(any_, vm),
+        in_specs=[pl.BlockSpec(memory_space=pltpu.SMEM), any_, any_, vm, vm] + [any_] * 5,
+        out_specs=(any_, vm, vm),
         scratch_shapes=[
             VMEM((count, width), f32),
             VMEM((count, width), bf),
@@ -670,64 +807,19 @@
             VMEM((2, blocks, WINDOW, 2 * BLOCK), bf),
             VMEM((slots, 128), f32),
             VMEM((slots, 128), f32),
-            VMEM((SUM_ROWS, 8, width), f32),
+            VMEM((EARLY, 8, width), f32),
+            VMEM((8, 8, width), f32),
+            VMEM((LAYERS, steps + 1, EARLY, width), f32),
+            VMEM((LAYERS, steps, EARLY, width), f32),
+            VMEM((steps + 1, 8, width), f32),
+            VMEM((steps, 8, width), f32),
             DMA((3,)), DMA((2,)), DMA((2,)), DMA((2,)), DMA((2,)), DMA((3,)), DMA,
+            DMA((LAYERS, steps)), DMA((LAYERS, steps)), DMA((steps,)), DMA((steps,)),
         ],
-        compiler_params=pltpu.CompilerParams(vmem_limit_bytes=58 << 20),
-    )(wbuf, cotangent, real, vectors, *saved)
-
-
-def reduce_kernel(devices, x, out, got, ssem, rsem):
-    me = lax.axis_index("dp")
-    steps = devices.bit_length() - 1
-    mates = [me + (1 << i) - 2 * (1 << i) * lax.rem(me >> i, 2) for i in range(steps)]
-    bar = pltpu.get_barrier_semaphore()
-    for to in mates:
-        pl.semaphore_signal(bar, inc=1, device_id=(to,), device_id_type=MESH)
-    pl.semaphore_wait(bar, steps)
-    out[0] = x[...]
-    for i, to in enumerate(mates):
-        copy = pltpu.make_async_remote_copy(
-            src_ref=out.at[i],
-            dst_ref=got.at[i],
-            send_sem=ssem.at[i],
-            recv_sem=rsem.at[i],
-            device_id=(to,),
-            device_id_type=MESH,
-        )
-        copy.start()
-        copy.wait()
-        out[i + 1] = out[i] + got[i]
-
-
-def all_sum(x, devices):
-    steps = devices.bit_length() - 1
-    out = pl.pallas_call(
-        functools.partial(reduce_kernel, devices),
-        out_shape=jax.ShapeDtypeStruct((steps + 1,) + x.shape, x.dtype),
-        in_specs=[pl.BlockSpec(memory_space=VMEM)],
-        out_specs=pl.BlockSpec(memory_space=VMEM),
-        scratch_shapes=[VMEM((steps,) + x.shape, x.dtype), DMA((steps,)), DMA((steps,))],
-        compiler_params=pltpu.CompilerParams(collective_id=1, has_side_effects=True),
-    )(x)
-    return out[steps]
-
-
-def pack(devices, w_query, w_key, w_value, w_out, w_inner, w_outer):
-    layers, rows, width = w_query.shape
-    hidden = w_inner.shape[2]
-
-    def halves(m):
-        return m.astype(jnp.bfloat16).reshape(layers, rows, -1, WIDTH).transpose(0, 2, 1, 3)
-
-    inner = w_inner.astype(jnp.bfloat16).reshape(layers, rows, devices, hidden // width, rows)
-    inner = inner.transpose(0, 3, 2, 1, 4)
-    inner = inner.reshape(layers, hidden // WIDTH, WIDTH // rows, rows, rows)
-    inner = inner.transpose(0, 1, 3, 2, 4).reshape(layers, hidden // WIDTH, rows, WIDTH)
-    outer = w_outer.astype(jnp.bfloat16).reshape(layers, hidden // width, rows, width // WIDTH, WIDTH)
-    outer = outer.transpose(0, 3, 1, 2, 4).reshape(layers, -1, rows, WIDTH)
-    parts = [halves(m) for m in (w_query, w_key, w_value, w_out)] + [inner, outer]
-    return jnp.concatenate(parts, axis=1).reshape(layers * GROUPS, rows, WIDTH)
+        compiler_params=pltpu.CompilerParams(
+            vmem_limit_bytes=58 << 20, collective_id=1, has_side_effects=True
+        ),
+    )(lengths, wbuf, cotangent, gain_attn, gain_ffn, *saved)
 
 
 def per_device(
@@ -755,43 +847,25 @@
     hidden = bias_inner.shape[1]
     unit = w_query.shape[1]
     count = rows * slots
-    segments = lengths.shape[1]
-    ends = jnp.cumsum(lengths, axis=-1)
-    position = jnp.arange(slots, dtype=jnp.int32)
-    numbers = jnp.sum((position[None, :, None] >= ends[:, None, :]).astype(jnp.int32), axis=-1)
-    is_real = numbers < segments - 1
-    ids = jnp.where(is_real, numbers, PADDING_ID + position[None, :])
-    id_row = ids[:, None, :]
-    id_col = jnp.broadcast_to(ids[:, :, None], (rows, slots, 128))
-    real = is_real.astype(jnp.float32).reshape(count, 1)
-    vectors = jnp.stack(
-        [bias_query, jnp.zeros_like(bias_query), bias_value, bias_out, bias_outer,
-         shift_attn, shift_ffn, gain_attn, gain_ffn],
-        axis=1,
-    )
-    inner_bias = (
-        bias_inner.reshape(LAYERS, devices, hidden // width, unit)
-        .transpose(0, 2, 1, 3)
-        .reshape(LAYERS, 1, hidden)
-    )
-    own = pack(devices, w_query, w_key, w_value, w_out, w_inner, w_outer)
+    vectors = (
+        bias_query, bias_value, bias_out, bias_outer, shift_attn, shift_ffn, gain_attn, gain_ffn,
+    )
+    matrices = (w_query, w_key, w_value, w_out, w_inner, w_outer)
     wbuf, out, *saved = forward(
-        devices, own, tokens.reshape(count, width), id_row, id_col, vectors, inner_bias, rows, slots
+        devices, lengths, matrices, tokens.reshape(count, width), vectors, bias_inner, rows, slots
     )
     wbuf = wbuf.reshape(LAYERS * GROUPS, width, WIDTH)
-    grad, sums = backward(
-        wbuf, cotangent.reshape(count, width), real, vectors, saved, rows, slots
-    )
-    sums = all_sum(sums, devices)
-    grad_inner = sums[:, D_INNER : D_INNER + hidden // width].reshape(
-        LAYERS, hidden // width, devices, unit
-    )
+    grad, sums, late = backward(
+        devices, lengths, wbuf, cotangent.reshape(count, width), gain_attn, gain_ffn, saved, rows, slots
+    )
+    late = late.reshape(4, 2, width)[:LAYERS]
+    grad_inner = sums[:, D_INNER:].reshape(LAYERS, hidden // width, devices, unit)
     grad_inner = grad_inner.transpose(0, 2, 1, 3).reshape(LAYERS, hidden)
     return (
         out.reshape(rows, slots, width),
         grad.reshape(rows, slots, width),
-        sums[:, D_Q],
-        sums[:, D_V],
+        late[:, 0],
+        late[:, 1],
         sums[:, D_OUT],
         grad_inner,
         sums[:, D_OUTER],

time: 475 us -> 394 us (0.83)
  Pallas kernels: 443 us -> 382 us
  local copies, waits for them, and re-layouts: 26.7 us -> 10.4 us
    pallas_call x1, Pallas kernels: 289 us -> 243 us  [forward(): pl.pallas_call(functools.partial(forward_kernel, (rows, slots), devices_d...]
    pallas_call x2 -> x1, Pallas kernels: 154 us -> 139 us  [backward(): pl.pallas_call(functools.partial(backward_kernel, (rows, slots), devices)...]
    another operation x10 -> x0, local copies, waits for them, and re-layouts: 6.98 us -> none  [per_device(): jnp.stack([bias_query, jnp.zeros_like(bias_query), bias_value, bias_out,...]
    reshape x12 -> x1, local copies, waits for them, and re-layouts: 6.04 us -> 0.1 us  [per_device(): sums[:, D_INNER:].reshape(LAYERS, hidden // width, devices, unit)]
where the time goes in v3:
time: 394 us; the launch traced here: 393 us
  Pallas kernels  382 us (97%)
  local copies, waits for them, and re-layouts  10.4 us (3%)
    pallas_call x1, Pallas kernels, forward(): pl.pallas_call(functools.partial(forward_kernel, (rows, slots), devices_d...  243 us
    pallas_call x1, Pallas kernels, backward(): pl.pallas_call(functools.partial(backward_kernel, (rows, slots), devices)...  139 us

profile of v3, /device:TPU:0, one launch (start us, length us, event | category | flops | bytes accessed | tf_op | source)
XLA Modules:
  0.0 393.2 jit_solution(8311805401270741872)
XLA Ops:
  0.6 242.7 %shard_map.241 = (bf16[48,4,2,2,2,32,512]{6,5,4,3,2,1,0:T(8,128)(2,1)}, bf16[1024,1024]{1,0:T(8,128)(2,1)}, bf16[2,3,1024,1024]{3,2,1,0:T(8,128)(2,1)}, bf16[2,1...) custom-call(s32[2,16]{1,0:T(2,128)} %lengths.3, ...), custom_call_target="tpu_custom_call" | custom-call | tf_op jit(solution)/shard_map/pallas_call | solution.py:453
  243.4 0.0 copy-start.1
  243.4 139.3 %shard_map.242 = (f32[1024,1024]{1,0:T(8,128)}, f32[2,8,1024]{2,1,0:T(8,128)}, f32[8,1024]{1,0:T(8,128)}) custom-call(s32[2,16]{1,0:T(2,128)} %lengths.3, bf16[48,1024,512]{2,1,0:T(8,128)(2,1)} %bitcast.18, bf16[1024,1024]{1,0:T(8,128)(2,1)} %bitcast.20, f32[2,1024]{1,0:T(2,128)} %gain_attn.1, f32[2,1024]{1,0:T(2,128)} %gain_ffn.1, ...), custom_call_target="tpu_custom_call" | custom-call | tf_op jit(solution)/shard_map/pallas_call | solution.py:787
  382.8 0.8 slice.27
  383.6 0.6 copy_bitcast_fusion
  384.2 0.8 slice.32
  385.0 1.0 fusion
  386.0 0.6 copy_bitcast_fusion.2
  386.6 0.6 copy_bitcast_fusion.4
  387.3 0.1 reshape.46
  387.4 0.1 copy.29
  387.4 0.8 reshape.47
  388.2 0.0 copy-done.1
  388.2 0.0 copy-start
  388.2 1.3 copy.44
  389.5 1.6 copy-done
  391.2 2.0 copy.45
  (2 shorter events, 0.0 us)
Async XLA Ops:
  243.4 144.8 %copy-start.1 = (bf16[1024,1024]{1,0:T(8,128)(2,1)S(1)}, bf16[1024,1024]{1,0:T(8,128)(2,1)}, u32[]{:S(2)}) copy-start(bf16[1024,1024]{1,0:T(8,128)(2,1)} %get-tuple-element.19) | copy-start | bytes 6291460
  388.2 2.9 copy-start

commit v4 on v3

--- a/solution.py
+++ b/solution.py
@@ -37,7 +37,8 @@
     return (1 << first, 1 << second, 1 << (bits - first - second))
 
 
-ORDERS = (((0, 2, 1), (1, 0, 2)), ((0, 1, 2), (2, 0, 1)))
+RELAY = 4
+ORDERS = (((0, 4, 2, 1, 3), (1, 0, 4, 2, 3)), ((0, 4, 1, 2, 3), (2, 0, 4, 1, 3)))
 SLOTS = 8
 
 
@@ -51,19 +52,20 @@
         chip = self.me // 2
         self.at = (chip // (n1 * n2), lax.rem(chip // n2, n1), lax.rem(chip, n2))
         self.step = (n1 * n2 * 2, n2 * 2, 2)
+        self.relay = dims[0] == 4
+        self.orders = ORDERS
+        if not self.relay:
+            self.orders = tuple(
+                tuple(tuple(d for d in order if d != RELAY) for order in pair) for pair in ORDERS
+            )
+        self.phases = len(self.orders[0][0])
         rows, cols = own.shape[-2:]
-        if rows % 32 == 0:
-            cut = rows * 3 // 4
-            self.parts = (
-                (pl.ds(0, cut), pl.ds(0, cols)),
-                (pl.ds(cut, rows - cut), pl.ds(0, cols)),
-            )
+        if rows % 16 == 0:
+            half = rows // 2
+            self.parts = tuple((pl.ds(c * half, half), pl.ds(0, cols)) for c in range(2))
         else:
-            cut = cols * 3 // 4
-            self.parts = (
-                (pl.ds(0, rows), pl.ds(0, cut)),
-                (pl.ds(0, rows), pl.ds(cut, cols - cut)),
-            )
+            half = cols // 2
+            self.parts = tuple((pl.ds(0, rows), pl.ds(c * half, half)) for c in range(2))
 
     def peers(self, dim):
         if dim == 3:
@@ -74,38 +76,58 @@
             out.append(self.me + (to - self.at[dim]) * self.step[dim])
         return out
 
-    def copies(self, g, par, s, p):
-        order = ORDERS[par][s] + (3,)
-        full = order[:p]
-        where = tuple(
-            pl.ds(0, self.dims[d]) if d in full else self.at[d] for d in range(3)
-        )
+    def moves(self, g, par, s, p):
+        order = self.orders[par][s]
+        dim, full = order[p], order[:p]
+        n0, n1, n2 = self.dims
+        first = (0, n0, n0 + n1 - 1, n0 + n1 + n2 - 2, n0 - 1)[dim]
+        where = [pl.ds(0, self.dims[d]) if d in full else self.at[d] for d in range(3)]
+        slot = lax.rem(g, SLOTS)
+        z = self.at[0]
+        if dim == RELAY:
+            middle = (z == 1) | (z == 2)
+            where[0] = jnp.where(z < 2, 3, 0)
+            targets = [self.me + (3 - where[0] - z) * self.step[0]]
+            guards = [(middle, jnp.logical_not(middle))]
+        else:
+            targets = self.peers(dim)
+            guards = [(None, None)] * len(targets)
+            if dim == 0 and self.relay:
+                guards = [
+                    (jnp.abs(lax.rem(z + d, 4) - z) != 3, jnp.abs(lax.rem(z + 4 - d, 4) - z) != 3)
+                    if d != 2
+                    else (None, None)
+                    for d in (1, 2, 3)
+                ]
         sub = self.parts[s]
-        dst = self.buf.at[(g,) + where + (self.core,) + sub]
+        dst = self.buf.at[(g,) + tuple(where) + (self.core,) + sub]
         src = self.own.at[(g,) + sub] if p == 0 else dst
-        slot = lax.rem(g, SLOTS)
-        first = sum(self.dims[d] - 1 for d in order[:p])
         return [
-            pltpu.make_async_remote_copy(
-                src_ref=src,
-                dst_ref=dst,
-                send_sem=self.ssem.at[slot, s, first + i],
-                recv_sem=self.rsem.at[slot, s, first + i],
-                device_id=(to,),
-                device_id_type=MESH,
+            (
+                pltpu.make_async_remote_copy(
+                    src_ref=src,
+                    dst_ref=dst,
+                    send_sem=self.ssem.at[slot, s, first + i],
+                    recv_sem=self.rsem.at[slot, s, first + i],
+                    device_id=(to,),
+                    device_id_type=MESH,
+                ),
+                *guard,
             )
-            for i, to in enumerate(self.peers(order[p]))
+            for i, (to, guard) in enumerate(zip(targets, guards))
         ]
 
-    def barrier(self):
+    def greet(self):
         bar = pltpu.get_barrier_semaphore()
-        everyone = [to for d in range(4) for to in self.peers(d)]
-        for to in everyone:
-            pl.semaphore_signal(bar, inc=1, device_id=(to,), device_id_type=MESH)
-        pl.semaphore_wait(bar, len(everyone))
+        for d in range(4):
+            for to in self.peers(d):
+                pl.semaphore_signal(bar, inc=1, device_id=(to,), device_id_type=MESH)
+
+    def meet(self):
+        pl.semaphore_wait(pltpu.get_barrier_semaphore(), sum(self.dims) - 3 + 1)
 
     def pump(self, pair_step, par):
-        for p in (3, 2, 1, 0):
+        for p in range(self.phases, -1, -1):
             pair = pair_step - p
 
             @pl.when((pair >= 0) & (pair < self.total // 2))
@@ -113,18 +135,18 @@
                 g = 2 * pair + par
                 for s in range(2):
                     if p > 0:
-                        for c in self.copies(g, par, s, p - 1):
-                            c.wait()
-                    for c in self.copies(g, par, s, p):
-                        c.start()
-
-        pair = pair_step - 4
-
-        @pl.when((pair >= 0) & (pair < self.total // 2))
-        def _():
-            for s in range(2):
-                for c in self.copies(2 * pair + par, par, s, 3):
-                    c.wait()
+                        for copy, sends, receives in self.moves(g, par, s, p - 1):
+                            if sends is None:
+                                copy.wait()
+                            else:
+                                pl.when(sends)(copy.wait_send)
+                                pl.when(receives)(copy.wait_recv)
+                    if p < self.phases:
+                        for copy, sends, _ in self.moves(g, par, s, p):
+                            if sends is None:
+                                copy.start()
+                            else:
+                                pl.when(sends)(copy.start)
 
 
 def matmul(left, right):
@@ -240,16 +262,30 @@
 
             @pl.when(lax.rem(half, 2) == par)
             def _():
-                gather.pump(half // 2 + 4, par)
-
+                gather.pump(half // 2 + gather.phases, par)
+
+    gather.greet()
     load = pltpu.make_async_copy(tokens, a, tsem)
     load.start()
     unit = own.shape[1]
+
+    def cast(l, m):
+        matrix = (w_query, w_key, w_value, w_out)[m]
+        for c in range(2):
+            own[l * GROUPS + 2 * m + c] = matrix[l, :, tile(c, WIDTH)].astype(jnp.bfloat16)
+
+    def start(i):
+        for par in range(2):
+            gather.pump(i, par)
+
+    cast(0, 0)
+    gather.meet()
+    start(0)
     for l in range(LAYERS):
         at = l * GROUPS
-        for m, matrix in enumerate((w_query, w_key, w_value, w_out)):
-            for c in range(2):
-                own[at + 2 * m + c] = matrix[l, :, c * WIDTH : (c + 1) * WIDTH].astype(jnp.bfloat16)
+        for m in range(4):
+            if (l, m) != (0, 0):
+                cast(l, m)
         for c in range(2):
             for kc in range(4):
                 piece = w_outer[l, kc * unit : (kc + 1) * unit, c * WIDTH : (c + 1) * WIDTH]
@@ -264,14 +300,8 @@
         own, wbuf.at[(pl.ds(0, total),) + gather.at + (gather.core,)], hsem
     )
     here.start()
-    gather.barrier()
     here.wait()
-
-    def start(i):
-        for par in range(2):
-            gather.pump(i, par)
-
-    start(0)
+    start(1)
 
     def keep_bias(b, x):
         inner_bias[:, b * 128 : (b + 1) * 128] = x
@@ -289,7 +319,7 @@
 
     loop(count // ROW_TILE, widen)
 
-    for i in (1, 2, 3):
+    for i in range(2, gather.phases):
         start(i)
     pump(0)
     wload(0).start()
@@ -349,9 +379,9 @@
             pltpu.make_async_copy(qkv.at[m], saved_qkv.at[l, m], qsem.at[m]).start()
 
         def attend(i):
-            @pl.when(lax.rem(i, 2) == 0)
+            @pl.when(lax.rem(i, 3) == 0)
             def _():
-                pump(base + 7 + i // 2)
+                pump(base + 7 + i // 3)
 
             r = i // pairs
             lanes = tile(lax.rem(i, pairs), 128)
@@ -380,7 +410,7 @@
         loop(rows * pairs, attend)
 
         def attn_out(i):
-            pump(base + 15 + i)
+            pump(base + 13 + i)
             cols = tile(i, WIDTH)
             h[:, cols] += matmul(o[...], weights(base + AT_OUT + i))
 
@@ -388,9 +418,9 @@
         normalize(l, 0)
 
         def inner(i):
-            @pl.when(i < 6)
+            @pl.when(lax.rem(i, 4) < 3)
             def _():
-                pump(base + 17 + i)
+                pump(base + 15 + i - i // 4)
 
             cols = tile(i, WIDTH)
             u[...] = matmul(a[...], weights(base + AT_INNER + i)) + inner_bias[pl.ds(l, 1), cols]
@@ -415,9 +445,13 @@
         loop(8, inner)
 
         def outer(i):
-            @pl.when(i < 2)
+            @pl.when((lax.rem(i, 2) == 0) & (i > 0))
             def _():
-                pump(base + 23 + i)
+                pump(base + 20 + i // 2)
+
+            @pl.when(i == 7)
+            def _():
+                pump(base + 24)
 
             cols = tile(i // 4, WIDTH)
             h[:, cols] += matmul(z[lax.rem(i, 4)], weights(base + AT_OUTER + i))
@@ -447,7 +481,7 @@
     blocks = slots // BLOCK
     devices_dims = chip_dims(devices)
     held = devices_dims + (2, unit, WIDTH)
-    sems = sum(d - 1 for d in devices_dims) + 1
+    sems = sum(devices_dims) - 1
     any_ = pl.BlockSpec(memory_space=HBM)
     vm = pl.BlockSpec(memory_space=VMEM)
     return pl.pallas_call(
@@ -822,6 +856,46 @@
     )(lengths, wbuf, cotangent, gain_attn, gain_ffn, *saved)
 
 
+def finish_kernel(unit, sums, late, query, value, out, inner, outer, attn, ffn):
+    width = sums.shape[2]
+    devices = width // unit
+    for l in range(LAYERS):
+        here = slice(l, l + 1)
+        for row, ref in ((D_OUT, out), (D_OUTER, outer), (D_ATTN, attn), (D_FFN, ffn)):
+            ref[here, :] = sums[l, row : row + 1, :]
+        query[here, :] = late[2 * l : 2 * l + 1, :]
+        value[here, :] = late[2 * l + 1 : 2 * l + 2, :]
+        for b in range(inner.shape[1] // 128):
+            block = None
+            for piece in range(128 // unit):
+                device, quarter = divmod(b * (128 // unit) + piece, inner.shape[1] // width)
+                source = device * unit
+                row = D_INNER + quarter
+                first = source // 128 * 128
+                x = sums[l, row : row + 1, first : first + 128]
+                shift = (piece * unit - source) % 128
+                if shift:
+                    x = pltpu.roll(x, shift, axis=1)
+                if block is None:
+                    block = x
+                else:
+                    lane = lax.broadcasted_iota(jnp.int32, x.shape, 1)
+                    block = jnp.where(lane >= piece * unit, x, block)
+            inner[here, b * 128 : (b + 1) * 128] = block
+
+
+def finish(unit, hidden, sums, late):
+    width = sums.shape[2]
+    vm = pl.BlockSpec(memory_space=VMEM)
+    sizes = (width, width, width, hidden, width, width, width)
+    return pl.pallas_call(
+        functools.partial(finish_kernel, unit),
+        out_shape=tuple(jax.ShapeDtypeStruct((LAYERS, n), jnp.float32) for n in sizes),
+        in_specs=[vm, vm],
+        out_specs=(vm,) * 7,
+    )(sums, late)
+
+
 def per_device(
     devices,
     tokens,
@@ -858,19 +932,10 @@
     grad, sums, late = backward(
         devices, lengths, wbuf, cotangent.reshape(count, width), gain_attn, gain_ffn, saved, rows, slots
     )
-    late = late.reshape(4, 2, width)[:LAYERS]
-    grad_inner = sums[:, D_INNER:].reshape(LAYERS, hidden // width, devices, unit)
-    grad_inner = grad_inner.transpose(0, 2, 1, 3).reshape(LAYERS, hidden)
     return (
         out.reshape(rows, slots, width),
         grad.reshape(rows, slots, width),
-        late[:, 0],
-        late[:, 1],
-        sums[:, D_OUT],
-        grad_inner,
-        sums[:, D_OUTER],
-        sums[:, D_ATTN],
-        sums[:, D_FFN],
+        *finish(unit, hidden, sums, late),
     )
 
 

time: 394 us -> 368 us (0.934)
  Pallas kernels: 382 us -> 362 us
  local copies, waits for them, and re-layouts: 10.4 us -> 4.96 us
    pallas_call x1, Pallas kernels: 243 us -> 223 us  [forward(): pl.pallas_call(functools.partial(forward_kernel, (rows, slots), devices_d...]
where the time goes in v4:
time: 368 us; the launch traced here: 367 us
  Pallas kernels  362 us (98%)
  local copies, waits for them, and re-layouts  4.96 us (1%)
    pallas_call x1, Pallas kernels, forward(): pl.pallas_call(functools.partial(forward_kernel, (rows, slots), devices_d...  223 us
    pallas_call x1, Pallas kernels, backward(): pl.pallas_call(functools.partial(backward_kernel, (rows, slots), devices)...  137 us

profile of v4, /device:TPU:0, one launch (start us, length us, event | category | flops | bytes accessed | tf_op | source)
XLA Modules:
  0.0 367.3 jit_solution(15037908655286859275)
XLA Ops:
  0.6 222.9 %shard_map.241 = (bf16[48,4,2,2,2,32,512]{6,5,4,3,2,1,0:T(8,128)(2,1)}, bf16[1024,1024]{1,0:T(8,128)(2,1)}, bf16[2,3,1024,1024]{3,2,1,0:T(8,128)(2,1)}, bf16[2,1...) custom-call(s32[2,16]{1,0:T(2,128)} %lengths.3, ...), custom_call_target="tpu_custom_call" | custom-call | tf_op jit(solution)/shard_map/pallas_call | solution.py:487
  223.6 0.0 copy-start.1
  223.6 137.0 %shard_map.242 = (f32[1024,1024]{1,0:T(8,128)}, f32[2,8,1024]{2,1,0:T(8,128)}, f32[8,1024]{1,0:T(8,128)}) custom-call(s32[2,16]{1,0:T(2,128)} %lengths.3, bf16[48,1024,512]{2,1,0:T(8,128)(2,1)} %bitcast.5, bf16[1024,1024]{1,0:T(8,128)(2,1)} %bitcast.7, f32[2,1024]{1,0:T(2,128)} %gain_attn.1, f32[2,1024]{1,0:T(2,128)} %gain_ffn.1, ...), custom_call_target="tpu_custom_call" | custom-call | tf_op jit(solution)/shard_map/pallas_call | solution.py:821
  360.6 1.7 shard_map.243
  362.3 0.0 copy-start
  362.3 0.0 copy-done.1
  362.3 1.3 copy.29
  363.7 1.6 copy-done
  365.3 2.0 copy.30
Async XLA Ops:
  223.6 138.8 %copy-start.1 = (bf16[1024,1024]{1,0:T(8,128)(2,1)S(1)}, bf16[1024,1024]{1,0:T(8,128)(2,1)}, u32[]{:S(2)}) copy-start(bf16[1024,1024]{1,0:T(8,128)(2,1)} %get-tuple-element.26) | copy-start | bytes 6291460
  362.3 2.9 copy-start

commit v5 on v4

--- a/solution.py
+++ b/solution.py
@@ -393,13 +393,18 @@
                 store_p.wait()
 
             top = pl.multiple_of(r * slots, slots)
-            for b, start in enumerate(window_starts(slots)):
-                qm = pair_stack(qkv[0, pl.ds(top + b * BLOCK, BLOCK), lanes])
-                km = qkv[1, pl.ds(top + start, WINDOW), lanes]
+            starts = window_starts(slots)
+            scores = [
+                matmul_nt(
+                    qkv[1, pl.ds(top + start, WINDOW), lanes],
+                    pair_stack(qkv[0, pl.ds(top + b * BLOCK, BLOCK), lanes]),
+                )
+                for b, start in enumerate(starts)
+            ]
+            for b, start in enumerate(starts):
                 vm = qkv[2, pl.ds(top + start, WINDOW), lanes]
                 same = id_col[r, start : start + WINDOW, :] == id_row[r, :1, b * BLOCK : (b + 1) * BLOCK]
-                s = matmul_nt(km, qm)
-                s = jnp.where(jnp.concatenate([same, same], axis=1), s, NEGATIVE)
+                s = jnp.where(jnp.concatenate([same, same], axis=1), scores[b], NEGATIVE)
                 e = jnp.exp(s - jnp.max(s, axis=0, keepdims=True))
                 p = e * (1.0 / jnp.sum(e, axis=0, keepdims=True))
                 p = p.astype(jnp.bfloat16)
@@ -522,27 +527,51 @@
     )(lengths, *matrices, tokens, *vectors, inner_bias)
 
 
+def digits(devices):
+    out, stride = [], 1
+    while stride < devices:
+        size = 2 if stride == 1 else min(4, devices // stride)
+        out.append((stride, size))
+        stride *= size
+    return out
+
+
 class Exchange:
-    def __init__(self, mates, held, got, ssem, rsem):
-        self.mates, self.held, self.got = mates, held, got
-        self.ssem, self.rsem = ssem, rsem
-
-    def copy(self, k):
-        return pltpu.make_async_remote_copy(
-            src_ref=self.held.at[k],
-            dst_ref=self.got.at[k],
-            send_sem=self.ssem.at[k],
-            recv_sem=self.rsem.at[k],
-            device_id=(self.mates[k],),
-            device_id_type=MESH,
-        )
+    def __init__(self, me, places, held, got, ssem, rsem):
+        self.me, self.places = me, places
+        self.held, self.got, self.ssem, self.rsem = held, got, ssem, rsem
+
+    def copies(self, k):
+        stride, size = self.places[k]
+        digit = lax.rem(self.me // stride, size)
+        out = []
+        for d in range(1, size):
+            to = self.me + (lax.rem(digit + d, size) - digit) * stride
+            out.append(
+                pltpu.make_async_remote_copy(
+                    src_ref=self.held.at[k],
+                    dst_ref=self.got.at[k, digit],
+                    send_sem=self.ssem.at[k, d],
+                    recv_sem=self.rsem.at[k, d],
+                    device_id=(to,),
+                    device_id_type=MESH,
+                )
+            )
+        return out, digit, size
 
     def step(self, k):
         if k > 0:
-            self.copy(k - 1).wait()
-            self.held[k] = self.held[k - 1] + self.got[k - 1]
-        if k < len(self.mates):
-            self.copy(k).start()
+            copies, digit, size = self.copies(k - 1)
+            for c in copies:
+                c.wait()
+            self.got[k - 1, digit] = self.held[k - 1]
+            total = self.got[k - 1, 0]
+            for j in range(1, size):
+                total = total + self.got[k - 1, j]
+            self.held[k] = total
+        if k < len(self.places):
+            for c in self.copies(k)[0]:
+                c.start()
 
 
 def fold(x):
@@ -551,38 +580,48 @@
 
 
 def backward_kernel(
-    dims, devices,
+    dims, places,
     lengths, wbuf, cotangent, gain_attn, gain_ffn, saved_qkv, saved_p, saved_x, saved_s, saved_d,
     grad, sums, late_sums,
-    g, db, du, dh, qkv, dqkv, x, sc, d, w, p, dk, dv, part, late,
+    g, db, du, qkv, dqkv, x, sc, d, w, p, dk, dv, part, late,
     held, got, late_held, late_got,
-    wsem, psem, dsem, xsem, ssem, qsem, gsem, send_sem, recv_sem, late_send, late_recv,
+    wsem, psem, dsem, xsem, ssem, qsem, csem, gsem, send_sem, recv_sem, late_send, late_recv,
 ):
     rows, slots = dims
     count, width = g.shape
     pairs = HEADS // 2
-    total = LAYERS * GROUPS
+    per_layer = GROUPS // 2
+    total = LAYERS * per_layer
     items = rows * pairs
-
-    def block_of(i):
-        l = LAYERS - 1 - i // GROUPS
-        j = lax.rem(i, GROUPS)
-        quarter, within = j // 4, lax.rem(j, 4)
-        ffn = jnp.where(within < 2, AT_OUTER + 4 * within + quarter, AT_INNER + 2 * quarter + within - 2)
-        late = jnp.where(j < 18, AT_OUT + j - 16, j - 18)
-        return l * GROUPS + jnp.where(j < 16, ffn, late)
+    steps = len(places)
+    chunk = 256
+    chunks = [slice(c * chunk, (c + 1) * chunk) for c in range(width // chunk)]
 
     def wload(i):
+        l = LAYERS - 1 - i // per_layer
+        j = lax.rem(i, per_layer)
+        outer = (j < 8) & (lax.rem(j, 2) == 0)
+        ffn = jnp.where(outer, AT_OUTER + j // 2, AT_INNER + j // 2 * 2)
+        block = l * GROUPS + jnp.where(j < 8, ffn, jnp.where(j == 8, AT_OUT, 2 * (j - 9)))
         slot = lax.rem(i, 3)
-        return pltpu.make_async_copy(wbuf.at[block_of(i)], w.at[slot], wsem.at[slot])
+        apart = jnp.where(outer, 4, 1)
+        return [
+            pltpu.make_async_copy(wbuf.at[block + c * apart], w.at[slot, c], wsem.at[slot, c])
+            for c in range(2)
+        ]
 
     def weights(i):
         @pl.when(i + 2 < total)
         def _():
-            wload(i + 2).start()
-
-        wload(i).wait()
+            for c in wload(i + 2):
+                c.start()
+
+        for c in wload(i):
+            c.wait()
         return lax.rem(i, 3)
+
+    def product(left, slot, n):
+        return matmul_nt(left[:, :WIDTH], w[slot, 0, n, :]) + matmul_nt(left[:, WIDTH:], w[slot, 1, n, :])
 
     def xload(l, which):
         return (
@@ -590,32 +629,36 @@
             pltpu.make_async_copy(saved_s.at[l, which], sc.at[which], ssem.at[which]),
         )
 
-    def dload(l, i):
-        slot = lax.rem(i, 2)
-        return pltpu.make_async_copy(saved_d.at[l, i], d.at[slot], dsem.at[slot])
+    def dload(l, quarter):
+        slot = lax.rem(quarter, 2)
+        return pltpu.make_async_copy(saved_d.at[l, pl.ds(2 * quarter, 2)], d.at[slot], dsem.at[slot])
 
     def pload(l, i):
-        slot = lax.rem(i, 2)
+        slot = lax.rem(i, 3)
         return pltpu.make_async_copy(saved_p.at[l, i], p.at[slot], psem.at[slot])
 
     def qload(l):
         return [pltpu.make_async_copy(saved_qkv.at[l, m], qkv.at[m], qsem.at[m]) for m in range(3)]
 
     top_layer = LAYERS - 1
-    first = pltpu.make_async_copy(cotangent, db, gsem)
+    first = pltpu.make_async_copy(cotangent, db, csem)
     first.start()
-    for which in (1, 0):
-        for c in xload(top_layer, which):
+    for c in xload(top_layer, 1):
+        c.start()
+    for i in range(2):
+        for c in wload(i):
             c.start()
-    wload(0).start()
-    wload(1).start()
     dload(top_layer, 0).start()
+    for c in xload(top_layer, 0):
+        c.start()
     me = lax.axis_index("dp")
-    steps = devices.bit_length() - 1
-    mates = [me + (1 << k) - 2 * (1 << k) * lax.rem(me // (1 << k), 2) for k in range(steps)]
-    barrier = pltpu.get_barrier_semaphore()
-    for to in mates:
-        pl.semaphore_signal(barrier, inc=1, device_id=(to,), device_id_type=MESH)
+    if steps:
+        barrier = pltpu.get_barrier_semaphore()
+        for stride, size in places:
+            digit = lax.rem(me // stride, size)
+            for k in range(1, size):
+                to = me + (lax.rem(digit + k, size) - digit) * stride
+                pl.semaphore_signal(barrier, inc=1, device_id=(to,), device_id_type=MESH)
     first.wait()
     for r in range(rows):
         real = slots - lengths[r, lengths.shape[1] - 1]
@@ -626,7 +669,8 @@
             g[t, :] = jnp.where(slot < real, db[t, :].astype(jnp.float32), 0.0)
 
         loop(slots // ROW_TILE, widen)
-    pl.semaphore_wait(barrier, steps)
+    if steps:
+        pl.semaphore_wait(barrier, sum(size - 1 for _, size in places))
 
     def normalize_back(l, which):
         gain = (gain_attn, gain_ffn)[which]
@@ -658,53 +702,34 @@
             for c in xload(l - 1, which):
                 c.start()
 
+    last_sums = Exchange(me, places, late_held, late_got, late_send, late_recv)
+
     def layer(step):
         l = top_layer - step
-        base = step * GROUPS
-        for c in qload(l):
-            c.start()
+        base = step * per_layer
         normalize_back(l, 1)
 
         def quarter(kc):
-            at = base + 4 * kc
-            slot = weights(at)
-            for c in range(width // 256):
-                n = slice(c * 256, (c + 1) * 256)
-                dh[:, n] = matmul_nt(db[:, :WIDTH], w[slot, n, :])
-            slot = weights(at + 1)
-            for c in range(width // 256):
-                n = slice(c * 256, (c + 1) * 256)
-                dh[:, n] += matmul_nt(db[:, WIDTH:], w[slot, n, :])
-
-            total_ = []
-            for half in range(2):
-                i = 2 * kc + half
-
-                @pl.when(i + 1 < 8)
-                def _():
-                    dload(l, i + 1).start()
-
-                dload(l, i).wait()
-
-                def slope(t, carry):
-                    tl = tile(t, ROW_TILE)
-                    cols = pl.ds(half * WIDTH, WIDTH)
-                    low = (dh[tl, cols] * d[half, tl, :].astype(jnp.float32)).astype(jnp.bfloat16)
-                    du[tl, cols] = low
-                    return carry + fold(low.astype(jnp.float32))
-
-                total_.append(
-                    lax.fori_loop(0, count // ROW_TILE, slope, jnp.zeros((8, WIDTH), jnp.float32))
-                )
-            part[D_INNER + kc] = jnp.concatenate(total_, axis=1)
-
-            def into(half):
-                slot = weights(at + 2 + half)
-                for c in range(width // 256):
-                    n = slice(c * 256, (c + 1) * 256)
-                    g[:, n] += matmul_nt(du[:, tile(half, WIDTH)], w[slot, n, :])
-
-            loop(2, into)
+            @pl.when(kc + 1 < 4)
+            def _():
+                dload(l, kc + 1).start()
+
+            @pl.when(kc == 1)
+            def _():
+                for c in qload(l):
+                    c.start()
+
+            slot = weights(base + 2 * kc)
+            dload(l, kc).wait()
+            for c, n in enumerate(chunks):
+                within = slice(c * chunk % WIDTH, c * chunk % WIDTH + chunk)
+                slope = d[lax.rem(kc, 2), c * chunk // WIDTH, :, within].astype(jnp.float32)
+                low = (product(db, slot, n) * slope).astype(jnp.bfloat16)
+                du[:, n] = low
+                part[D_INNER + kc, :, n] = fold(low.astype(jnp.float32))
+            slot = weights(base + 2 * kc + 1)
+            for n in chunks:
+                g[:, n] += product(du, slot, n)
 
         loop(4, quarter)
 
@@ -713,64 +738,57 @@
             dload(l - 1, 0).start()
 
         pload(l, 0).start()
+        pload(l, 1).start()
         normalize_back(l, 0)
-
-        slot = weights(base + 16)
-        for c in range(width // 256):
-            n = slice(c * 256, (c + 1) * 256)
-            dh[:, n] = matmul_nt(db[:, :WIDTH], w[slot, n, :])
-        slot = weights(base + 17)
-        for c in range(width // 256):
-            n = slice(c * 256, (c + 1) * 256)
-            du[:, n] = (dh[:, n] + matmul_nt(db[:, WIDTH:], w[slot, n, :])).astype(jnp.bfloat16)
+        slot = weights(base + 8)
+        for n in chunks:
+            du[:, n] = product(db, slot, n).astype(jnp.bfloat16)
         for c in qload(l):
             c.wait()
-
-        early = Exchange(mates, held.at[l], got.at[l], send_sem.at[l], recv_sem.at[l])
+        early = Exchange(me, places, held.at[l], got.at[l], send_sem.at[l], recv_sem.at[l])
         held[l, 0] = jnp.sum(part[...], axis=1)
         early.step(0)
-        apart = (items - 1) // steps
 
         def attend(i):
             for k in range(1, steps + 1):
 
-                @pl.when(i == k * apart)
+                @pl.when(i == 3 * k)
                 def _():
                     early.step(k)
 
             r = i // pairs
             lanes = tile(lax.rem(i, pairs), 128)
-            slot = lax.rem(i, 2)
-
-            @pl.when(i + 1 < items)
-            def _():
-                pload(l, i + 1).start()
+            slot = lax.rem(i, 3)
+
+            @pl.when(i + 2 < items)
+            def _():
+                pload(l, i + 2).start()
 
             pload(l, i).wait()
             dk[...] = jnp.zeros_like(dk)
             dv[...] = jnp.zeros_like(dv)
             top = pl.multiple_of(r * slots, slots)
-            for b, start in enumerate(window_starts(slots)):
-                mine = pl.ds(top + b * BLOCK, BLOCK)
-                reach = pl.ds(top + start, WINDOW)
-                qm = pair_stack(qkv[0, mine, lanes])
-                om = pair_stack(du[mine, lanes])
+            starts = window_starts(slots)
+            mine = [pl.ds(top + b * BLOCK, BLOCK) for b in range(len(starts))]
+            reach = [pl.ds(top + start, WINDOW) for start in starts]
+            stacked = [pair_stack(du[rows_, lanes]) for rows_ in mine]
+            dps = [matmul_nt(qkv[2, keys, lanes], om) for keys, om in zip(reach, stacked)]
+            for b, start in enumerate(starts):
+                qm = pair_stack(qkv[0, mine[b], lanes])
                 pb = p[slot, b]
                 pf = pb.astype(jnp.float32)
-                dp = matmul_nt(qkv[2, reach, lanes], om)
-                weighted = pf * dp
+                weighted = pf * dps[b]
                 ds = weighted - pf * jnp.sum(weighted, axis=0, keepdims=True)
                 ds = ds.astype(jnp.bfloat16)
                 dk[start : start + WINDOW, :] += matmul(ds, qm)
-                dv[start : start + WINDOW, :] += matmul(pb, om)
-                dq = pair_join(matmul_tn(ds, qkv[1, reach, lanes]))
-                dqkv[0, mine, lanes] = (dq * (width // HEADS) ** -0.5).astype(jnp.bfloat16)
+                dv[start : start + WINDOW, :] += matmul(pb, stacked[b])
+                dq = pair_join(matmul_tn(ds, qkv[1, reach[b], lanes]))
+                dqkv[0, mine[b], lanes] = (dq * (width // HEADS) ** -0.5).astype(jnp.bfloat16)
             every = pl.ds(top, slots)
             dqkv[1, every, lanes] = dk[...].astype(jnp.bfloat16)
             dqkv[2, every, lanes] = dv[...].astype(jnp.bfloat16)
 
         loop(items, attend)
-
         sums[l] = held[l, steps]
         for m, row in ((0, 0), (2, 1)):
 
@@ -786,40 +804,42 @@
             late_held[0] = jnp.sum(late[...], axis=1)
             last_sums.step(0)
 
-        def project(i):
-            for k in range(1, min(steps, 5) + 1):
-
-                @pl.when((l == 0) & (i == k))
+        for m in range(3):
+            slot = weights(base + 9 + m)
+            for c, n in enumerate(chunks):
+                g[:, n] += product(dqkv.at[m], slot, n)
+                if m == 2:
+
+                    @pl.when(l == 0)
+                    def _():
+                        pltpu.make_async_copy(g.at[:, n], grad.at[:, n], gsem.at[c]).start()
+
+            if m + 1 < steps:
+
+                @pl.when(l == 0)
                 def _():
-                    last_sums.step(k)
-
-            slot = weights(base + 18 + i)
-            for c in range(width // 256):
-                n = slice(c * 256, (c + 1) * 256)
-                g[:, n] += matmul_nt(dqkv[i // 2, :, tile(lax.rem(i, 2), WIDTH)], w[slot, n, :])
-
-        loop(6, project)
-
-    last_sums = Exchange(mates, late_held, late_got, late_send, late_recv)
+                    last_sums.step(m + 1)
+
     late[...] = jnp.zeros_like(late)
     loop(LAYERS, layer)
-    last = pltpu.make_async_copy(g, grad, gsem)
-    last.start()
-    for k in range(min(steps, 5) + 1, steps + 1):
-        last_sums.step(k)
+    for k in range(min(steps, 3), steps + 1):
+        if k > 0:
+            last_sums.step(k)
     late_sums[...] = late_held[steps]
-    last.wait()
+    for c, n in enumerate(chunks):
+        pltpu.make_async_copy(g.at[:, n], grad.at[:, n], gsem.at[c]).wait()
 
 
 def backward(devices, lengths, wbuf, cotangent, gain_attn, gain_ffn, saved, rows, slots):
     count, width = cotangent.shape
     bf, f32 = jnp.bfloat16, jnp.float32
     blocks = slots // BLOCK
-    steps = devices.bit_length() - 1
+    places = digits(devices)
+    steps = max(len(places), 1)
     any_ = pl.BlockSpec(memory_space=HBM)
     vm = pl.BlockSpec(memory_space=VMEM)
     return pl.pallas_call(
-        functools.partial(backward_kernel, (rows, slots), devices),
+        functools.partial(backward_kernel, (rows, slots), places),
         out_shape=(
             jax.ShapeDtypeStruct((count, width), f32),
             jax.ShapeDtypeStruct((LAYERS, EARLY, width), f32),
@@ -831,27 +851,27 @@
             VMEM((count, width), f32),
             VMEM((count, width), bf),
             VMEM((count, width), bf),
-            VMEM((count, width), f32),
             VMEM((3, count, width), bf),
             VMEM((3, count, width), bf),
             VMEM((2, count, width), f32),
             VMEM((2, count, 128), f32),
-            VMEM((2, count, WIDTH), bf),
-            VMEM((3, width, WIDTH), bf),
-            VMEM((2, blocks, WINDOW, 2 * BLOCK), bf),
+            VMEM((2, 2, count, WIDTH), bf),
+            VMEM((3, 2, width, WIDTH), bf),
+            VMEM((3, blocks, WINDOW, 2 * BLOCK), bf),
             VMEM((slots, 128), f32),
             VMEM((slots, 128), f32),
             VMEM((EARLY, 8, width), f32),
             VMEM((8, 8, width), f32),
             VMEM((LAYERS, steps + 1, EARLY, width), f32),
-            VMEM((LAYERS, steps, EARLY, width), f32),
+            VMEM((LAYERS, steps, 4, EARLY, width), f32),
             VMEM((steps + 1, 8, width), f32),
-            VMEM((steps, 8, width), f32),
-            DMA((3,)), DMA((2,)), DMA((2,)), DMA((2,)), DMA((2,)), DMA((3,)), DMA,
-            DMA((LAYERS, steps)), DMA((LAYERS, steps)), DMA((steps,)), DMA((steps,)),
+            VMEM((steps, 4, 8, width), f32),
+            DMA((3, 2)), DMA((3,)), DMA((2,)), DMA((2,)), DMA((2,)), DMA((3,)), DMA, DMA((4,)),
+            DMA((LAYERS, steps, 4)), DMA((LAYERS, steps, 4)), DMA((steps, 4)), DMA((steps, 4)),
         ],
         compiler_params=pltpu.CompilerParams(
-            vmem_limit_bytes=58 << 20, collective_id=1, has_side_effects=True
+            vmem_limit_bytes=60 << 20,
+            **({"collective_id": 1, "has_side_effects": True} if places else {}),
         ),
     )(lengths, wbuf, cotangent, gain_attn, gain_ffn, *saved)
 

time: 368 us -> 346 us (0.940)
  Pallas kernels: 362 us -> 340 us
    pallas_call x1, Pallas kernels: 137 us -> 115 us  [backward(): pl.pallas_call(functools.partial(backward_kernel, (rows, slots), places),...]
where the time goes in v5:
time: 346 us; the launch traced here: 345 us
  Pallas kernels  340 us (98%)
  local copies, waits for them, and re-layouts  4.96 us (1%)
    pallas_call x1, Pallas kernels, forward(): pl.pallas_call(functools.partial(forward_kernel, (rows, slots), devices_d...  223 us
    pallas_call x1, Pallas kernels, backward(): pl.pallas_call(functools.partial(backward_kernel, (rows, slots), places),...  115 us

profile of v5, /device:TPU:0, one launch (start us, length us, event | category | flops | bytes accessed | tf_op | source)
XLA Modules:
  0.0 345.3 jit_solution(2457343519949534892)
XLA Ops:
  0.6 222.9 %shard_map.241 = (bf16[48,4,2,2,2,32,512]{6,5,4,3,2,1,0:T(8,128)(2,1)}, bf16[1024,1024]{1,0:T(8,128)(2,1)}, bf16[2,3,1024,1024]{3,2,1,0:T(8,128)(2,1)}, bf16[2,1...) custom-call(s32[2,16]{1,0:T(2,128)} %lengths.3, ...), custom_call_target="tpu_custom_call" | custom-call | tf_op jit(solution)/shard_map/pallas_call | solution.py:492
  223.6 0.0 copy-start.1
  223.6 115.0 %shard_map.242 = (f32[1024,1024]{1,0:T(8,128)}, f32[2,8,1024]{2,1,0:T(8,128)}, f32[8,1024]{1,0:T(8,128)}) custom-call(s32[2,16]{1,0:T(2,128)} %lengths.3, bf16[48,1024,512]{2,1,0:T(8,128)(2,1)} %bitcast.5, bf16[1024,1024]{1,0:T(8,128)(2,1)} %bitcast.7, f32[2,1024]{1,0:T(2,128)} %gain_attn.1, f32[2,1024]{1,0:T(2,128)} %gain_ffn.1, ...), custom_call_target="tpu_custom_call" | custom-call | tf_op jit(solution)/shard_map/pallas_call | solution.py:841
  338.6 1.7 shard_map.243
  340.4 0.0 copy-start
  340.4 0.0 copy-done.1
  340.4 1.3 copy.29
  341.7 1.6 copy-done
  343.3 2.0 copy.30
Async XLA Ops:
  223.6 116.8 %copy-start.1 = (bf16[1024,1024]{1,0:T(8,128)(2,1)S(1)}, bf16[1024,1024]{1,0:T(8,128)(2,1)}, u32[]{:S(2)}) copy-start(bf16[1024,1024]{1,0:T(8,128)(2,1)} %get-tuple-element.26) | copy-start | bytes 6291460
  340.4 2.9 copy-start

commit v6 on v5

--- a/solution.py
+++ b/solution.py
@@ -39,7 +39,9 @@
 
 RELAY = 4
 ORDERS = (((0, 4, 2, 1, 3), (1, 0, 4, 2, 3)), ((0, 4, 1, 2, 3), (2, 0, 4, 1, 3)))
-SLOTS = 8
+STARTS = ((0, 2, 4, 6, 8, 10), (0, 2, 4, 6, 8, 10))
+DEPTH = 10
+SLOTS = 4
 
 
 class Gather:
@@ -53,19 +55,23 @@
         self.at = (chip // (n1 * n2), lax.rem(chip // n2, n1), lax.rem(chip, n2))
         self.step = (n1 * n2 * 2, n2 * 2, 2)
         self.relay = dims[0] == 4
-        self.orders = ORDERS
+        self.orders, self.starts = ORDERS, STARTS
         if not self.relay:
             self.orders = tuple(
                 tuple(tuple(d for d in order if d != RELAY) for order in pair) for pair in ORDERS
             )
+            self.starts = ((0, 2, 4, 6, 8), (0, 2, 4, 6, 8))
         self.phases = len(self.orders[0][0])
         rows, cols = own.shape[-2:]
-        if rows % 16 == 0:
-            half = rows // 2
-            self.parts = tuple((pl.ds(c * half, half), pl.ds(0, cols)) for c in range(2))
+        half = cols // 2
+        if rows % 32 == 0:
+            q = rows // 4
+            self.parts = (
+                ((pl.ds(0, q), pl.ds(0, cols)), (pl.ds(q, q), pl.ds(0, half))),
+                ((pl.ds(2 * q, 2 * q), pl.ds(0, cols)), (pl.ds(q, q), pl.ds(half, half))),
+            )
         else:
-            half = cols // 2
-            self.parts = tuple((pl.ds(0, rows), pl.ds(c * half, half)) for c in range(2))
+            self.parts = tuple(((pl.ds(0, rows), pl.ds(c * half, half)),) for c in range(2))
 
     def peers(self, dim):
         if dim == 3:
@@ -99,23 +105,21 @@
                     else (None, None)
                     for d in (1, 2, 3)
                 ]
-        sub = self.parts[s]
-        dst = self.buf.at[(g,) + tuple(where) + (self.core,) + sub]
-        src = self.own.at[(g,) + sub] if p == 0 else dst
-        return [
-            (
-                pltpu.make_async_remote_copy(
+        out = []
+        for n, sub in enumerate(self.parts[s]):
+            dst = self.buf.at[(g,) + tuple(where) + (self.core,) + sub]
+            src = self.own.at[(g,) + sub] if p == 0 else dst
+            for i, (to, guard) in enumerate(zip(targets, guards)):
+                copy = pltpu.make_async_remote_copy(
                     src_ref=src,
                     dst_ref=dst,
-                    send_sem=self.ssem.at[slot, s, first + i],
-                    recv_sem=self.rsem.at[slot, s, first + i],
+                    send_sem=self.ssem.at[slot, s, n, first + i],
+                    recv_sem=self.rsem.at[slot, s, n, first + i],
                     device_id=(to,),
                     device_id_type=MESH,
-                ),
-                *guard,
-            )
-            for i, (to, guard) in enumerate(zip(targets, guards))
-        ]
+                )
+                out.append((copy, *guard))
+        return out
 
     def greet(self):
         bar = pltpu.get_barrier_semaphore()
@@ -126,23 +130,23 @@
     def meet(self):
         pl.semaphore_wait(pltpu.get_barrier_semaphore(), sum(self.dims) - 3 + 1)
 
-    def pump(self, pair_step, par):
+    def pump(self, step, par):
         for p in range(self.phases, -1, -1):
-            pair = pair_step - p
-
-            @pl.when((pair >= 0) & (pair < self.total // 2))
-            def _():
-                g = 2 * pair + par
-                for s in range(2):
+            for s in range(2):
+                g = step - self.starts[s][p]
+                kind = (par - self.starts[s][p]) % 2
+
+                @pl.when((g >= 0) & (g < self.total))
+                def _():
                     if p > 0:
-                        for copy, sends, receives in self.moves(g, par, s, p - 1):
+                        for copy, sends, receives in self.moves(g, kind, s, p - 1):
                             if sends is None:
                                 copy.wait()
                             else:
                                 pl.when(sends)(copy.wait_send)
                                 pl.when(receives)(copy.wait_recv)
                     if p < self.phases:
-                        for copy, sends, _ in self.moves(g, par, s, p):
+                        for copy, sends, _ in self.moves(g, kind, s, p):
                             if sends is None:
                                 copy.start()
                             else:
@@ -229,15 +233,27 @@
     return jnp.where(number < segments - 1, number, PADDING_ID + position)
 
 
+def fold(x):
+    rows, width = x.shape
+    return jnp.sum(x.reshape(rows // 8, 8, width), axis=0)
+
+
+def norm_back(up, xhat, scale, gain_row):
+    scaled = up * gain_row
+    m1 = jnp.mean(scaled, axis=1, keepdims=True)
+    m2 = jnp.mean(scaled * xhat, axis=1, keepdims=True)
+    return scale * (scaled - m1 - xhat * m2)
+
+
 def forward_kernel(
     dims, devices_dims,
-    lengths, w_query, w_key, w_value, w_out, w_inner, w_outer, tokens, *rest,
+    lengths, w_query, w_key, w_value, w_out, w_inner, w_outer, tokens, cotangent, *rest,
 ):
     vectors, rest = rest[:8], rest[8:]
     (
-        inner_raw, wbuf, out, saved_qkv, saved_p, saved_x, saved_s, saved_d,
-        h, a, qkv, o, z, u, w, p_stage, d_stage, x_stage, s_stage, own, id_row, id_col, inner_bias,
-        wsem, psem, dsem, xsem, ssem, qsem, tsem, hsem, send_sem, recv_sem,
+        inner_raw, wbuf, out, first_sums, saved_f, saved_qkv, saved_p, saved_x, saved_s, saved_d,
+        h, a, qkv, o, z, u, w, p_stage, d_stage, x_stage, s_stage, own, id_row, id_col, inner_bias, cot,
+        wsem, psem, dsem, xsem, ssem, qsem, tsem, hsem, csem, send_sem, recv_sem,
     ) = rest
     rows, slots = dims
     count = h.shape[0]
@@ -262,11 +278,13 @@
 
             @pl.when(lax.rem(half, 2) == par)
             def _():
-                gather.pump(half // 2 + gather.phases, par)
+                gather.pump(half + DEPTH, par)
 
     gather.greet()
     load = pltpu.make_async_copy(tokens, a, tsem)
     load.start()
+    load_cot = pltpu.make_async_copy(cotangent, cot, csem)
+    load_cot.start()
     unit = own.shape[1]
 
     def cast(l, m):
@@ -274,17 +292,26 @@
         for c in range(2):
             own[l * GROUPS + 2 * m + c] = matrix[l, :, tile(c, WIDTH)].astype(jnp.bfloat16)
 
+    def here(first, count):
+        blocks = pl.ds(first, count)
+        return pltpu.make_async_copy(
+            own.at[blocks], wbuf.at[(blocks,) + gather.at + (gather.core,)], hsem
+        )
+
     def start(i):
-        for par in range(2):
-            gather.pump(i, par)
-
-    cast(0, 0)
+        gather.pump(i, i % 2)
+
+    for m in range(4):
+        cast(0, m)
+    here(0, AT_INNER).start()
     gather.meet()
     start(0)
+    here(0, AT_INNER).wait()
+    start(1)
     for l in range(LAYERS):
         at = l * GROUPS
         for m in range(4):
-            if (l, m) != (0, 0):
+            if l > 0:
                 cast(l, m)
         for c in range(2):
             for kc in range(4):
@@ -296,12 +323,11 @@
             unit,
             w_inner.shape[2],
         )
-    here = pltpu.make_async_copy(
-        own, wbuf.at[(pl.ds(0, total),) + gather.at + (gather.core,)], hsem
-    )
-    here.start()
-    here.wait()
-    start(1)
+        if l == 0:
+            start(2)
+    here(AT_INNER, total - AT_INNER).start()
+    start(3)
+    here(AT_INNER, total - AT_INNER).wait()
 
     def keep_bias(b, x):
         inner_bias[:, b * 128 : (b + 1) * 128] = x
@@ -312,6 +338,8 @@
     for r in range(rows):
         id_row[r] = slot_ids(lengths, r, lax.broadcasted_iota(jnp.int32, (8, slots), 1))
         id_col[r] = slot_ids(lengths, r, lax.broadcasted_iota(jnp.int32, (slots, 128), 0))
+    first_sums[...] = jnp.zeros_like(first_sums)
+    load_cot.wait()
     load.wait()
 
     def widen(i):
@@ -319,7 +347,7 @@
 
     loop(count // ROW_TILE, widen)
 
-    for i in range(2, gather.phases):
+    for i in range(4, DEPTH):
         start(i)
     pump(0)
     wload(0).start()
@@ -350,6 +378,22 @@
             y = xhat * vectors[gain][pl.ds(l, 1), :] + vectors[shift][pl.ds(l, 1), :]
             h[t, :] = y
             a[t, :] = y.astype(jnp.bfloat16)
+            if which == 1:
+
+                @pl.when(l == LAYERS - 1)
+                def _():
+                    r = i // (slots // ROW_TILE)
+                    real = slots - lengths[r, lengths.shape[1] - 1]
+                    slot = lax.rem(i * ROW_TILE, slots) + lax.broadcasted_iota(
+                        jnp.int32, (ROW_TILE, h.shape[1]), 0
+                    )
+                    up = jnp.where(slot < real, cot[t, :].astype(jnp.float32), 0.0)
+                    down = norm_back(up, xhat, scale, vectors[gain][pl.ds(l, 1), :])
+                    x_stage[t, :] = down
+                    low = down.astype(jnp.bfloat16)
+                    cot[t, :] = low
+                    first_sums[0] += fold(up)
+                    first_sums[1] += fold(low.astype(jnp.float32))
 
         loop(count // ROW_TILE, body)
         store_x.start()
@@ -423,9 +467,9 @@
         normalize(l, 0)
 
         def inner(i):
-            @pl.when(lax.rem(i, 4) < 3)
+            @pl.when(lax.rem(i, 3) < 2)
             def _():
-                pump(base + 15 + i - i // 4)
+                pump(base + 15 + i - i // 3)
 
             cols = tile(i, WIDTH)
             u[...] = matmul(a[...], weights(base + AT_INNER + i)) + inner_bias[pl.ds(l, 1), cols]
@@ -467,6 +511,8 @@
     loop(LAYERS, layer)
     store = pltpu.make_async_copy(a, out, tsem)
     store.start()
+    store_f = pltpu.make_async_copy(cot, saved_f, csem)
+    store_f.start()
     last = LAYERS - 1
     for m in range(3):
         pltpu.make_async_copy(qkv.at[m], saved_qkv.at[last, m], qsem.at[m]).wait()
@@ -476,9 +522,10 @@
     pltpu.make_async_copy(x_stage, saved_x.at[last, 1], xsem).wait()
     pltpu.make_async_copy(s_stage, saved_s.at[last, 1], ssem).wait()
     store.wait()
-
-
-def forward(devices, lengths, matrices, tokens, vectors, inner_bias, rows, slots):
+    store_f.wait()
+
+
+def forward(devices, lengths, matrices, tokens, cotangent, vectors, inner_bias, rows, slots):
     count, width = tokens.shape
     hidden = inner_bias.shape[-1]
     unit = matrices[0].shape[1]
@@ -494,14 +541,16 @@
         out_shape=(
             jax.ShapeDtypeStruct((LAYERS * GROUPS,) + held, bf),
             jax.ShapeDtypeStruct((count, width), bf),
+            jax.ShapeDtypeStruct((2, 8, width), f32),
+            jax.ShapeDtypeStruct((count, width), bf),
             jax.ShapeDtypeStruct((LAYERS, 3, count, width), bf),
             jax.ShapeDtypeStruct((LAYERS, rows * HEADS // 2, blocks, WINDOW, 2 * BLOCK), bf),
             jax.ShapeDtypeStruct((LAYERS, 2, count, width), f32),
             jax.ShapeDtypeStruct((LAYERS, 2, count, 128), f32),
             jax.ShapeDtypeStruct((LAYERS, hidden // WIDTH, count, WIDTH), bf),
         ),
-        in_specs=[pl.BlockSpec(memory_space=pltpu.SMEM)] + [vm] * 6 + [any_] + [vm] * 9,
-        out_specs=(any_,) * 7,
+        in_specs=[pl.BlockSpec(memory_space=pltpu.SMEM)] + [vm] * 6 + [any_] * 2 + [vm] * 9,
+        out_specs=(any_, any_, vm) + (any_,) * 6,
         scratch_shapes=[
             VMEM((count, width), f32),
             VMEM((count, width), bf),
@@ -518,13 +567,14 @@
             VMEM((rows, 8, slots), jnp.int32),
             VMEM((rows, slots, 128), jnp.int32),
             VMEM((LAYERS, hidden), f32),
-            DMA((2,)), DMA((2,)), DMA((2,)), DMA, DMA, DMA((3,)), DMA, DMA,
-            DMA((SLOTS, 2, sems)), DMA((SLOTS, 2, sems)),
+            VMEM((count, width), bf),
+            DMA((2,)), DMA((2,)), DMA((2,)), DMA, DMA, DMA((3,)), DMA, DMA, DMA,
+            DMA((SLOTS, 2, 2, sems)), DMA((SLOTS, 2, 2, sems)),
         ],
         compiler_params=pltpu.CompilerParams(
             vmem_limit_bytes=58 << 20, collective_id=0, has_side_effects=True
         ),
-    )(lengths, *matrices, tokens, *vectors, inner_bias)
+    )(lengths, *matrices, tokens, cotangent, *vectors, inner_bias)
 
 
 def digits(devices):
@@ -574,14 +624,9 @@
                 c.start()
 
 
-def fold(x):
-    rows, width = x.shape
-    return jnp.sum(x.reshape(rows // 8, 8, width), axis=0)
-
-
 def backward_kernel(
     dims, places,
-    lengths, wbuf, cotangent, gain_attn, gain_ffn, saved_qkv, saved_p, saved_x, saved_s, saved_d,
+    wbuf, gain_attn, gain_ffn, first_sums, saved_f, saved_qkv, saved_p, saved_x, saved_s, saved_d,
     grad, sums, late_sums,
     g, db, du, qkv, dqkv, x, sc, d, w, p, dk, dv, part, late,
     held, got, late_held, late_got,
@@ -641,16 +686,22 @@
         return [pltpu.make_async_copy(saved_qkv.at[l, m], qkv.at[m], qsem.at[m]) for m in range(3)]
 
     top_layer = LAYERS - 1
-    first = pltpu.make_async_copy(cotangent, db, csem)
-    first.start()
-    for c in xload(top_layer, 1):
+    opening = [
+        pltpu.make_async_copy(saved_f, db, csem.at[0]),
+        pltpu.make_async_copy(saved_x.at[top_layer, 1], g, csem.at[1]),
+    ]
+    opening[0].start()
+    for c in wload(0):
         c.start()
-    for i in range(2):
-        for c in wload(i):
-            c.start()
     dload(top_layer, 0).start()
+    for c in wload(1):
+        c.start()
+    opening[1].start()
     for c in xload(top_layer, 0):
         c.start()
+    if top_layer:
+        for c in xload(top_layer - 1, 1):
+            c.start()
     me = lax.axis_index("dp")
     if steps:
         barrier = pltpu.get_barrier_semaphore()
@@ -659,16 +710,10 @@
             for k in range(1, size):
                 to = me + (lax.rem(digit + k, size) - digit) * stride
                 pl.semaphore_signal(barrier, inc=1, device_id=(to,), device_id_type=MESH)
-    first.wait()
-    for r in range(rows):
-        real = slots - lengths[r, lengths.shape[1] - 1]
-
-        def widen(i):
-            t = pl.ds(pl.multiple_of(r * slots + i * ROW_TILE, ROW_TILE), ROW_TILE)
-            slot = i * ROW_TILE + lax.broadcasted_iota(jnp.int32, (ROW_TILE, width), 0)
-            g[t, :] = jnp.where(slot < real, db[t, :].astype(jnp.float32), 0.0)
-
-        loop(slots // ROW_TILE, widen)
+    for c in opening:
+        c.wait()
+    part[D_FFN] = first_sums[0]
+    part[D_OUTER] = first_sums[1]
     if steps:
         pl.semaphore_wait(barrier, sum(size - 1 for _, size in places))
 
@@ -683,10 +728,7 @@
             t = tile(i, ROW_TILE)
             up = g[t, :]
             xh = x[which, t, :]
-            scaled = up * gain[pl.ds(l, 1), :]
-            m1 = jnp.mean(scaled, axis=1, keepdims=True)
-            m2 = jnp.mean(scaled * xh, axis=1, keepdims=True)
-            down = sc[which, t, :1] * (scaled - m1 - xh * m2)
+            down = norm_back(up, xh, sc[which, t, :1], gain[pl.ds(l, 1), :])
             g[t, :] = down
             low = down.astype(jnp.bfloat16)
             db[t, :] = low
@@ -707,7 +749,10 @@
     def layer(step):
         l = top_layer - step
         base = step * per_layer
-        normalize_back(l, 1)
+
+        @pl.when(step > 0)
+        def _():
+            normalize_back(l, 1)
 
         def quarter(kc):
             @pl.when(kc + 1 < 4)
@@ -830,8 +875,8 @@
         pltpu.make_async_copy(g.at[:, n], grad.at[:, n], gsem.at[c]).wait()
 
 
-def backward(devices, lengths, wbuf, cotangent, gain_attn, gain_ffn, saved, rows, slots):
-    count, width = cotangent.shape
+def backward(devices, wbuf, gain_attn, gain_ffn, first_sums, saved, rows, slots):
+    count, width = saved[0].shape
     bf, f32 = jnp.bfloat16, jnp.float32
     blocks = slots // BLOCK
     places = digits(devices)
@@ -845,7 +890,7 @@
             jax.ShapeDtypeStruct((LAYERS, EARLY, width), f32),
             jax.ShapeDtypeStruct((8, width), f32),
         ),
-        in_specs=[pl.BlockSpec(memory_space=pltpu.SMEM), any_, any_, vm, vm] + [any_] * 5,
+        in_specs=[any_, vm, vm, vm] + [any_] * 6,
         out_specs=(any_, vm, vm),
         scratch_shapes=[
             VMEM((count, width), f32),
@@ -866,14 +911,14 @@
             VMEM((LAYERS, steps, 4, EARLY, width), f32),
             VMEM((steps + 1, 8, width), f32),
             VMEM((steps, 4, 8, width), f32),
-            DMA((3, 2)), DMA((3,)), DMA((2,)), DMA((2,)), DMA((2,)), DMA((3,)), DMA, DMA((4,)),
+            DMA((3, 2)), DMA((3,)), DMA((2,)), DMA((2,)), DMA((2,)), DMA((3,)), DMA((2,)), DMA((4,)),
             DMA((LAYERS, steps, 4)), DMA((LAYERS, steps, 4)), DMA((steps, 4)), DMA((steps, 4)),
         ],
         compiler_params=pltpu.CompilerParams(
             vmem_limit_bytes=60 << 20,
             **({"collective_id": 1, "has_side_effects": True} if places else {}),
         ),
-    )(lengths, wbuf, cotangent, gain_attn, gain_ffn, *saved)
+    )(wbuf, gain_attn, gain_ffn, first_sums, *saved)
 
 
 def finish_kernel(unit, sums, late, query, value, out, inner, outer, attn, ffn):
@@ -945,12 +990,13 @@
         bias_query, bias_value, bias_out, bias_outer, shift_attn, shift_ffn, gain_attn, gain_ffn,
     )
     matrices = (w_query, w_key, w_value, w_out, w_inner, w_outer)
-    wbuf, out, *saved = forward(
-        devices, lengths, matrices, tokens.reshape(count, width), vectors, bias_inner, rows, slots
+    wbuf, out, first_sums, *saved = forward(
+        devices, lengths, matrices, tokens.reshape(count, width), cotangent.reshape(count, width),
+        vectors, bias_inner, rows, slots,
     )
     wbuf = wbuf.reshape(LAYERS * GROUPS, width, WIDTH)
     grad, sums, late = backward(
-        devices, lengths, wbuf, cotangent.reshape(count, width), gain_attn, gain_ffn, saved, rows, slots
+        devices, wbuf, gain_attn, gain_ffn, first_sums, saved, rows, slots
     )
     return (
         out.reshape(rows, slots, width),

time: 346 us -> 344 us (level)
  no operation moved by 1% of the time
where the time goes in v6:
time: 344 us
  Pallas kernels  338 us (98%)
  local copies, waits for them, and re-layouts  4.96 us (1%)
    pallas_call x1, Pallas kernels, forward(): pl.pallas_call(functools.partial(forward_kernel, (rows, slots), devices_d...  221 us
    pallas_call x1, Pallas kernels, backward(): pl.pallas_call(functools.partial(backward_kernel, (rows, slots), places),...  115 us

profile of v6, /device:TPU:0, one launch (start us, length us, event | category | flops | bytes accessed | tf_op | source)
XLA Modules:
  0.0 343.8 jit_solution(7466424375977692817)
XLA Ops:
  0.6 221.5 %shard_map.241 = (bf16[48,4,2,2,2,32,512]{6,5,4,3,2,1,0:T(8,128)(2,1)}, bf16[1024,1024]{1,0:T(8,128)(2,1)}, f32[2,8,1024]{2,1,0:T(8,128)}, bf16[1024,1024]{1,0:T...) custom-call(s32[2,16]{1,0:T(2,128)} %lengths.1, ...), custom_call_target="tpu_custom_call" | custom-call | tf_op jit(solution)/shard_map/pallas_call | solution.py:539
  222.1 0.0 copy-start.1
  222.1 115.0 %shard_map.242 = (f32[1024,1024]{1,0:T(8,128)}, f32[2,8,1024]{2,1,0:T(8,128)}, f32[8,1024]{1,0:T(8,128)}) custom-call(bf16[48,1024,512]{2,1,0:T(8,128)(2,1)} %bitcast.5, f32[2,1024]{1,0:T(2,128)} %gain_attn.1, f32[2,1024]{1,0:T(2,128)} %gain_ffn.1, f32[2,8,1024]{2,1,0:T(8,128)} %get-tuple-element.30.first_sums, ...), custom_call_target="tpu_custom_call" | custom-call | tf_op jit(solution)/shard_map/pallas_call | solution.py:886
  337.1 1.7 shard_map.243
  338.8 0.0 copy-start
  338.8 0.0 copy-done.1
  338.8 1.3 copy.29
  340.2 1.6 copy-done
  341.8 2.0 copy.30
Async XLA Ops:
  222.1 116.7 %copy-start.1 = (bf16[1024,1024]{1,0:T(8,128)(2,1)S(1)}, bf16[1024,1024]{1,0:T(8,128)(2,1)}, u32[]{:S(2)}) copy-start(bf16[1024,1024]{1,0:T(8,128)(2,1)} %get-tuple-element.28) | copy-start | bytes 6291460
  338.8 2.9 copy-start

commit v7 on v6

--- a/solution.py
+++ b/solution.py
@@ -38,9 +38,9 @@
 
 
 RELAY = 4
-ORDERS = (((0, 4, 2, 1, 3), (1, 0, 4, 2, 3)), ((0, 4, 1, 2, 3), (2, 0, 4, 1, 3)))
-STARTS = ((0, 2, 4, 6, 8, 10), (0, 2, 4, 6, 8, 10))
-DEPTH = 10
+ORDERS = ((0, 4, 2, 1, 3), (0, 4, 1, 2, 3), (1, 0, 4, 2, 3), (2, 0, 4, 1, 3))
+STARTS = (0, 2, 4, 6, 8, 9)
+DEPTH = STARTS[-1]
 SLOTS = 4
 
 
@@ -55,23 +55,21 @@
         self.at = (chip // (n1 * n2), lax.rem(chip // n2, n1), lax.rem(chip, n2))
         self.step = (n1 * n2 * 2, n2 * 2, 2)
         self.relay = dims[0] == 4
-        self.orders, self.starts = ORDERS, STARTS
+        self.orders = ORDERS
         if not self.relay:
-            self.orders = tuple(
-                tuple(tuple(d for d in order if d != RELAY) for order in pair) for pair in ORDERS
-            )
-            self.starts = ((0, 2, 4, 6, 8), (0, 2, 4, 6, 8))
-        self.phases = len(self.orders[0][0])
+            self.orders = tuple(tuple(d for d in order if d != RELAY) for order in ORDERS)
+        self.phases = len(self.orders[0])
         rows, cols = own.shape[-2:]
-        half = cols // 2
+        q, c = rows // 4, cols // 4
         if rows % 32 == 0:
-            q = rows // 4
             self.parts = (
-                ((pl.ds(0, q), pl.ds(0, cols)), (pl.ds(q, q), pl.ds(0, half))),
-                ((pl.ds(2 * q, 2 * q), pl.ds(0, cols)), (pl.ds(q, q), pl.ds(half, half))),
+                ((pl.ds(0, q), pl.ds(0, 3 * c)),),
+                ((pl.ds(q, q), pl.ds(0, 3 * c)),),
+                ((pl.ds(2 * q, q), pl.ds(0, cols)), (pl.ds(0, q), pl.ds(3 * c, c))),
+                ((pl.ds(3 * q, q), pl.ds(0, cols)), (pl.ds(q, q), pl.ds(3 * c, c))),
             )
         else:
-            self.parts = tuple(((pl.ds(0, rows), pl.ds(c * half, half)),) for c in range(2))
+            self.parts = tuple(((pl.ds(0, rows), pl.ds(n * c, c)),) for n in range(4))
 
     def peers(self, dim):
         if dim == 3:
@@ -82,8 +80,8 @@
             out.append(self.me + (to - self.at[dim]) * self.step[dim])
         return out
 
-    def moves(self, g, par, s, p):
-        order = self.orders[par][s]
+    def moves(self, g, s, p):
+        order = self.orders[s]
         dim, full = order[p], order[:p]
         n0, n1, n2 = self.dims
         first = (0, n0, n0 + n1 - 1, n0 + n1 + n2 - 2, n0 - 1)[dim]
@@ -106,15 +104,15 @@
                     for d in (1, 2, 3)
                 ]
         out = []
-        for n, sub in enumerate(self.parts[s]):
+        for n, sub in enumerate(self.parts[s], sum(len(part) for part in self.parts[:s])):
             dst = self.buf.at[(g,) + tuple(where) + (self.core,) + sub]
             src = self.own.at[(g,) + sub] if p == 0 else dst
             for i, (to, guard) in enumerate(zip(targets, guards)):
                 copy = pltpu.make_async_remote_copy(
                     src_ref=src,
                     dst_ref=dst,
-                    send_sem=self.ssem.at[slot, s, n, first + i],
-                    recv_sem=self.rsem.at[slot, s, n, first + i],
+                    send_sem=self.ssem.at[slot, n, first + i],
+                    recv_sem=self.rsem.at[slot, n, first + i],
                     device_id=(to,),
                     device_id_type=MESH,
                 )
@@ -130,23 +128,22 @@
     def meet(self):
         pl.semaphore_wait(pltpu.get_barrier_semaphore(), sum(self.dims) - 3 + 1)
 
-    def pump(self, step, par):
+    def pump(self, step):
         for p in range(self.phases, -1, -1):
-            for s in range(2):
-                g = step - self.starts[s][p]
-                kind = (par - self.starts[s][p]) % 2
-
-                @pl.when((g >= 0) & (g < self.total))
-                def _():
+            g = step - (DEPTH if p == self.phases else STARTS[p])
+
+            @pl.when((g >= 0) & (g < self.total))
+            def _():
+                for s in range(len(self.orders)):
                     if p > 0:
-                        for copy, sends, receives in self.moves(g, kind, s, p - 1):
+                        for copy, sends, receives in self.moves(g, s, p - 1):
                             if sends is None:
                                 copy.wait()
                             else:
                                 pl.when(sends)(copy.wait_send)
                                 pl.when(receives)(copy.wait_recv)
                     if p < self.phases:
-                        for copy, sends, _ in self.moves(g, kind, s, p):
+                        for copy, sends, _ in self.moves(g, s, p):
                             if sends is None:
                                 copy.start()
                             else:
@@ -274,11 +271,7 @@
         return w[lax.rem(g, 2)].reshape(h.shape[1], WIDTH)
 
     def pump(half):
-        for par in range(2):
-
-            @pl.when(lax.rem(half, 2) == par)
-            def _():
-                gather.pump(half + DEPTH, par)
+        gather.pump(half + DEPTH)
 
     gather.greet()
     load = pltpu.make_async_copy(tokens, a, tsem)
@@ -299,7 +292,7 @@
         )
 
     def start(i):
-        gather.pump(i, i % 2)
+        gather.pump(i)
 
     for m in range(4):
         cast(0, m)
@@ -423,9 +416,10 @@
             pltpu.make_async_copy(qkv.at[m], saved_qkv.at[l, m], qsem.at[m]).start()
 
         def attend(i):
-            @pl.when(lax.rem(i, 3) == 0)
-            def _():
-                pump(base + 7 + i // 3)
+            @pl.when(lax.rem(i, 4) == 0)
+            def _():
+                pump(base + 7 + i // 4)
+
 
             r = i // pairs
             lanes = tile(lax.rem(i, pairs), 128)
@@ -459,7 +453,10 @@
         loop(rows * pairs, attend)
 
         def attn_out(i):
-            pump(base + 13 + i)
+            @pl.when(i == 1)
+            def _():
+                pump(base + 11)
+
             cols = tile(i, WIDTH)
             h[:, cols] += matmul(o[...], weights(base + AT_OUT + i))
 
@@ -467,9 +464,8 @@
         normalize(l, 0)
 
         def inner(i):
-            @pl.when(lax.rem(i, 3) < 2)
-            def _():
-                pump(base + 15 + i - i // 3)
+            pump(base + 12 + i)
+
 
             cols = tile(i, WIDTH)
             u[...] = matmul(a[...], weights(base + AT_INNER + i)) + inner_bias[pl.ds(l, 1), cols]
@@ -494,13 +490,26 @@
         loop(8, inner)
 
         def outer(i):
-            @pl.when((lax.rem(i, 2) == 0) & (i > 0))
-            def _():
-                pump(base + 20 + i // 2)
+            @pl.when(i == 0)
+            def _():
+                pump(base + 20)
+
+            @pl.when(i == 1)
+            def _():
+                pump(base + 21)
+
+            @pl.when(i == 3)
+            def _():
+                pump(base + 22)
+
+            @pl.when(i == 5)
+            def _():
+                pump(base + 23)
 
             @pl.when(i == 7)
             def _():
                 pump(base + 24)
+
 
             cols = tile(i // 4, WIDTH)
             h[:, cols] += matmul(z[lax.rem(i, 4)], weights(base + AT_OUTER + i))
@@ -569,7 +578,7 @@
             VMEM((LAYERS, hidden), f32),
             VMEM((count, width), bf),
             DMA((2,)), DMA((2,)), DMA((2,)), DMA, DMA, DMA((3,)), DMA, DMA, DMA,
-            DMA((SLOTS, 2, 2, sems)), DMA((SLOTS, 2, 2, sems)),
+            DMA((SLOTS, 6, sems)), DMA((SLOTS, 6, sems)),
         ],
         compiler_params=pltpu.CompilerParams(
             vmem_limit_bytes=58 << 20, collective_id=0, has_side_effects=True
@@ -797,7 +806,7 @@
         def attend(i):
             for k in range(1, steps + 1):
 
-                @pl.when(i == 3 * k)
+                @pl.when(i == (items - 1) // steps * k)
                 def _():
                     early.step(k)
 
@@ -921,8 +930,24 @@
     )(wbuf, gain_attn, gain_ffn, first_sums, *saved)
 
 
-def finish_kernel(unit, sums, late, query, value, out, inner, outer, attn, ffn):
-    width = sums.shape[2]
+def finish_kernel(
+    unit,
+    sums, late, grad_in, result_in,
+    grad, result, query, value, out, inner, outer, attn, ffn,
+    grad_hold, result_hold, load_sem, store_sem,
+):
+    count, width = grad.shape
+    part = count // 4
+    moves = []
+    for c in range(4):
+        for n, (source, hold, target) in enumerate(
+            ((result_in, result_hold, result), (grad_in, grad_hold, grad))
+        ):
+            rows_ = pl.ds(c * part, part)
+            load = pltpu.make_async_copy(source.at[rows_], hold.at[rows_], load_sem.at[n, c])
+            store = pltpu.make_async_copy(hold.at[rows_], target.at[rows_], store_sem.at[n, c])
+            load.start()
+            moves.append((load, store))
     devices = width // unit
     for l in range(LAYERS):
         here = slice(l, l + 1)
@@ -947,18 +972,31 @@
                     lane = lax.broadcasted_iota(jnp.int32, x.shape, 1)
                     block = jnp.where(lane >= piece * unit, x, block)
             inner[here, b * 128 : (b + 1) * 128] = block
-
-
-def finish(unit, hidden, sums, late):
+    for load, store in moves:
+        load.wait()
+        store.start()
+    for _, store in moves:
+        store.wait()
+
+
+def finish(unit, hidden, sums, late, grad, result):
     width = sums.shape[2]
     vm = pl.BlockSpec(memory_space=VMEM)
+    any_ = pl.BlockSpec(memory_space=HBM)
     sizes = (width, width, width, hidden, width, width, width)
+    large = tuple(jax.ShapeDtypeStruct(x.shape, x.dtype) for x in (grad, result))
     return pl.pallas_call(
         functools.partial(finish_kernel, unit),
-        out_shape=tuple(jax.ShapeDtypeStruct((LAYERS, n), jnp.float32) for n in sizes),
-        in_specs=[vm, vm],
-        out_specs=(vm,) * 7,
-    )(sums, late)
+        out_shape=large + tuple(jax.ShapeDtypeStruct((LAYERS, n), jnp.float32) for n in sizes),
+        in_specs=[vm, vm, any_, any_],
+        out_specs=(any_, any_) + (vm,) * 7,
+        scratch_shapes=[
+            VMEM(grad.shape, grad.dtype),
+            VMEM(result.shape, result.dtype),
+            DMA((2, 4)),
+            DMA((2, 4)),
+        ],
+    )(sums, late, grad, result)
 
 
 def per_device(
@@ -998,11 +1036,8 @@
     grad, sums, late = backward(
         devices, wbuf, gain_attn, gain_ffn, first_sums, saved, rows, slots
     )
-    return (
-        out.reshape(rows, slots, width),
-        grad.reshape(rows, slots, width),
-        *finish(unit, hidden, sums, late),
-    )
+    grad, out, *small = finish(unit, hidden, sums, late, grad, out)
+    return (out.reshape(rows, slots, width), grad.reshape(rows, slots, width), *small)
 
 
 def solution(mesh):

time: 344 us -> 335 us (0.974)
  local copies, waits for them, and re-layouts: 4.96 us -> 0 us
  Pallas kernels: 338 us -> 334 us
    pallas_call x1, Pallas kernels: 1.73 us -> 7.08 us  [finish(): pl.pallas_call(functools.partial(finish_kernel, unit), out_shape=large +...]
    pallas_call x1, Pallas kernels: 221 us -> 216 us  [forward(): pl.pallas_call(functools.partial(forward_kernel, (rows, slots), devices_d...]
    unnamed x6 -> x0, local copies, waits for them, and re-layouts: 4.96 us -> none
    pallas_call x1, Pallas kernels: 115 us -> 110 us  [backward(): pl.pallas_call(functools.partial(backward_kernel, (rows, slots), places),...]
where the time goes in v7:
time: 335 us; the launch traced here: 334 us
  Pallas kernels  334 us (100%)
    pallas_call x1, Pallas kernels, forward(): pl.pallas_call(functools.partial(forward_kernel, (rows, slots), devices_d...  216 us
    pallas_call x1, Pallas kernels, backward(): pl.pallas_call(functools.partial(backward_kernel, (rows, slots), places),...  110 us
    pallas_call x1, Pallas kernels, finish(): pl.pallas_call(functools.partial(finish_kernel, unit), out_shape=large +...  7.08 us

profile of v7, /device:TPU:0, one launch (start us, length us, event | category | flops | bytes accessed | tf_op | source)
XLA Modules:
  0.0 334.4 jit_solution(10836760555653616420)
XLA Ops:
  0.6 216.3 %shard_map.241 = (bf16[48,4,2,2,2,32,512]{6,5,4,3,2,1,0:T(8,128)(2,1)}, bf16[1024,1024]{1,0:T(8,128)(2,1)}, f32[2,8,1024]{2,1,0:T(8,128)}, bf16[1024,1024]{1,0:T...) custom-call(s32[2,16]{1,0:T(2,128)} %lengths.1, ...), custom_call_target="tpu_custom_call" | custom-call | tf_op jit(solution)/shard_map/pallas_call | solution.py:548
  217.0 110.1 %shard_map.242 = (f32[1024,1024]{1,0:T(8,128)}, f32[2,8,1024]{2,1,0:T(8,128)}, f32[8,1024]{1,0:T(8,128)}) custom-call(bf16[48,1024,512]{2,1,0:T(8,128)(2,1)} %bitcast.5, f32[2,1024]{1,0:T(2,128)} %gain_attn.1, f32[2,1024]{1,0:T(2,128)} %gain_ffn.1, f32[2,8,1024]{2,1,0:T(8,128)} %get-tuple-element.31.first_sums, ...), custom_call_target="tpu_custom_call" | custom-call | tf_op jit(solution)/shard_map/pallas_call | solution.py:895
  327.1 7.1 %shard_map.243 = (f32[1024,1024]{1,0:T(8,128)}, bf16[1024,1024]{1,0:T(8,128)(2,1)}, f32[2,1024]{1,0:T(2,128)}, f32[2,1024]{1,0:T(2,128)}, f32[2,1024]{1,0:T(2,12...) custom-call(f32[2,8,1024]{2,1,0:T(8,128)} %get-tuple-element.38.sums, ...), custom_call_target="tpu_custom_call" | custom-call | tf_op jit(solution)/shard_map/pallas_call | solution.py:988

commit v8 on v7

--- a/solution.py
+++ b/solution.py
@@ -416,7 +416,7 @@
             pltpu.make_async_copy(qkv.at[m], saved_qkv.at[l, m], qsem.at[m]).start()
 
         def attend(i):
-            @pl.when(lax.rem(i, 4) == 0)
+            @pl.when(lax.rem(i, 4) == 2)
             def _():
                 pump(base + 7 + i // 4)
 
@@ -948,6 +948,9 @@
             store = pltpu.make_async_copy(hold.at[rows_], target.at[rows_], store_sem.at[n, c])
             load.start()
             moves.append((load, store))
+    for load, store in moves:
+        load.wait()
+        store.start()
     devices = width // unit
     for l in range(LAYERS):
         here = slice(l, l + 1)
@@ -972,9 +975,6 @@
                     lane = lax.broadcasted_iota(jnp.int32, x.shape, 1)
                     block = jnp.where(lane >= piece * unit, x, block)
             inner[here, b * 128 : (b + 1) * 128] = block
-    for load, store in moves:
-        load.wait()
-        store.start()
     for _, store in moves:
         store.wait()
 

time: 335 us -> 333 us (level)
  no operation moved by 1% of the time
where the time goes in v8:
time: 333 us
  Pallas kernels  332 us (100%)
    pallas_call x1, Pallas kernels, forward(): pl.pallas_call(functools.partial(forward_kernel, (rows, slots), devices_d...  214 us
    pallas_call x1, Pallas kernels, backward(): pl.pallas_call(functools.partial(backward_kernel, (rows, slots), places),...  110 us
    pallas_call x1, Pallas kernels, finish(): pl.pallas_call(functools.partial(finish_kernel, unit), out_shape=large +...  7.13 us

profile of v8, /device:TPU:0, one launch (start us, length us, event | category | flops | bytes accessed | tf_op | source)
XLA Modules:
  0.0 332.8 jit_solution(12281641485114431174)
XLA Ops:
  0.6 214.4 %shard_map.241 = (bf16[48,4,2,2,2,32,512]{6,5,4,3,2,1,0:T(8,128)(2,1)}, bf16[1024,1024]{1,0:T(8,128)(2,1)}, f32[2,8,1024]{2,1,0:T(8,128)}, bf16[1024,1024]{1,0:T...) custom-call(s32[2,16]{1,0:T(2,128)} %lengths.1, ...), custom_call_target="tpu_custom_call" | custom-call | tf_op jit(solution)/shard_map/pallas_call | solution.py:548
  215.1 110.4 %shard_map.242 = (f32[1024,1024]{1,0:T(8,128)}, f32[2,8,1024]{2,1,0:T(8,128)}, f32[8,1024]{1,0:T(8,128)}) custom-call(bf16[48,1024,512]{2,1,0:T(8,128)(2,1)} %bitcast.5, f32[2,1024]{1,0:T(2,128)} %gain_attn.1, f32[2,1024]{1,0:T(2,128)} %gain_ffn.1, f32[2,8,1024]{2,1,0:T(8,128)} %get-tuple-element.31.first_sums, ...), custom_call_target="tpu_custom_call" | custom-call | tf_op jit(solution)/shard_map/pallas_call | solution.py:895
  325.5 7.1 %shard_map.243 = (f32[1024,1024]{1,0:T(8,128)}, bf16[1024,1024]{1,0:T(8,128)(2,1)}, f32[2,1024]{1,0:T(2,128)}, f32[2,1024]{1,0:T(2,128)}, f32[2,1024]{1,0:T(2,12...) custom-call(f32[2,8,1024]{2,1,0:T(8,128)} %get-tuple-element.38.sums, ...), custom_call_target="tpu_custom_call" | custom-call | tf_op jit(solution)/shard_map/pallas_call | solution.py:988

commit v9 on v8

--- a/solution.py
+++ b/solution.py
@@ -244,12 +244,15 @@
 
 def forward_kernel(
     dims, devices_dims,
-    lengths, w_query, w_key, w_value, w_out, w_inner, w_outer, tokens, cotangent, *rest,
+    lengths, *rest,
 ):
+    matrices, rest = rest[:6], rest[6:]
+    (tokens, cotangent), rest = rest[:2], rest[2:]
     vectors, rest = rest[:8], rest[8:]
     (
         inner_raw, wbuf, out, first_sums, saved_f, saved_qkv, saved_p, saved_x, saved_s, saved_d,
         h, a, qkv, o, z, u, w, p_stage, d_stage, x_stage, s_stage, own, id_row, id_col, inner_bias, cot,
+        w_query, w_key, w_value, w_out, w_inner, w_outer, msem,
         wsem, psem, dsem, xsem, ssem, qsem, tsem, hsem, csem, send_sem, recv_sem,
     ) = rest
     rows, slots = dims
@@ -274,6 +277,14 @@
         gather.pump(half + DEPTH)
 
     gather.greet()
+    fetches = [
+        pltpu.make_async_copy(source, target, msem.at[n])
+        for n, (source, target) in enumerate(
+            zip(matrices, (w_query, w_key, w_value, w_out, w_inner, w_outer))
+        )
+    ]
+    for fetch in fetches:
+        fetch.start()
     load = pltpu.make_async_copy(tokens, a, tsem)
     load.start()
     load_cot = pltpu.make_async_copy(cotangent, cot, csem)
@@ -295,12 +306,15 @@
         gather.pump(i)
 
     for m in range(4):
+        fetches[m].wait()
         cast(0, m)
     here(0, AT_INNER).start()
     gather.meet()
     start(0)
     here(0, AT_INNER).wait()
     start(1)
+    fetches[4].wait()
+    fetches[5].wait()
     for l in range(LAYERS):
         at = l * GROUPS
         for m in range(4):
@@ -558,7 +572,7 @@
             jax.ShapeDtypeStruct((LAYERS, 2, count, 128), f32),
             jax.ShapeDtypeStruct((LAYERS, hidden // WIDTH, count, WIDTH), bf),
         ),
-        in_specs=[pl.BlockSpec(memory_space=pltpu.SMEM)] + [vm] * 6 + [any_] * 2 + [vm] * 9,
+        in_specs=[pl.BlockSpec(memory_space=pltpu.SMEM)] + [any_] * 8 + [vm] * 9,
         out_specs=(any_, any_, vm) + (any_,) * 6,
         scratch_shapes=[
             VMEM((count, width), f32),
@@ -577,6 +591,8 @@
             VMEM((rows, slots, 128), jnp.int32),
             VMEM((LAYERS, hidden), f32),
             VMEM((count, width), bf),
+            *(VMEM(m.shape, f32) for m in matrices),
+            DMA((6,)),
             DMA((2,)), DMA((2,)), DMA((2,)), DMA, DMA, DMA((3,)), DMA, DMA, DMA,
             DMA((SLOTS, 6, sems)), DMA((SLOTS, 6, sems)),
         ],

time: 333 us -> 332 us (level)
  no operation moved by 1% of the time
where the time goes in v9:
time: 332 us
  Pallas kernels  331 us (100%)
    pallas_call x1, Pallas kernels, forward(): pl.pallas_call(functools.partial(forward_kernel, (rows, slots), devices_d...  213 us
    pallas_call x1, Pallas kernels, backward(): pl.pallas_call(functools.partial(backward_kernel, (rows, slots), places),...  110 us
    pallas_call x1, Pallas kernels, finish(): pl.pallas_call(functools.partial(finish_kernel, unit), out_shape=large +...  7.13 us

profile of v9, /device:TPU:0, one launch (start us, length us, event | category | flops | bytes accessed | tf_op | source)
XLA Modules:
  0.0 331.8 jit_solution(3860816182156411760)
XLA Ops:
  0.6 213.4 %shard_map.241 = (bf16[48,4,2,2,2,32,512]{6,5,4,3,2,1,0:T(8,128)(2,1)}, bf16[1024,1024]{1,0:T(8,128)(2,1)}, f32[2,8,1024]{2,1,0:T(8,128)}, bf16[1024,1024]{1,0:T...) custom-call(s32[2,16]{1,0:T(2,128)} %lengths.1, ...), custom_call_target="tpu_custom_call" | custom-call | tf_op jit(solution)/shard_map/pallas_call | solution.py:562
  214.1 110.4 %shard_map.242 = (f32[1024,1024]{1,0:T(8,128)}, f32[2,8,1024]{2,1,0:T(8,128)}, f32[8,1024]{1,0:T(8,128)}) custom-call(bf16[48,1024,512]{2,1,0:T(8,128)(2,1)} %bitcast.5, f32[2,1024]{1,0:T(2,128)} %gain_attn.1, f32[2,1024]{1,0:T(2,128)} %gain_ffn.1, f32[2,8,1024]{2,1,0:T(8,128)} %get-tuple-element.31.first_sums, ...), custom_call_target="tpu_custom_call" | custom-call | tf_op jit(solution)/shard_map/pallas_call | solution.py:911
  324.5 7.1 %shard_map.243 = (f32[1024,1024]{1,0:T(8,128)}, bf16[1024,1024]{1,0:T(8,128)(2,1)}, f32[2,1024]{1,0:T(2,128)}, f32[2,1024]{1,0:T(2,128)}, f32[2,1024]{1,0:T(2,12...) custom-call(f32[2,8,1024]{2,1,0:T(8,128)} %get-tuple-element.38.sums, ...), custom_call_target="tpu_custom_call" | custom-call | tf_op jit(solution)/shard_map/pallas_call | solution.py:1004

commit v10 on v9

--- a/solution.py
+++ b/solution.py
@@ -430,9 +430,9 @@
             pltpu.make_async_copy(qkv.at[m], saved_qkv.at[l, m], qsem.at[m]).start()
 
         def attend(i):
-            @pl.when(lax.rem(i, 4) == 2)
-            def _():
-                pump(base + 7 + i // 4)
+            @pl.when((lax.rem(i, 3) == 1) & (i < 15))
+            def _():
+                pump(base + 7 + i // 3)
 
 
             r = i // pairs
@@ -469,7 +469,7 @@
         def attn_out(i):
             @pl.when(i == 1)
             def _():
-                pump(base + 11)
+                pump(base + 12)
 
             cols = tile(i, WIDTH)
             h[:, cols] += matmul(o[...], weights(base + AT_OUT + i))
@@ -478,7 +478,9 @@
         normalize(l, 0)
 
         def inner(i):
-            pump(base + 12 + i)
+            @pl.when(i != 3)
+            def _():
+                pump(base + 13 + i - i // 4)
 
 
             cols = tile(i, WIDTH)

time: 332 us -> 331 us (level)
  no operation moved by 1% of the time
where the time goes in v10:
time: 331 us
  Pallas kernels  330 us (100%)
    pallas_call x1, Pallas kernels, forward(): pl.pallas_call(functools.partial(forward_kernel, (rows, slots), devices_d...  213 us
    pallas_call x1, Pallas kernels, backward(): pl.pallas_call(functools.partial(backward_kernel, (rows, slots), places),...  110 us
    pallas_call x1, Pallas kernels, finish(): pl.pallas_call(functools.partial(finish_kernel, unit), out_shape=large +...  7.13 us

profile of v10, /device:TPU:0, one launch (start us, length us, event | category | flops | bytes accessed | tf_op | source)
XLA Modules:
  0.0 331.1 jit_solution(18332457695414521724)
XLA Ops:
  0.6 213.1 %shard_map.241 = (bf16[48,4,2,2,2,32,512]{6,5,4,3,2,1,0:T(8,128)(2,1)}, bf16[1024,1024]{1,0:T(8,128)(2,1)}, f32[2,8,1024]{2,1,0:T(8,128)}, bf16[1024,1024]{1,0:T...) custom-call(s32[2,16]{1,0:T(2,128)} %lengths.1, ...), custom_call_target="tpu_custom_call" | custom-call | tf_op jit(solution)/shard_map/pallas_call | solution.py:564
  213.7 110.0 %shard_map.242 = (f32[1024,1024]{1,0:T(8,128)}, f32[2,8,1024]{2,1,0:T(8,128)}, f32[8,1024]{1,0:T(8,128)}) custom-call(bf16[48,1024,512]{2,1,0:T(8,128)(2,1)} %bitcast.5, f32[2,1024]{1,0:T(2,128)} %gain_attn.1, f32[2,1024]{1,0:T(2,128)} %gain_ffn.1, f32[2,8,1024]{2,1,0:T(8,128)} %get-tuple-element.31.first_sums, ...), custom_call_target="tpu_custom_call" | custom-call | tf_op jit(solution)/shard_map/pallas_call | solution.py:913
  323.8 7.1 %shard_map.243 = (f32[1024,1024]{1,0:T(8,128)}, bf16[1024,1024]{1,0:T(8,128)(2,1)}, f32[2,1024]{1,0:T(2,128)}, f32[2,1024]{1,0:T(2,128)}, f32[2,1024]{1,0:T(2,12...) custom-call(f32[2,8,1024]{2,1,0:T(8,128)} %get-tuple-element.38.sums, ...), custom_call_target="tpu_custom_call" | custom-call | tf_op jit(solution)/shard_map/pallas_call | solution.py:1006
